TPU v7x, 32 devices: a whole 2x2x4 slice. The times are simulated.
32 devices in a mesh: fsdp: 8 (over z, y), seq: 4 (over x, core).
Axes of the slice: x: 2, y: 2, z: 4, core: 2. Of those that a mesh axis runs over, the one named last changes fastest.
Arguments:
- layer_input: bfloat16 [4096, 2048], P(('fsdp', 'seq')), may hold values from -6 to 6
- segment_ids: int32 [8, 512], P('fsdp'), may hold values from 0 to 7, as said below
- positions: int32 [4096], P('fsdp'), may hold values from 0 to 766, as said below
- ln1_gain: bfloat16 [2048], P(('fsdp', 'seq')), may hold values from 0.5 to 1.5
- ln1_bias: bfloat16 [2048], P(('fsdp', 'seq')), may hold values from -4 to 4
- qkv_weight: bfloat16 [2048, 6144], P(('fsdp', 'seq')), may hold values from -0.125 to 0.125
- qkv_bias: bfloat16 [6144], P(('fsdp', 'seq')), may hold values from -6 to 6
- out_weight: bfloat16 [2048, 2048], P(('fsdp', 'seq')), may hold values from -0.75 to 0.75
- ln2_gain: bfloat16 [2048], P(('fsdp', 'seq')), may hold values from 0.5 to 1.5
- ln2_bias: bfloat16 [2048], P(('fsdp', 'seq')), may hold values from -4 to 4
- gate_weight: bfloat16 [2048, 5632], P(('fsdp', 'seq')), may hold values from -0.125 to 0.125
- up_weight: bfloat16 [2048, 5632], P(('fsdp', 'seq')), may hold values from -0.125 to 0.125
- down_weight: bfloat16 [2048, 5632], P(('fsdp', 'seq')), may hold values from -0.078125 to 0.078125
- cotangent: bfloat16 [4096, 2048], P(('fsdp', 'seq')), may hold values from -6 to 6
Outputs:
- layer_output: bfloat16 [4096, 2048], P(('fsdp', 'seq'))
- input_grad: float32 [4096, 2048], P(('fsdp', 'seq'))
- ln1_gain_grad: float32 [2048], P(('fsdp', 'seq'))
- ln1_bias_grad: float32 [2048], P(('fsdp', 'seq'))
- qkv_weight_grad: float32 [2048, 6144], P(('fsdp', 'seq'))
- qkv_bias_grad: float32 [6144], P(('fsdp', 'seq'))
- out_weight_grad: float32 [2048, 2048], P(('fsdp', 'seq'))
- ln2_gain_grad: float32 [2048], P(('fsdp', 'seq'))
- ln2_bias_grad: float32 [2048], P(('fsdp', 'seq'))
- gate_weight_grad: float32 [2048, 5632], P(('fsdp', 'seq'))
- up_weight_grad: float32 [2048, 5632], P(('fsdp', 'seq'))
- down_weight_grad: float32 [2048, 5632], P(('fsdp', 'seq'))
Inputs may be any that keep to these rules, and one draw needn't show every extreme that they name: `segment_ids`: segment ids never fall along a sequence; each document holds 64 to 256 tokens, the first and last of a sequence may be cut. `positions`: A token's position counts from its document's first token, which for a sequence's first document may lie up to 511 tokens before the sequence.
All inputs are finite; a program needn't handle non-finite values.
Results may differ from a plain program's by a relative error of at most 0.012.
Values may be sent and summed in bfloat16 or wider, within the bound.
No kernel may reach another device: no remote copies, remote signals or barrier semaphores. Data moves between devices by JAX's collectives and lax.ppermute only.
A program may use at most 256 MiB of HBM per device.

v0:
```python
import jax
import jax.numpy as jnp
from jax import lax
from jax.sharding import PartitionSpec as P

HEADS = 32
HEAD_DIM = 64


def layer_norm(values, gain, shift):
    center = jnp.mean(values, axis=-1, keepdims=True)
    centered = values - center
    spread = jnp.mean(centered * centered, axis=-1, keepdims=True)
    return centered * lax.rsqrt(spread + 1e-05) * gain + shift


def rotary_tables(spots):
    inverse = 10000.0 ** (-jnp.arange(8).astype(jnp.float32) / 8.0)
    angle = spots.astype(jnp.float32)[:, None] * inverse[None, :]
    return (jnp.cos(angle), jnp.sin(angle))


def rotate(heads_view, cosine, sine):
    first = heads_view[..., :8]
    second = heads_view[..., 8:16]
    rest = heads_view[..., 16:]
    cos_part = cosine[:, None, :]
    sin_part = sine[:, None, :]
    return jnp.concatenate(
        [first * cos_part - second * sin_part, second * cos_part + first * sin_part, rest], axis=-1
    )


def contract_rows(left, right):
    return lax.dot_general(
        left, right, (((0,), (0,)), ((), ())), preferred_element_type=jnp.float32
    )


def contract_cols(left, right):
    return lax.dot_general(
        left, right, (((1,), (1,)), ((), ())), preferred_element_type=jnp.float32
    )


def swiglu(gate, up):
    return jax.nn.silu(gate) * up


def fetch_all(first, second, third, fourth, fifth):
    return (
        lax.all_gather(first, ("fsdp", "seq"), axis=0, tiled=True),
        lax.all_gather(second, ("fsdp", "seq"), axis=0, tiled=True),
        lax.all_gather(third, ("fsdp", "seq"), axis=0, tiled=True),
        lax.all_gather(fourth, ("fsdp", "seq"), axis=0, tiled=True),
        lax.all_gather(fifth, ("fsdp", "seq"), axis=0, tiled=True),
    )


def sum_all(first, second, third, fourth, fifth):
    return (
        lax.psum_scatter(first, ("fsdp", "seq"), scatter_dimension=0, tiled=True),
        lax.psum_scatter(second, ("fsdp", "seq"), scatter_dimension=0, tiled=True),
        lax.psum_scatter(third, ("fsdp", "seq"), scatter_dimension=0, tiled=True),
        lax.psum_scatter(fourth, ("fsdp", "seq"), scatter_dimension=0, tiled=True),
        lax.psum_scatter(fifth, ("fsdp", "seq"), scatter_dimension=0, tiled=True),
    )


def fetch_block(first, second):
    columns = (
        lax.all_to_all(first, "seq", split_axis=2, concat_axis=0, tiled=True),
        lax.all_to_all(second, "seq", split_axis=2, concat_axis=0, tiled=True),
    )
    return (
        lax.all_gather(columns[0], "fsdp", axis=0, tiled=True),
        lax.all_gather(columns[1], "fsdp", axis=0, tiled=True),
    )


def return_block(first, second):
    summed = (
        lax.psum_scatter(first, "fsdp", scatter_dimension=0, tiled=True),
        lax.psum_scatter(second, "fsdp", scatter_dimension=0, tiled=True),
    )
    return (
        lax.all_to_all(summed[0], "seq", split_axis=0, concat_axis=2, tiled=True),
        lax.all_to_all(summed[1], "seq", split_axis=0, concat_axis=2, tiled=True),
    )


def seq_rows(values):
    return lax.all_gather(values, "seq", axis=0, tiled=True)


def seq_sums(values):
    return lax.psum_scatter(values, "seq", scatter_dimension=0, tiled=True)


def split_heads(
    layer_input,
    segment_ids,
    positions,
    ln1_gain,
    ln1_bias,
    qkv_weight,
    qkv_bias,
    out_weight,
    ln2_gain,
    ln2_bias,
    gate_weight,
    up_weight,
    down_weight,
    cotangent,
):
    width = layer_input.shape[1]
    own_rows = qkv_weight.shape[0]
    hidden_units = gate_weight.shape[1]
    quarter = lax.axis_size("seq")
    seq_spot = lax.axis_index("seq")
    width_part = width // quarter
    units_part = hidden_units // quarter
    heads_here = HEADS // quarter
    small = fetch_all(qkv_bias, ln1_gain, ln1_bias, ln2_gain, ln2_bias)
    gain_one = small[1].astype(jnp.float32)
    shift_one = small[2].astype(jnp.float32)
    gain_two = small[3].astype(jnp.float32)
    shift_two = small[4].astype(jnp.float32)
    bias_here = (
        lax.dynamic_slice_in_dim(small[0].reshape(3, width), seq_spot * width_part, width_part, 1)
        .astype(jnp.float32)
        .reshape(3 * width_part)
    )

    def attn_blocks():
        return fetch_block(
            qkv_weight.reshape(own_rows, 3, width), out_weight.reshape(own_rows, 1, width)
        )

    def mlp_blocks():
        return fetch_block(
            jnp.stack([gate_weight, up_weight], axis=1),
            down_weight.reshape(own_rows, 1, hidden_units),
        )

    attn_fwd = attn_blocks()
    qkv_block = attn_fwd[0].reshape(width, 3 * width_part)
    out_block = attn_fwd[1].reshape(width, width_part)
    inputs = layer_input.astype(jnp.float32)
    normed_low = layer_norm(inputs, gain_one, shift_one).astype(jnp.bfloat16)
    normed_all = seq_rows(normed_low)
    length = normed_all.shape[0]
    mixed = jnp.dot(normed_all, qkv_block, preferred_element_type=jnp.float32) + bias_here
    cosine, sine = rotary_tables(positions)
    query_low = rotate(
        mixed[:, :width_part].reshape(length, heads_here, HEAD_DIM), cosine, sine
    ).astype(jnp.bfloat16)
    key_low = rotate(
        mixed[:, width_part : 2 * width_part].reshape(length, heads_here, HEAD_DIM), cosine, sine
    ).astype(jnp.bfloat16)
    value_low = (
        mixed[:, 2 * width_part :].reshape(length, heads_here, HEAD_DIM).astype(jnp.bfloat16)
    )
    segment_row = segment_ids[0]
    index = jnp.arange(length)

    def block_scores():
        scores = (
            jnp.einsum("thd,lhd->htl", query_low, key_low, preferred_element_type=jnp.float32)
            * 0.125
        )
        allowed = (segment_row[:, None] == segment_row[None, :]) & (
            index[None, :] <= index[:, None]
        )
        return jnp.where(allowed[None], scores, -1e30)

    scores = block_scores()
    top = jnp.max(scores, axis=-1, keepdims=True)
    expo = jnp.exp(scores - top)
    total = jnp.sum(expo, axis=-1, keepdims=True)
    probs = (expo / total).astype(jnp.bfloat16)
    log_sums = top + jnp.log(total)
    pieces = jnp.einsum("htl,lhd->thd", probs, value_low, preferred_element_type=jnp.float32)
    attended_low = pieces.reshape(length, width_part).astype(jnp.bfloat16)
    hidden = inputs + seq_sums(contract_cols(attended_low, out_block))
    mlp_fwd = mlp_blocks()
    pair_block = mlp_fwd[0].reshape(width, 2 * units_part)
    down_block = mlp_fwd[1].reshape(width, units_part)
    normed2_low = layer_norm(hidden, gain_two, shift_two).astype(jnp.bfloat16)
    normed2_all = seq_rows(normed2_low)
    gate_up = jnp.dot(normed2_all, pair_block, preferred_element_type=jnp.float32)
    gate = gate_up[:, :units_part]
    up = gate_up[:, units_part:]
    inner_low = swiglu(gate, up).astype(jnp.bfloat16)
    result = hidden + seq_sums(contract_cols(inner_low, down_block))
    mlp_back = mlp_blocks()
    pair_back = mlp_back[0].reshape(width, 2 * units_part)
    down_back = mlp_back[1].reshape(width, units_part)
    cotangent_all = seq_rows(cotangent)
    inner_grad = jnp.dot(cotangent_all, down_back, preferred_element_type=jnp.float32)
    down_grad = contract_rows(cotangent_all, inner_low)
    unused, pull_swiglu = jax.vjp(swiglu, gate, up)
    gate_grad, up_grad = pull_swiglu(inner_grad)
    pair_low = jnp.concatenate(
        [gate_grad.astype(jnp.bfloat16), up_grad.astype(jnp.bfloat16)], axis=1
    )
    pair_wgrad = contract_rows(normed2_all, pair_low)
    normed2_grad = seq_sums(contract_cols(pair_low, pair_back))
    unused_two, pull_norm_two = jax.vjp(layer_norm, hidden, gain_two, shift_two)
    hidden_part, gain_two_grad, shift_two_grad = pull_norm_two(normed2_grad)
    hidden_grad = cotangent.astype(jnp.float32) + hidden_part
    mlp_shares = return_block(
        pair_wgrad.reshape(width, 2, units_part), down_grad.reshape(width, 1, units_part)
    )
    attn_back = attn_blocks()
    qkv_back = attn_back[0].reshape(width, 3 * width_part)
    out_back = attn_back[1].reshape(width, width_part)
    branch_all = seq_rows(hidden_grad.astype(jnp.bfloat16))
    out_wgrad = contract_rows(branch_all, attended_low)
    attended_grad = (
        jnp.dot(branch_all, out_back, preferred_element_type=jnp.float32)
        .astype(jnp.bfloat16)
        .reshape(length, heads_here, HEAD_DIM)
    )
    scores = block_scores()
    probs = jnp.exp(scores - log_sums)
    probs_low = probs.astype(jnp.bfloat16)
    value_grad = jnp.einsum(
        "htl,thd->lhd", probs_low, attended_grad, preferred_element_type=jnp.float32
    )
    probs_grad = jnp.einsum(
        "thd,lhd->htl", attended_grad, value_low, preferred_element_type=jnp.float32
    )
    center = jnp.sum(probs * probs_grad, axis=-1, keepdims=True)
    scores_low = (probs * (probs_grad - center)).astype(jnp.bfloat16)
    query_pieces = (
        jnp.einsum("htl,lhd->thd", scores_low, key_low, preferred_element_type=jnp.float32) * 0.125
    )
    key_grad = (
        jnp.einsum("htl,thd->lhd", scores_low, query_low, preferred_element_type=jnp.float32)
        * 0.125
    )
    query_back = rotate(query_pieces, cosine, -sine).reshape(length, width_part)
    key_back = rotate(key_grad, cosine, -sine).reshape(length, width_part)
    mixed_low = jnp.concatenate(
        [query_back, key_back, value_grad.reshape(length, width_part)], axis=1
    ).astype(jnp.bfloat16)
    qkv_wgrad = contract_rows(normed_all, mixed_low)
    bias_part = jnp.sum(mixed_low.astype(jnp.float32), axis=0).reshape(3, width_part)
    slot_mask = (jnp.arange(quarter) == seq_spot).astype(jnp.float32)
    bias_whole = (bias_part[:, None, :] * slot_mask[None, :, None]).reshape(3 * width)
    normed_grad = seq_sums(contract_cols(mixed_low, qkv_back))
    unused_one, pull_norm_one = jax.vjp(layer_norm, inputs, gain_one, shift_one)
    input_part, gain_one_grad, shift_one_grad = pull_norm_one(normed_grad)
    input_grad = hidden_grad + input_part
    attn_shares = return_block(
        qkv_wgrad.reshape(width, 3, width_part), out_wgrad.reshape(width, 1, width_part)
    )
    small_shares = sum_all(bias_whole, gain_one_grad, shift_one_grad, gain_two_grad, shift_two_grad)
    gate_wgrad = mlp_shares[0][:, 0, :]
    up_wgrad = mlp_shares[0][:, 1, :]
    down_wgrad = mlp_shares[1].reshape(own_rows, hidden_units)
    qkv_share = attn_shares[0].reshape(own_rows, 3 * width)
    out_share = attn_shares[1].reshape(own_rows, width)
    return (
        result.astype(jnp.bfloat16),
        input_grad,
        small_shares[1],
        small_shares[2],
        qkv_share,
        small_shares[0],
        out_share,
        small_shares[3],
        small_shares[4],
        gate_wgrad,
        up_wgrad,
        down_wgrad,
    )


def body(
    layer_input,
    segment_ids,
    positions,
    ln1_gain,
    ln1_bias,
    qkv_weight,
    qkv_bias,
    out_weight,
    ln2_gain,
    ln2_bias,
    gate_weight,
    up_weight,
    down_weight,
    cotangent,
):
    return split_heads(
        layer_input,
        segment_ids,
        positions,
        ln1_gain,
        ln1_bias,
        qkv_weight,
        qkv_bias,
        out_weight,
        ln2_gain,
        ln2_bias,
        gate_weight,
        up_weight,
        down_weight,
        cotangent,
    )


def solution(mesh):
    placed = (
        P(("fsdp", "seq"), None),
        P("fsdp", None),
        P("fsdp"),
        P(("fsdp", "seq")),
        P(("fsdp", "seq")),
        P(("fsdp", "seq"), None),
        P(("fsdp", "seq")),
        P(("fsdp", "seq"), None),
        P(("fsdp", "seq")),
        P(("fsdp", "seq")),
        P(("fsdp", "seq"), None),
        P(("fsdp", "seq"), None),
        P(("fsdp", "seq"), None),
        P(("fsdp", "seq"), None),
    )
    return jax.shard_map(
        body,
        mesh=mesh,
        in_specs=placed,
        out_specs=(
            P(("fsdp", "seq"), None),
            P(("fsdp", "seq"), None),
            P(("fsdp", "seq")),
            P(("fsdp", "seq")),
            P(("fsdp", "seq"), None),
            P(("fsdp", "seq")),
            P(("fsdp", "seq"), None),
            P(("fsdp", "seq")),
            P(("fsdp", "seq")),
            P(("fsdp", "seq"), None),
            P(("fsdp", "seq"), None),
            P(("fsdp", "seq"), None),
        ),
        check_vma=False,
    )
```

profile of v0, /device:TPU:0, one launch (start us, length us, event | category | flops | bytes accessed | tf_op | source)
XLA Modules:
  0.0 2342.8 jit_solution(12369615966745718935)
XLA Ops:
  13.2 15.8 all_to_all.155
  35.5 43.4 %all-reduce.15 = (bf16[2048]{0:T(1024)(128)(2,1)S(1)}, bf16[2048]{0:T(1024)(128)(2,1)S(1)}, bf16[3,2048]{1,0:T(4,128)(2,1)S(1)}, bf16[2048]{0:T(1024)(128)(2,1)}, bf16[2048]{0:T(1024)(128)(2,1)}) all-reduce(bf16[2048]{0:T(1024)(128)(2,1)S(1)} %dynamic-update-slice.1, ...), channel_id=1, replica_groups=mesh['fsdp'=8,'seq'=4] {'fsdp','seq'}, use_global_device_ids=true, to_apply=%add.1 | all-reduce | flops 14336 | bytes 57344
  82.4 11.5 reduce
  106.9 28.3 %all-gather.11.cloned.1.call-done = bf16[2048,3,512]{2,0,1:T(8,128)(2,1)} async-done(((bf16[256,3,512]{2,0,1:T(8,128)(2,1)}), bf16[2048,3,512]{2,0,1:T(8,128)(2,1)}) %all-gather.11.cloned.1.call-update) | async-done | bytes 6291472 | tf_op jit(solution)/shard_map/all_gather | solution.py:76
  144.2 14.0 all-gather.9.cloned.1.call-done
  178.6 31.6 %all-gather.13.cloned.1.call-done = bf16[2048,1,512]{2,0,1:T(8,128)(2,1)} async-done(((bf16[256,1,512]{2,0,1:T(8,128)(2,1)}), bf16[2048,1,512]{2,0,1:T(8,128)(2,1)}) %all-gather.13.cloned.1.call-update) | async-done | bytes 2097168 | tf_op jit(solution)/shard_map/all_gather | solution.py:77
  227.2 38.5 %all_to_all.156 = bf16[4,2,90112]{2,1,0:T(2,128)(2,1)} all-to-all(bf16[4,2,90112]{2,1,0:T(2,128)(2,1)} %reshape.345), channel_id=1, replica_groups=mesh['fsdp'=8,'seq'=4] {'seq'}, dimensions={0} | all-to-all | bytes 2883584 | tf_op jit(solution)/shard_map/all_to_all | solution.py:72
  285.5 31.6 %reduce.1 = bf16[5632,64]{1,0:T(8,128)(2,1)S(1)} reduce(bf16[5632,1,64]{2,1,0:T(2,128)(2,1)} %bitcast.128, bf16[]{:T(256)} %broadcast.232), dimensions={1}, to_apply=%bitcast.94.reduce_sub_computation | reduce | bytes 1441794
  319.5 14.4 all_to_all.157
  344.1 94.2 %all-gather.17.cloned.1.call-done = bf16[2048,2,1408]{2,0,1:T(8,128)(2,1)} async-done(((bf16[256,2,1408]{2,0,1:T(8,128)(2,1)}), bf16[2048,2,1408]{2,0,1:T(8,128)(2,1)}) %all-gather.17.cloned.1.call-update) | async-done | bytes 11534352 | tf_op jit(solution)/shard_map/all_gather | solution.py:76
  438.4 15.4 copy.149
  461.2 12.6 fusion.58
  473.8 11.7 all-gather.21.cloned.1.call-done
  485.5 95.7 %all-gather.19.cloned.1.call-done = bf16[2048,1,1408]{2,0,1:T(8,128)(2,1)} async-done(((bf16[256,1,1408]{2,0,1:T(8,128)(2,1)}), bf16[2048,1,1408]{2,0,1:T(8,128)(2,1)}) %all-gather.19.cloned.1.call-update) | async-done | bytes 5767184 | tf_op jit(solution)/shard_map/all_gather | solution.py:77
  607.6 35.0 %reduce-scatter.11.cloned.1.call-done = f32[128,2048]{1,0:T(8,128)} async-done(((f32[512,2048]{1,0:T(8,128)}), f32[128,2048]{1,0:T(8,128)}) %reduce-scatter.11.cloned.1.call-update) | async-done | bytes 1048592 | tf_op jit(solution)/shard_map/reduce_scatter | solution.py:97
  644.3 45.3 %reduce-scatter.9.cloned.1.call-done = f32[128,2048]{1,0:T(8,128)} async-done(((f32[512,2048]{1,0:T(8,128)}), f32[128,2048]{1,0:T(8,128)}) %reduce-scatter.9.cloned.1.call-update) | async-done | bytes 1048592 | tf_op jit(solution)/shard_map/reduce_scatter | solution.py:97
  694.4 22.5 all-gather.23.cloned.1.call-done
  732.4 12.8 fusion.18
  745.2 26.9 %reshape.325 = f32[2048,2,1408]{2,1,0:T(2,128)} reshape(f32[2048,2816]{1,0:T(8,128)} %fusion.18) | data formatting | bytes 46137344 | tf_op jit(solution)/shard_map/reshape | solution.py:213
  796.4 18.1 copy.156
  828.3 178.2 %reduce-scatter.17.cloned.1.call-done = f32[256,1,1408]{0,2,1:T(8,128)} async-done(((f32[2048,1,1408]{0,2,1:T(8,128)}), f32[256,1,1408]{0,2,1:T(8,128)}) %reduce-scatter.17.cloned.1.call-update) | async-done | bytes 1441808 | tf_op jit(solution)/shard_map/reduce_scatter | solution.py:84
  1016.8 1175.2 %all-reduce.18.cloned.1.call-done = (f32[2048,3,512]{2,1,0:T(4,128)}, f32[2048,2,1408]{2,1,0:T(2,128)}) async-done(((f32[2048,3,512]{2,1,0:T(4,128)}, f32[2048,2,1408]{2,1,0:T(2,128)}), (f32[2048,3,512]{2,1,0:T(4,128)}, f32[2048,2,1408]{2,1,0:T(2,128)})) %all-reduce.18.cloned.1.call-update) | async-done | bytes 35651600
  2205.1 32.4 %all-to-all-done.4 = f32[256,3,512]{2,1,0:T(4,128)S(1)} async-done(((f32[256,3,512]{2,1,0:T(4,128)}), f32[256,3,512]{2,1,0:T(4,128)S(1)}, u32[]{:S(2)}, u32[]{:S(2)}) %all-to-all-start.4) | async-done | bytes 1572896 | tf_op jit(solution)/shard_map/all_to_all | solution.py:87
  2255.3 56.4 %all-reduce.13 = (f32[2048]{0:T(1024)S(1)}, f32[2048]{0:T(1024)S(1)}, f32[6144]{0:T(1024)S(1)}, f32[2048]{0:T(1024)S(1)}, f32[2048]{0:T(1024)S(1)}) all-reduce(f32[2048]{0:T(1024)S(1)} %get-tuple-element.14, f32[2048]{0:T(1024)S(1)} %get-tuple-element.17, ...), channel_id=6, replica_groups=mesh['fsdp'=8,'seq'=4] {'fsdp','seq'}, use_global_device_ids=true, to_apply=%region_16.17.clone | all-reduce | flops 14336 | bytes 114688
  (297 shorter events, 265.3 us)
Async XLA Ops:
  7.2 128.1 %all-gather.11.cloned.1.call-start = ((), (), s32[]{:S(2)}) async-start(), calls=%async_computation.15 | async-start | bytes 7077888 | tf_op jit(solution)/shard_map/all_gather | solution.py:76
  29.0 49.9 %copy-start.1 = (bf16[128,2048]{1,0:T(8,128)(2,1)S(1)}, bf16[128,2048]{1,0:T(8,128)(2,1)}, u32[]{:S(2)}) copy-start(bf16[128,2048]{1,0:T(8,128)(2,1)} %param.14) | copy-start | bytes 1572868
  32.0 49.2 %copy-start.35 = (bf16[64,2048]{1,0:T(8,128)(2,1)S(1)}, bf16[64,2048]{1,0:T(8,128)(2,1)}, u32[]{:S(2)}) copy-start(bf16[64,2048]{1,0:T(8,128)(2,1)} %param.21) | copy-start | bytes 786436
  34.2 124.0 %all-gather.9.cloned.1.call-start = ((), (), s32[]{:S(2)}) async-start(), calls=%async_computation.14 | async-start | bytes 2621440 | tf_op jit(solution)/shard_map/all_gather | solution.py:93
  95.1 9.6 all-to-all-start.1
  98.6 111.6 %all-gather.13.cloned.1.call-start = ((), (), s32[]{:S(2)}) async-start(), calls=%async_computation.16 | async-start | bytes 2359296 | tf_op jit(solution)/shard_map/all_gather | solution.py:77
  106.8 170.2 %reduce-scatter.7.cloned.1.call-start = ((), (), s32[]{:S(2)}) async-start(), calls=%async_computation.17 | async-start | bytes 5242880 | tf_op jit(solution)/shard_map/reduce_scatter | solution.py:97
  215.1 223.2 %all-gather.17.cloned.1.call-start = ((), (), s32[]{:S(2)}) async-start(), calls=%async_computation.19 | async-start | bytes 12976128 | tf_op jit(solution)/shard_map/all_gather | solution.py:76
  276.9 184.3 %all-gather.15.cloned.1.call-start = ((), (), s32[]{:S(2)}) async-start(), calls=%async_computation.18 | async-start | bytes 2621440 | tf_op jit(solution)/shard_map/all_gather | solution.py:93
  279.9 205.6 %all-gather.21.cloned.1.call-start = ((), (), s32[]{:S(2)}) async-start(), calls=%async_computation.22 | async-start | bytes 2621440 | tf_op jit(solution)/shard_map/all_gather | solution.py:93
  280.6 300.5 %all-gather.19.cloned.1.call-start = ((), (), s32[]{:S(2)}) async-start(), calls=%async_computation.20 | async-start | bytes 6488064 | tf_op jit(solution)/shard_map/all_gather | solution.py:77
  343.7 298.9 %reduce-scatter.11.cloned.1.call-start = ((), (), s32[]{:S(2)}) async-start(), calls=%async_computation.23 | async-start | bytes 5242880 | tf_op jit(solution)/shard_map/reduce_scatter | solution.py:97
  599.7 89.8 %reduce-scatter.9.cloned.1.call-start = ((), (), s32[]{:S(2)}) async-start(), calls=%async_computation.21 | async-start | bytes 5242880 | tf_op jit(solution)/shard_map/reduce_scatter | solution.py:97
  607.5 109.4 %all-gather.23.cloned.1.call-start = ((), (), s32[]{:S(2)}) async-start(), calls=%async_computation.24 | async-start | bytes 2621440 | tf_op jit(solution)/shard_map/all_gather | solution.py:93
  644.3 72.7 %copy-start.23 = (bf16[8,64,512]{2,1,0:T(8,128)(2,1)S(1)}, bf16[8,64,512]{2,1,0:T(8,128)(2,1)}, u32[]{:S(2)}) copy-start(bf16[8,64,512]{2,1,0:T(8,128)(2,1)} %copy-done.22) | copy-start | bytes 1572868
  694.2 128.2 %reduce-scatter.15.cloned.1.call-start = ((), (), s32[]{:S(2)}) async-start(), calls=%async_computation.26 | async-start | bytes 4718592 | tf_op jit(solution)/shard_map/reduce_scatter | solution.py:84
  721.8 284.6 %reduce-scatter.17.cloned.1.call-start = ((), (), s32[]{:S(2)}) async-start(), calls=%async_computation.27 | async-start | bytes 12976128 | tf_op jit(solution)/shard_map/reduce_scatter | solution.py:84
  730.8 1461.1 %all-reduce.18.cloned.1.call-start = ((), (), s32[]{:S(2)}) async-start(), calls=%async_computation.28 | async-start | bytes 79691776
  814.5 1437.5 %reduce-scatter.13.cloned.1.call-start = ((), (), s32[]{:S(2)}) async-start(), calls=%async_computation.25 | async-start | bytes 5242880 | tf_op jit(solution)/shard_map/reduce_scatter | solution.py:97
  824.8 186.4 %all-to-all-start.5 = ((f32[256,1,512]{2,1,0:T(1,128)}), f32[256,1,512]{2,1,0:T(1,128)S(1)}, u32[]{:S(2)}, u32[]{:S(2)}) async-start(f32[256,1,512]{2,1,0:T(1,128)} %copy.159), calls=%async_computation.10 | async-start | bytes 1048576 | tf_op jit(solution)/shard_map/all_to_all | solution.py:88
  828.3 187.3 %copy-start.59 = (u32[32]{0:T(128)S(1)}, u32[32]{0:T(128)}, u32[]{:S(2)}) copy-start(u32[32]{0:T(128)} %constant.71) | copy-start | bytes 388
  1012.0 1183.3 %all-to-all-start.7 = ((f32[256,1,1408]{2,1,0:T(1,128)}), f32[256,1,1408]{2,1,0:T(1,128)S(1)}, u32[]{:S(2)}, u32[]{:S(2)}) async-start(f32[256,1,1408]{2,1,0:T(1,128)} %copy.162), calls=%async_computation.13 | async-start | bytes 2883584 | tf_op jit(solution)/shard_map/all_to_all | solution.py:88
  2196.4 41.2 %all-to-all-start.4 = ((f32[256,3,512]{2,1,0:T(4,128)}), f32[256,3,512]{2,1,0:T(4,128)S(1)}, u32[]{:S(2)}, u32[]{:S(2)}) async-start(f32[256,3,512]{2,1,0:T(4,128)} %constant_dynamic-slice_fusion.1), calls=%async_computation.8 | async-start | bytes 4194304 | tf_op jit(solution)/shard_map/all_to_all | solution.py:87
  2238.9 88.6 %all-to-all-start.6 = ((f32[256,2,1408]{2,1,0:T(2,128)}), f32[256,2,1408]{2,1,0:T(2,128)S(1)}, u32[]{:S(2)}, u32[]{:S(2)}) async-start(f32[256,2,1408]{2,1,0:T(2,128)} %constant_dynamic-slice_fusion), calls=%async_computation.11 | async-start | bytes 5767168 | tf_op jit(solution)/shard_map/all_to_all | solution.py:87
  (61 other events, 562.6 us)
Sparse Core Ops, SparseCore 0:
  34.3 100.9 all-gather.10
  137.4 20.7 all-gather.8
  160.9 49.2 all-gather.12
  215.2 58.4 reduce-scatter.6
  277.1 161.2 all-gather.16
  440.4 20.7 all-gather.14
  462.9 22.5 all-gather.20
  488.5 92.6 all-gather.18
  599.9 42.6 reduce-scatter.10
  645.0 44.4 reduce-scatter.8
  694.3 22.5 all-gather.22
  722.0 87.8 reduce-scatter.14
  813.5 192.8 reduce-scatter.16
  1010.7 1181.2 all-reduce.17
  2194.3 57.5 reduce-scatter.12
where the time goes:
time: 2350 us; the launch traced here: 2340 us
  waiting for transfers between devices  1780 us (76%)
  local copies, waits for them, and re-layouts  180 us (8%)
  blocking collectives  168 us (7%)
  matrix products  106 us (5%)
  other arithmetic  69.2 us (3%)
    unnamed x16, waiting for transfers between devices  1180 us
    reduce_scatter x2, waiting for transfers between devices, return_block(): lax.psum_scatter(second, 'fsdp', scatter_dimension=0, tiled=True)  178 us
    all_gather x2, waiting for transfers between devices, fetch_block(): lax.all_gather(columns[1], 'fsdp', axis=0, tiled=True)  127 us
    all_gather x2, waiting for transfers between devices, fetch_block(): lax.all_gather(columns[0], 'fsdp', axis=0, tiled=True)  123 us
    unnamed x2, blocking collectives  99.8 us
    reduce_scatter x4, waiting for transfers between devices, seq_sums(): return lax.psum_scatter(values, 'seq', scatter_dimension=0, tiled=True)  88 us
    all_gather x4, waiting for transfers between devices, seq_rows(): return lax.all_gather(values, 'seq', axis=0, tiled=True)  55.6 us
    all_to_all x2, blocking collectives, fetch_block(): lax.all_to_all(first, 'seq', split_axis=2, concat_axis=0, tiled=True)  54.2 us
  transfers between devices with their start and end apart: 20, of which 15 were waited for; matrix products, arithmetic and copies ran while one was open for 12% of the time, Pallas kernels for 0%

commit v1 on v0

v1 whole, which is shorter than its diff:
```python
import jax
import jax.numpy as jnp
from jax import lax
from jax.sharding import PartitionSpec as P

HEADS = 32
HEAD_DIM = 64
AXES = ("fsdp", "seq")
F32 = jnp.float32
BF16 = jnp.bfloat16


def layer_norm(values, gain, shift):
    center = jnp.mean(values, axis=-1, keepdims=True)
    centered = values - center
    spread = jnp.mean(centered * centered, axis=-1, keepdims=True)
    return centered * lax.rsqrt(spread + 1e-05) * gain + shift


def norm_back(values, gain, grad):
    center = jnp.mean(values, axis=-1, keepdims=True)
    centered = values - center
    scale = lax.rsqrt(jnp.mean(centered * centered, axis=-1, keepdims=True) + 1e-05)
    hat = centered * scale
    lifted = grad * gain
    inner = jnp.mean(lifted * hat, axis=-1, keepdims=True)
    pulled = scale * (lifted - jnp.mean(lifted, axis=-1, keepdims=True) - hat * inner)
    return pulled, jnp.sum(grad * hat, axis=0), jnp.sum(grad, axis=0)


def rotary_tables(spots):
    inverse = 10000.0 ** (-jnp.arange(8).astype(F32) / 8.0)
    angle = spots.astype(F32)[..., None] * inverse
    return jnp.cos(angle), jnp.sin(angle)


def rotate(view, cosine, sine):
    first = view[..., :8]
    second = view[..., 8:16]
    rest = view[..., 16:]
    return jnp.concatenate(
        [first * cosine - second * sine, second * cosine + first * sine, rest], axis=-1
    )


def dot_rows(left, right, kind=F32):
    return lax.dot_general(
        left, right, (((0,), (0,)), ((), ())), preferred_element_type=F32
    ).astype(kind)


def dot_cols(left, right, kind=F32):
    return lax.dot_general(
        left, right, (((1,), (1,)), ((), ())), preferred_element_type=F32
    ).astype(kind)


def dot(left, right):
    return jnp.dot(left, right, preferred_element_type=F32)


class Places:
    def __init__(self):
        self.fsdp = lax.axis_size("fsdp")
        self.seq = lax.axis_size("seq")
        self.count = self.fsdp * self.seq
        self.outer = self.fsdp // 4
        spot = lax.axis_index("fsdp")
        side = lax.axis_index("seq")
        self.a = spot // 4
        self.b = (spot // 2) % 2
        self.e = spot % 2
        self.x = side // 2
        self.c = side % 2

    def flip(self, values, c=0, x=0, e=0, b=0):
        mask = c + 2 * x + self.seq * (e + 2 * b)
        return lax.ppermute(values, AXES, [(i, i ^ mask) for i in range(self.count)])

    def shift(self, values, steps):
        stride = 4 * self.seq
        return lax.ppermute(
            values, AXES, [((i + steps * stride) % self.count, i) for i in range(self.count)]
        )

    def push(self, values, steps):
        stride = 4 * self.seq
        return lax.ppermute(
            values, AXES, [(i, (i + steps * stride) % self.count) for i in range(self.count)]
        )


def pick(bit, first, second):
    return jnp.where(bit == 0, first, second)


def joined(bit, own, other, axis):
    return pick(
        bit, jnp.concatenate([own, other], axis=axis), jnp.concatenate([other, own], axis=axis)
    )


def to_relative(at, values):
    width = values.shape[-1] // (at.outer * 4)
    parts = []
    for i in range(at.outer):
        for j in range(2):
            for k in range(2):
                spot = (((at.a + i) % at.outer) * 2 + k) * 2 + (at.e ^ j)
                parts.append(
                    lax.dynamic_slice_in_dim(values, spot * width, width, values.ndim - 1)
                )
    return jnp.concatenate(parts, axis=-1)


def to_absolute(at, values):
    width = values.shape[-1] // (at.outer * 4)
    parts = []
    for i in range(at.outer):
        for k in range(2):
            for j in range(2):
                spot = (((i - at.a) % at.outer) * 2 + (at.e ^ j)) * 2 + k
                parts.append(
                    lax.dynamic_slice_in_dim(values, spot * width, width, values.ndim - 1)
                )
    return jnp.concatenate(parts, axis=-1)


def gather_tokens(at, values):
    near = [
        values,
        at.flip(values, x=1),
        at.flip(values, b=1),
        at.flip(values, x=1, b=1),
    ]
    return jnp.concatenate(near + [at.flip(v, c=1) for v in near], axis=0)


def sum_tokens(at, own, other):
    total = own + at.flip(other, c=1).astype(F32)
    rows = total.shape[0] // 4
    far = total[rows:].astype(BF16)
    out = total[:rows]
    out = out + at.flip(far[:rows], x=1).astype(F32)
    out = out + at.flip(far[rows : 2 * rows], b=1).astype(F32)
    out = out + at.flip(far[2 * rows :], x=1, b=1).astype(F32)
    return out


def fetch(at, weights, parts):
    pieces = []
    for w, n in zip(weights, parts):
        width = w.shape[1] // (8 * n)
        for p in range(n):
            pieces.append(
                [w[:, (p * 8 + j) * width : (p * 8 + j + 1) * width] for j in range(8)]
            )
    def half(side):
        return jnp.concatenate(
            [
                pick(side, piece[2 * g], piece[2 * g + 1])
                for g in range(4)
                for piece in pieces
            ],
            axis=1,
        )

    block = joined(at.c, half(at.c), at.flip(half(1 - at.c), c=1), 0)
    wide = block.shape[1] // 4
    quarter = [block[:, i * wide : (i + 1) * wide] for i in range(4)]
    def side_of(side):
        return jnp.concatenate(
            [pick(side, quarter[0], quarter[1]), pick(side, quarter[2], quarter[3])], axis=1
        )

    block = joined(at.x, side_of(at.x), at.flip(side_of(1 - at.x), x=1), 0)
    low, high = block[:, :wide], block[:, wide:]
    block = joined(at.b, pick(at.b, low, high), at.flip(pick(at.b, high, low), b=1), 0)
    blocks = []
    for i in range(at.outer):
        here = block if i == 0 else at.shift(block, i)
        blocks.append(here)
        blocks.append(at.flip(here, e=1))
    return blocks


def deliver(at, make, parts):
    outer = at.outer
    sent = [at.flip(make(2 * i + 1, BF16), e=1) for i in range(outer)]
    total = None
    for i in list(range(1, outer)) + [0]:
        here = make(2 * i, F32) + sent[i].astype(F32)
        if i:
            here = at.push(here.astype(BF16), i).astype(F32)
        total = here if total is None else total + here
    block = total.astype(BF16)
    rows = block.shape[0] // 2
    low, high = block[:rows], block[rows:]
    block = joined(at.b, pick(at.b, low, high), at.flip(pick(at.b, high, low), b=1), 1)
    rows = rows // 2
    low, high = block[:rows], block[rows:]
    own, other = pick(at.x, low, high), at.flip(pick(at.x, high, low), x=1)
    wide = own.shape[1] // 2
    block = jnp.concatenate(
        [
            joined(at.x, own[:, :wide], other[:, :wide], 1),
            joined(at.x, own[:, wide:], other[:, wide:], 1),
        ],
        axis=1,
    )
    rows = rows // 2
    low, high = block[:rows], block[rows:]
    own, other = pick(at.c, low, high), at.flip(pick(at.c, high, low), c=1)
    width = wide // parts
    outs = []
    for p in range(parts):
        cols = []
        for g in range(4):
            at_col = (g * parts + p) * width
            cols.append(
                joined(
                    at.c,
                    own[:, at_col : at_col + width].astype(F32),
                    other[:, at_col : at_col + width].astype(F32),
                    1,
                )
            )
        outs.append(jnp.concatenate(cols, axis=1))
    return outs


def fetch_small(at, values):
    block = values[None]
    block = joined(at.c, block, at.flip(block, c=1), 0)
    block = joined(at.x, block, at.flip(block, x=1), 0)
    block = joined(at.b, block, at.flip(block, b=1), 0)
    whole = jnp.stack([block] + [at.shift(block, i) for i in range(1, at.outer)])
    return jnp.stack([whole, at.flip(whole, e=1)], axis=1)


def deliver_small(at, values):
    whole = values[:, 0] + at.flip(values[:, 1], e=1)
    block = whole[0]
    for i in range(1, at.outer):
        block = block + at.push(whole[i], i)
    for bit, name in ((at.b, "b"), (at.x, "x"), (at.c, "c")):
        rows = block.shape[0] // 2
        low, high = block[:rows], block[rows:]
        block = pick(bit, low, high) + at.flip(pick(bit, high, low), **{name: 1})
    return block[0]


def order_tokens(at, values):
    seqs, length = values.shape
    view = values.reshape(seqs, 2, 2, length // 4)
    view = pick(at.x, view, view[:, ::-1])
    view = pick(at.c, view, view[:, :, ::-1])
    return jnp.swapaxes(view, 1, 2).reshape(seqs, length)


def body(
    layer_input,
    segment_ids,
    positions,
    ln1_gain,
    ln1_bias,
    qkv_weight,
    qkv_bias,
    out_weight,
    ln2_gain,
    ln2_bias,
    gate_weight,
    up_weight,
    down_weight,
    cotangent,
):
    at = Places()
    width = layer_input.shape[1]
    rows = qkv_weight.shape[0]
    bias_rows = qkv_bias.shape[0]
    length = segment_ids.shape[1]
    heads_here = HEADS // 8
    part = width // 8
    units = gate_weight.shape[1] // 8
    step = width // (2 * at.outer)
    slot = at.b * 4 + at.x * 2 + at.c

    inputs_low = to_relative(at, layer_input)
    inputs = inputs_low.astype(F32)
    inputs_all = gather_tokens(at, inputs_low)
    qkv_blocks = fetch(at, [qkv_weight], [3])
    small = fetch_small(
        at, jnp.concatenate([qkv_bias, ln1_gain, ln1_bias, ln2_gain, ln2_bias])
    )
    spots = jnp.concatenate([segment_ids, positions[None]], axis=0)
    spots = jnp.stack([spots, at.flip(spots, b=1)])
    segments = order_tokens(at, spots[:, 0])
    places = order_tokens(at, spots[:, 1])
    index = order_tokens(at, jnp.arange(length)[None])[0]

    def vector(i):
        start = bias_rows + i * rows
        return small[..., start : start + rows].reshape(width).astype(F32)

    gain_one, shift_one, gain_two, shift_two = (vector(i) for i in range(4))
    bias = small[..., :bias_rows]
    bias = pick(at.e, bias, bias[:, ::-1])
    bias = jnp.roll(bias, at.a, axis=0)
    bias = bias.reshape(at.outer, 2, 2, 4, bias_rows).swapaxes(1, 2).reshape(3, 8, part)
    bias = lax.dynamic_index_in_dim(bias, slot, 1, keepdims=False).reshape(3 * part).astype(F32)

    def cut(values, i):
        return values[:, i * step : (i + 1) * step]

    def contract(values, blocks):
        total = dot(cut(values, 0), blocks[0])
        for i in range(1, len(blocks)):
            total = total + dot(cut(values, i), blocks[i])
        return total

    def expand(values, blocks):
        half = values.shape[0] // 2
        other = jnp.concatenate([dot_cols(values[half:], w, BF16) for w in blocks], axis=1)
        own = jnp.concatenate([dot_cols(values[:half], w) for w in blocks], axis=1)
        return sum_tokens(at, own, other)

    def by_sequence(values, n):
        view = values.reshape(2, 2, length // 2, n, HEAD_DIM)
        return view.transpose(1, 3, 0, 2, 4).reshape(2, n, length, HEAD_DIM)

    def by_token(values):
        n = values.shape[1]
        view = values.reshape(2, n, 2, length // 2, HEAD_DIM)
        return view.transpose(2, 0, 3, 1, 4).reshape(2 * length, n * HEAD_DIM)

    normed_all = layer_norm(inputs_all.astype(F32), gain_one, shift_one).astype(BF16)
    mixed = contract(normed_all, qkv_blocks) + bias
    cosine, sine = rotary_tables(places)
    cosine, sine = cosine[:, None], sine[:, None]
    query = rotate(by_sequence(mixed[:, :part], heads_here), cosine, sine).astype(BF16)
    key = rotate(by_sequence(mixed[:, part : 2 * part], heads_here), cosine, sine).astype(BF16)
    value = by_sequence(mixed[:, 2 * part :], heads_here).astype(BF16)
    allowed = (segments[:, :, None] == segments[:, None, :]) & (
        index[None, None, :] <= index[None, :, None]
    )
    scores = jnp.einsum("bhtd,bhld->bhtl", query, key, preferred_element_type=F32) * 0.125
    scores = jnp.where(allowed[:, None], scores, -1e30)
    top = jnp.max(scores, axis=-1, keepdims=True)
    expo = jnp.exp(scores - top)
    total = jnp.sum(expo, axis=-1, keepdims=True)
    probs = expo / total
    probs_low = probs.astype(BF16)
    attended = by_token(
        jnp.einsum("bhtl,bhld->bhtd", probs_low, value, preferred_element_type=F32)
    ).astype(BF16)

    out_blocks = fetch(at, [out_weight], [1])
    hidden = inputs + expand(attended, out_blocks)
    normed2 = layer_norm(hidden, gain_two, shift_two).astype(BF16)
    normed2_all = gather_tokens(at, normed2)
    pair_blocks = fetch(at, [gate_weight, up_weight], [1, 1])
    cotangent_low = to_relative(at, cotangent)
    cotangent_all = gather_tokens(at, cotangent_low)
    down_blocks = fetch(at, [down_weight], [1])

    gate_up = contract(normed2_all, pair_blocks)
    gate = gate_up[:, :units]
    up = gate_up[:, units:]
    sigmoid = 1.0 / (1.0 + jnp.exp(-gate))
    silu = gate * sigmoid
    inner = (silu * up).astype(BF16)
    down_grads = deliver(
        at, lambda i, kind: dot_rows(cut(cotangent_all, i), inner, kind), 1
    )
    inner_grad = contract(cotangent_all, down_blocks)
    gate_grad = inner_grad * up * sigmoid * (1.0 + gate * (1.0 - sigmoid))
    up_grad = inner_grad * silu
    pair_low = jnp.concatenate([gate_grad.astype(BF16), up_grad.astype(BF16)], axis=1)
    normed2_grad = expand(pair_low, pair_blocks)
    pair_grads = deliver(
        at, lambda i, kind: dot_rows(cut(normed2_all, i), pair_low, kind), 2
    )
    result = to_absolute(at, hidden + expand(inner, down_blocks))

    hidden_part, gain_two_grad, shift_two_grad = norm_back(hidden, gain_two, normed2_grad)
    hidden_grad = cotangent_low.astype(F32) + hidden_part
    branch_all = gather_tokens(at, hidden_grad.astype(BF16))
    attended_grad = by_sequence(contract(branch_all, out_blocks), heads_here).astype(BF16)
    out_grads = deliver(
        at, lambda i, kind: dot_rows(cut(branch_all, i), attended, kind), 1
    )
    value_grad = jnp.einsum(
        "bhtl,bhtd->bhld", probs_low, attended_grad, preferred_element_type=F32
    )
    probs_grad = jnp.einsum(
        "bhtd,bhld->bhtl", attended_grad, value, preferred_element_type=F32
    )
    center = jnp.sum(probs * probs_grad, axis=-1, keepdims=True)
    scores_low = (probs * (probs_grad - center)).astype(BF16)
    query_grad = (
        jnp.einsum("bhtl,bhld->bhtd", scores_low, key, preferred_element_type=F32) * 0.125
    )
    key_grad = (
        jnp.einsum("bhtl,bhtd->bhld", scores_low, query, preferred_element_type=F32) * 0.125
    )
    mixed_low = jnp.concatenate(
        [
            by_token(rotate(query_grad, cosine, -sine)),
            by_token(rotate(key_grad, cosine, -sine)),
            by_token(value_grad),
        ],
        axis=1,
    ).astype(BF16)
    qkv_grads = deliver(
        at, lambda i, kind: dot_rows(cut(normed_all, i), mixed_low, kind), 3
    )
    normed_grad = expand(mixed_low, qkv_blocks)
    input_part, gain_one_grad, shift_one_grad = norm_back(inputs, gain_one, normed_grad)
    input_grad = to_absolute(at, hidden_grad + input_part)

    bias_part = jnp.sum(mixed_low.astype(F32), axis=0).reshape(3, 1, part)
    own_slot = (jnp.arange(8) == slot).astype(F32)[None, :, None]
    bias_whole = (bias_part * own_slot).reshape(at.outer, 2, 2, 4, bias_rows).swapaxes(1, 2)
    bias_whole = jnp.roll(bias_whole, -at.a, axis=0)
    bias_whole = pick(at.e, bias_whole, bias_whole[:, ::-1]).reshape(at.outer, 2, 8, bias_rows)
    grads = [
        v.reshape(at.outer, 2, 8, rows)
        for v in (gain_one_grad, shift_one_grad, gain_two_grad, shift_two_grad)
    ]
    shares = deliver_small(at, jnp.concatenate([bias_whole] + grads, axis=-1))

    def share(i):
        return shares[bias_rows + i * rows : bias_rows + (i + 1) * rows]

    return (
        result.astype(BF16),
        input_grad,
        share(0),
        share(1),
        jnp.concatenate(qkv_grads, axis=1),
        shares[:bias_rows],
        out_grads[0],
        share(2),
        share(3),
        pair_grads[0],
        pair_grads[1],
        down_grads[0],
    )


def solution(mesh):
    both = ("fsdp", "seq")
    wide = P(both, None)
    flat = P(both)
    return jax.shard_map(
        body,
        mesh=mesh,
        in_specs=(
            wide, P("fsdp", None), P("fsdp"), flat, flat, wide, flat,
            wide, flat, flat, wide, wide, wide, wide,
        ),
        out_specs=(wide, wide, flat, flat, wide, flat, wide, flat, flat, wide, wide, wide),
        check_vma=False,
    )
```

time: 2350 us -> 955 us (0.41)
  waiting for transfers between devices: 1780 us -> 414 us
  blocking collectives: 168 us -> 0 us
  starting transfers between devices: 19.5 us -> 87.2 us
  other arithmetic: 69.2 us -> 129 us
  matrix products: 106 us -> 151 us
    unnamed x16 -> x0, waiting for transfers between devices: 1180 us -> none
    ppermute x0 -> x103, waiting for transfers between devices: none -> 414 us  [the longest x93 371 us: flip(): lax.ppermute(values, AXES, [(i, i ^ mask) for i in range(self.count)])]
    all_gather x8 -> x0, waiting for transfers between devices: 305 us -> none  [the longest x2 127 us: fetch_block(): lax.all_gather(columns[1], 'fsdp', axis=0, tiled=True)]
    reduce_scatter x6 -> x0, waiting for transfers between devices: 266 us -> none  [the longest x2 178 us: return_block(): lax.psum_scatter(second, 'fsdp', scatter_dimension=0, tiled=True)]
    unnamed x2 -> x0, blocking collectives: 99.8 us -> none
    ppermute x0 -> x103, starting transfers between devices: none -> 87.2 us  [the longest x93 69.4 us: flip(): lax.ppermute(values, AXES, [(i, i ^ mask) for i in range(self.count)])]
    all_to_all x3 -> x0, blocking collectives: 68.6 us -> none  [the longest x2 54.2 us: fetch_block(): lax.all_to_all(first, 'seq', split_axis=2, concat_axis=0, tiled=True)]
    unnamed x161 -> x428, local copies, waits for them, and re-layouts: 47.5 us -> 96.5 us
  transfers between devices with their start and end apart: 20 -> 103, of which waited for: 15 -> 46; matrix products, arithmetic and copies ran while one was open for 12% -> 43% of each run, Pallas kernels for 0% -> 0%
where the time goes in v1:
time: 955 us; the launch traced here: 946 us
  waiting for transfers between devices  414 us (43%)
  local copies, waits for them, and re-layouts  160 us (17%)
  matrix products  151 us (16%)
  other arithmetic  129 us (14%)
  starting transfers between devices  87.2 us (9%)
    ppermute x93, waiting for transfers between devices, flip(): lax.ppermute(values, AXES, [(i, i ^ mask) for i in range(self.count)])  371 us
    unnamed x428, local copies, waits for them, and re-layouts  96.5 us
    ppermute x93, starting transfers between devices, flip(): lax.ppermute(values, AXES, [(i, i ^ mask) for i in range(self.count)])  69.4 us
    dot_general x16, matrix products, dot(): return jnp.dot(left, right, preferred_element_type=F32)  48 us
    dot_general x32, matrix products, dot_cols(): lax.dot_general(left, right, (((1,), (1,)), ((), ())), preferred_element_...  45.5 us
    select_n x74, other arithmetic, pick(): return jnp.where(bit == 0, first, second)  45.1 us
    dot_general x16, matrix products, dot_rows(): lax.dot_general(left, right, (((0,), (0,)), ((), ())), preferred_element_...  36 us
    ppermute x5, waiting for transfers between devices, push(): lax.ppermute(values, AXES, [(i, (i + steps * stride) % self.count) for i...  32.5 us
  transfers between devices with their start and end apart: 103, of which 46 were waited for; matrix products, arithmetic and copies ran while one was open for 43% of the time, Pallas kernels for 0%

profile of v1, /device:TPU:0, one launch (start us, length us, event | category | flops | bytes accessed | tf_op | source)
XLA Modules:
  0.0 946.1 jit_solution(6064473915551399080)
XLA Ops:
  124.3 13.7 %collective-permute-done.54 = bf16[128,2048]{0,1:T(8,128)(2,1)S(1)} collective-permute-done((bf16[128,2048]{0,1:T(8,128)(2,1)S(1)}, bf16[128,2048]{0,1:T(8,128)(2,1)S(1)}, u32[]{:S(2)}, u32[]{:S(2)}) %collective-permute-start.54) | collective-permute-done | bytes 524320 | tf_op jit(solution)/shard_map/ppermute | solution.py:78
  174.9 20.7 %collective-permute-done.44 = bf16[256,704]{0,1:T(8,128)(2,1)S(1)} collective-permute-done((bf16[256,704]{0,1:T(8,128)(2,1)S(1)}, bf16[256,704]{0,1:T(8,128)(2,1)S(1)}, u32[]{:S(2)}, u32[]{:S(2)}) %collective-permute-start.44) | collective-permute-done | bytes 360480 | tf_op jit(solution)/shard_map/ppermute | solution.py:78
  197.4 8.1 collective-permute-done.17
  209.1 7.0 collective-permute-done.16
  219.2 11.9 %collective-permute-done.18 = bf16[512,768]{1,0:T(8,128)(2,1)S(1)} collective-permute-done((bf16[512,768]{1,0:T(8,128)(2,1)S(1)}, bf16[512,768]{1,0:T(8,128)(2,1)S(1)}, u32[]{:S(2)}, u32[]{:S(2)}) %collective-permute-start.18) | collective-permute-done | bytes 786464 | tf_op jit(solution)/shard_map/ppermute | solution.py:78
  247.1 7.8 fusion.189
  293.2 9.5 %collective-permute-done.28 = bf16[128,2048]{0,1:T(8,128)(2,1)S(1)} collective-permute-done((bf16[128,2048]{0,1:T(8,128)(2,1)S(1)}, bf16[128,2048]{0,1:T(8,128)(2,1)S(1)}, u32[]{:S(2)}, u32[]{:S(2)}) %collective-permute-start.28) | collective-permute-done | bytes 524320 | tf_op jit(solution)/shard_map/ppermute | solution.py:78
  304.2 17.6 %collective-permute-done.27 = bf16[128,2048]{0,1:T(8,128)(2,1)S(1)} collective-permute-done((bf16[128,2048]{0,1:T(8,128)(2,1)S(1)}, bf16[128,2048]{0,1:T(8,128)(2,1)S(1)}, u32[]{:S(2)}, u32[]{:S(2)}) %collective-permute-start.27) | collective-permute-done | bytes 524320 | tf_op jit(solution)/shard_map/ppermute | solution.py:78
  340.5 15.0 %collective-permute-done.30 = bf16[128,2048]{0,1:T(8,128)(2,1)S(1)} collective-permute-done((bf16[128,2048]{0,1:T(8,128)(2,1)}, bf16[128,2048]{0,1:T(8,128)(2,1)S(1)}, u32[]{:S(2)}, u32[]{:S(2)}) %collective-permute-start.30) | collective-permute-done | bytes 524320 | tf_op jit(solution)/shard_map/ppermute | solution.py:78
  356.4 17.5 %collective-permute-done.31 = bf16[128,2048]{0,1:T(8,128)(2,1)S(1)} collective-permute-done((bf16[128,2048]{0,1:T(8,128)(2,1)}, bf16[128,2048]{0,1:T(8,128)(2,1)S(1)}, u32[]{:S(2)}, u32[]{:S(2)}) %collective-permute-start.31) | collective-permute-done | bytes 524320 | tf_op jit(solution)/shard_map/ppermute | solution.py:78
  390.3 20.6 %collective-permute-done.39 = bf16[512,1408]{0,1:T(8,128)(2,1)S(1)} collective-permute-done((bf16[512,1408]{0,1:T(8,128)(2,1)}, bf16[512,1408]{0,1:T(8,128)(2,1)S(1)}, u32[]{:S(2)}, u32[]{:S(2)}) %collective-permute-start.39) | collective-permute-done | bytes 1441824 | tf_op jit(solution)/shard_map/ppermute | solution.py:78
  415.3 25.6 %collective-permute-done.41 = bf16[512,1408]{0,1:T(8,128)(2,1)S(1)} collective-permute-done((bf16[512,1408]{0,1:T(8,128)(2,1)}, bf16[512,1408]{0,1:T(8,128)(2,1)S(1)}, u32[]{:S(2)}, u32[]{:S(2)}) %collective-permute-start.41) | collective-permute-done | bytes 1441824 | tf_op jit(solution)/shard_map/ppermute | solution.py:78
  485.0 42.3 %collective-permute-done.97 = bf16[512,704]{0,1:T(8,128)(2,1)S(1)} collective-permute-done((bf16[512,704]{0,1:T(8,128)(2,1)S(1)}, bf16[512,704]{0,1:T(8,128)(2,1)S(1)}, u32[]{:S(2)}, u32[]{:S(2)}) %collective-permute-start.97) | collective-permute-done | bytes 720928 | tf_op jit(solution)/shard_map/ppermute | solution.py:78
  542.4 18.3 %collective-permute-done.98 = bf16[512,704]{0,1:T(8,128)(2,1)S(1)} collective-permute-done((bf16[512,704]{0,1:T(8,128)(2,1)S(1)}, bf16[512,704]{0,1:T(8,128)(2,1)S(1)}, u32[]{:S(2)}, u32[]{:S(2)}) %collective-permute-start.98) | collective-permute-done | bytes 720928 | tf_op jit(solution)/shard_map/ppermute | solution.py:88
  569.7 7.7 collective-permute-done.100
  588.1 10.5 %collective-permute-done.101 = bf16[128,1408]{0,1:T(8,128)(2,1)S(1)} collective-permute-done((bf16[128,1408]{0,1:T(8,128)(2,1)S(1)}, bf16[128,1408]{0,1:T(8,128)(2,1)S(1)}, u32[]{:S(2)}, u32[]{:S(2)}) %collective-permute-start.101) | collective-permute-done | bytes 360480 | tf_op jit(solution)/shard_map/ppermute | solution.py:78
  617.6 18.7 %collective-permute-done.61 = bf16[128,2048]{0,1:T(8,128)(2,1)} collective-permute-done((bf16[128,2048]{0,1:T(8,128)(2,1)}, bf16[128,2048]{0,1:T(8,128)(2,1)}, u32[]{:S(2)}, u32[]{:S(2)}) %collective-permute-start.61) | collective-permute-done | bytes 524320 | tf_op jit(solution)/shard_map/ppermute | solution.py:78
  640.7 7.7 collective-permute-done.51
  648.4 8.4 collective-permute-done.50
  679.2 8.8 collective-permute-done.65
  690.7 10.6 %collective-permute-done.94 = bf16[256,1408]{0,1:T(8,128)(2,1)S(1)} collective-permute-done((bf16[256,1408]{0,1:T(8,128)(2,1)S(1)}, bf16[256,1408]{0,1:T(8,128)(2,1)S(1)}, u32[]{:S(2)}, u32[]{:S(2)}) %collective-permute-start.94) | collective-permute-done | bytes 720928 | tf_op jit(solution)/shard_map/ppermute | solution.py:78
  770.4 23.2 %collective-permute-done.85 = bf16[512,256]{1,0:T(8,128)(2,1)S(1)} collective-permute-done((bf16[512,256]{1,0:T(8,128)(2,1)}, bf16[512,256]{1,0:T(8,128)(2,1)S(1)}, u32[]{:S(2)}, u32[]{:S(2)}) %collective-permute-start.85) | collective-permute-done | bytes 262176 | tf_op jit(solution)/shard_map/ppermute | solution.py:78
  796.5 11.9 %collective-permute-done.86 = bf16[512,256]{1,0:T(8,128)(2,1)S(1)} collective-permute-done((bf16[512,256]{1,0:T(8,128)(2,1)S(1)}, bf16[512,256]{1,0:T(8,128)(2,1)S(1)}, u32[]{:S(2)}, u32[]{:S(2)}) %collective-permute-start.86) | collective-permute-done | bytes 262176 | tf_op jit(solution)/shard_map/ppermute | solution.py:88
  893.3 16.4 %collective-permute-done.83 = bf16[128,1536]{1,0:T(8,128)(2,1)S(1)} collective-permute-done((bf16[128,1536]{1,0:T(8,128)(2,1)S(1)}, bf16[128,1536]{1,0:T(8,128)(2,1)S(1)}, u32[]{:S(2)}, u32[]{:S(2)}) %collective-permute-start.83) | collective-permute-done | bytes 393248 | tf_op jit(solution)/shard_map/ppermute | solution.py:78
  (975 shorter events, 581.8 us)
Async XLA Ops:
  8.4 97.7 %collective-permute-start.1 = (bf16[128,2048]{0,1:T(8,128)(2,1)S(1)}, bf16[128,2048]{0,1:T(8,128)(2,1)}, u32[]{:S(2)}, u32[]{:S(2)}) collective-permute-start(bf16[128,2048]{0,1:T(8,128)(2,1)S(1)} %get-tuple-element.375), channel_id=1, source_target_pairs={{0,2},{1,3},{2,0},{3,1},{4,6},{5,7},{6,4},{7,5},{8,10},{9,11},{10,... | collective-permute-start | bytes 1572872 | tf_op jit(solution)/shard_map/ppermute | solution.py:78
  11.3 97.4 %collective-permute-start.2 = (bf16[128,2048]{0,1:T(8,128)(2,1)S(1)}, bf16[128,2048]{0,1:T(8,128)(2,1)}, u32[]{:S(2)}, u32[]{:S(2)}) collective-permute-start(bf16[128,2048]{0,1:T(8,128)(2,1)S(1)} %get-tuple-element.375), channel_id=1, source_target_pairs={{0,8},{1,9},{2,10},{3,11},{4,12},{5,13},{6,14},{7,15},{8,0},{9,1},... | collective-permute-start | bytes 1572872 | tf_op jit(solution)/shard_map/ppermute | solution.py:78
  12.9 100.0 %collective-permute-start.3 = (bf16[128,2048]{0,1:T(8,128)(2,1)S(1)}, bf16[128,2048]{0,1:T(8,128)(2,1)}, u32[]{:S(2)}, u32[]{:S(2)}) collective-permute-start(bf16[128,2048]{0,1:T(8,128)(2,1)S(1)} %get-tuple-element.375), channel_id=1, source_target_pairs={{0,10},{1,11},{2,8},{3,9},{4,14},{5,15},{6,12},{7,13},{8,2},{9,3},... | collective-permute-start | bytes 1572872 | tf_op jit(solution)/shard_map/ppermute | solution.py:78
  14.2 69.9 %collective-permute-start.19 = (bf16[64,1024]{1,0:T(8,128)(2,1)}, bf16[64,1024]{1,0:T(8,128)(2,1)}, u32[]{:S(2)}, u32[]{:S(2)}) collective-permute-start(bf16[64,1024]{1,0:T(8,128)(2,1)} %pad_maximum_fusion.21), channel_id=1, source_target_pairs={{0,1},{1,0},{2,3},{3,2},{4,5},{5,4},{6,7},{7,6},{8,9},{9,8},{10,11... | collective-permute-start | bytes 393224 | tf_op jit(solution)/shard_map/ppermute | solution.py:78
  14.3 48.2 %collective-permute-start.8 = (bf16[1,448]{1,0:T(2,128)(2,1)S(1)}, bf16[1,448]{1,0:T(2,128)(2,1)S(1)}, u32[]{:S(2)}, u32[]{:S(2)}) collective-permute-start(bf16[1,448]{1,0:T(2,128)(2,1)S(1)} %broadcast_in_dim.14), channel_id=1, source_target_pairs={{0,1},{1,0},{2,3},{3,2},{4,5},{5,4},{6,7},{7,6},{8,9},{9,8},{10,11... | collective-permute-start | bytes 2696 | tf_op jit(solution)/shard_map/ppermute | solution.py:78
  138.0 126.4 %collective-permute-start.22 = (bf16[512,256]{1,0:T(8,128)(2,1)}, bf16[512,256]{1,0:T(8,128)(2,1)}, u32[]{:S(2)}, u32[]{:S(2)}) collective-permute-start(bf16[512,256]{1,0:T(8,128)(2,1)} %maximum_select_fusion.32), channel_id=1, source_target_pairs={{0,4},{1,5},{2,6},{3,7},{4,0},{5,1},{6,2},{7,3},{8,12},{9,13},{10,... | collective-permute-start | bytes 786440 | tf_op jit(solution)/shard_map/ppermute | solution.py:78
  167.2 95.9 %collective-permute-start.24 = (bf16[512,256]{1,0:T(8,128)(2,1)}, bf16[512,256]{1,0:T(8,128)(2,1)}, u32[]{:S(2)}, u32[]{:S(2)}) collective-permute-start(bf16[512,256]{1,0:T(8,128)(2,1)} %collective-permute-done.23), channel_id=1, source_target_pairs={{0,4},{1,5},{2,6},{3,7},{4,0},{5,1},{6,2},{7,3},{8,12},{9,13},{10,... | collective-permute-start | bytes 786440 | tf_op jit(solution)/shard_map/ppermute | solution.py:78
  173.3 96.5 %collective-permute-start.37 = (bf16[128,2816]{0,1:T(8,128)(2,1)}, bf16[128,2816]{0,1:T(8,128)(2,1)}, u32[]{:S(2)}, u32[]{:S(2)}) collective-permute-start(bf16[128,2816]{0,1:T(8,128)(2,1)} %pad_maximum_fusion.10), channel_id=1, source_target_pairs={{0,2},{1,3},{2,0},{3,1},{4,6},{5,7},{6,4},{7,5},{8,10},{9,11},{10,... | collective-permute-start | bytes 2162696 | tf_op jit(solution)/shard_map/ppermute | solution.py:78
  216.1 66.6 %collective-permute-start.46 = (bf16[512,704]{0,1:T(8,128)(2,1)S(1)}, bf16[512,704]{0,1:T(8,128)(2,1)}, u32[]{:S(2)}, u32[]{:S(2)}) collective-permute-start(bf16[512,704]{0,1:T(8,128)(2,1)S(1)} %maximum_select_fusion.10), channel_id=1, source_target_pairs={{16,0},{17,1},{18,2},{19,3},{20,4},{21,5},{22,6},{23,7},{24,8},{25... | collective-permute-start | bytes 2162696 | tf_op jit(solution)/shard_map/ppermute | solution.py:82
  231.1 93.4 %collective-permute-start.45 = (bf16[512,704]{0,1:T(8,128)(2,1)S(1)}, bf16[512,704]{0,1:T(8,128)(2,1)}, u32[]{:S(2)}, u32[]{:S(2)}) collective-permute-start(bf16[512,704]{0,1:T(8,128)(2,1)S(1)} %maximum_select_fusion.10), channel_id=1, source_target_pairs={{0,4},{1,5},{2,6},{3,7},{4,0},{5,1},{6,2},{7,3},{8,12},{9,13},{10,... | collective-permute-start | bytes 2162696 | tf_op jit(solution)/shard_map/ppermute | solution.py:78
  291.2 156.2 %collective-permute-start.47 = (bf16[512,704]{0,1:T(8,128)(2,1)}, bf16[512,704]{0,1:T(8,128)(2,1)S(1)}, u32[]{:S(2)}, u32[]{:S(2)}) collective-permute-start(bf16[512,704]{0,1:T(8,128)(2,1)} %collective-permute-done.46), channel_id=1, source_target_pairs={{0,4},{1,5},{2,6},{3,7},{4,0},{5,1},{6,2},{7,3},{8,12},{9,13},{10,... | collective-permute-start | bytes 2162696 | tf_op jit(solution)/shard_map/ppermute | solution.py:78
  302.7 73.6 %collective-permute-start.40 = (bf16[512,1408]{0,1:T(8,128)(2,1)}, bf16[512,1408]{0,1:T(8,128)(2,1)}, u32[]{:S(2)}, u32[]{:S(2)}) collective-permute-start(bf16[512,1408]{0,1:T(8,128)(2,1)} %maximum_select_fusion.2), channel_id=1, source_target_pairs={{16,0},{17,1},{18,2},{19,3},{20,4},{21,5},{22,6},{23,7},{24,8},{25... | collective-permute-start | bytes 4325384 | tf_op jit(solution)/shard_map/ppermute | solution.py:82
  376.8 64.1 %collective-permute-start.41 = (bf16[512,1408]{0,1:T(8,128)(2,1)}, bf16[512,1408]{0,1:T(8,128)(2,1)S(1)}, u32[]{:S(2)}, u32[]{:S(2)}) collective-permute-start(bf16[512,1408]{0,1:T(8,128)(2,1)} %collective-permute-done.40), channel_id=1, source_target_pairs={{0,4},{1,5},{2,6},{3,7},{4,0},{5,1},{6,2},{7,3},{8,12},{9,13},{10,... | collective-permute-start | bytes 4325384 | tf_op jit(solution)/shard_map/ppermute | solution.py:78
  470.0 107.9 %collective-permute-start.59 = (bf16[512,2048]{0,1:T(8,128)(2,1)S(1)}, bf16[512,2048]{0,1:T(8,128)(2,1)S(1)}, u32[]{:S(2)}, u32[]{:S(2)}) collective-permute-start(bf16[512,2048]{0,1:T(8,128)(2,1)S(1)} %pad_maximum_fusion.6), channel_id=1, source_target_pairs={{0,1},{1,0},{2,3},{3,2},{4,5},{5,4},{6,7},{7,6},{8,9},{9,8},{10,11... | collective-permute-start | bytes 6291464 | tf_op jit(solution)/shard_map/ppermute | solution.py:78
  476.9 105.7 %collective-permute-start.48 = (bf16[512,2048]{0,1:T(8,128)(2,1)S(1)}, bf16[512,2048]{0,1:T(8,128)(2,1)S(1)}, u32[]{:S(2)}, u32[]{:S(2)}) collective-permute-start(bf16[512,2048]{0,1:T(8,128)(2,1)S(1)} %pad_maximum_fusion.5), channel_id=1, source_target_pairs={{0,1},{1,0},{2,3},{3,2},{4,5},{5,4},{6,7},{7,6},{8,9},{9,8},{10,11... | collective-permute-start | bytes 6291464 | tf_op jit(solution)/shard_map/ppermute | solution.py:78
  477.4 85.7 %collective-permute-start.91 = (bf16[512,1408]{0,1:T(8,128)(2,1)S(1)}, bf16[512,1408]{0,1:T(8,128)(2,1)S(1)}, u32[]{:S(2)}, u32[]{:S(2)}) collective-permute-start(bf16[512,1408]{0,1:T(8,128)(2,1)S(1)} %convolution_convert_fusion.1), channel_id=1, source_target_pairs={{0,4},{1,5},{2,6},{3,7},{4,0},{5,1},{6,2},{7,3},{8,12},{9,13},{10,... | collective-permute-start | bytes 4325384 | tf_op jit(solution)/shard_map/ppermute | solution.py:78
  477.9 49.4 %collective-permute-start.97 = (bf16[512,704]{0,1:T(8,128)(2,1)S(1)}, bf16[512,704]{0,1:T(8,128)(2,1)S(1)}, u32[]{:S(2)}, u32[]{:S(2)}) collective-permute-start(bf16[512,704]{0,1:T(8,128)(2,1)S(1)} %convolution_convert_fusion.5), channel_id=1, source_target_pairs={{0,4},{1,5},{2,6},{3,7},{4,0},{5,1},{6,2},{7,3},{8,12},{9,13},{10,... | collective-permute-start | bytes 2162696 | tf_op jit(solution)/shard_map/ppermute | solution.py:78
  479.4 62.4 %collective-permute-start.99 = (bf16[512,704]{0,1:T(8,128)(2,1)S(1)}, bf16[512,704]{0,1:T(8,128)(2,1)S(1)}, u32[]{:S(2)}, u32[]{:S(2)}) collective-permute-start(bf16[512,704]{0,1:T(8,128)(2,1)S(1)} %convolution_convert_fusion.4), channel_id=1, source_target_pairs={{0,4},{1,5},{2,6},{3,7},{4,0},{5,1},{6,2},{7,3},{8,12},{9,13},{10,... | collective-permute-start | bytes 2162696 | tf_op jit(solution)/shard_map/ppermute | solution.py:78
  541.9 130.1 %collective-permute-start.93 = (bf16[512,1408]{0,1:T(8,128)(2,1)}, bf16[512,1408]{0,1:T(8,128)(2,1)}, u32[]{:S(2)}, u32[]{:S(2)}) collective-permute-start(bf16[512,1408]{0,1:T(8,128)(2,1)} %convolution_convert_fusion), channel_id=1, source_target_pairs={{0,4},{1,5},{2,6},{3,7},{4,0},{5,1},{6,2},{7,3},{8,12},{9,13},{10,... | collective-permute-start | bytes 4325384 | tf_op jit(solution)/shard_map/ppermute | solution.py:78
  566.6 105.5 %collective-permute-start.92 = (bf16[512,1408]{0,1:T(8,128)(2,1)}, bf16[512,1408]{0,1:T(8,128)(2,1)}, u32[]{:S(2)}, u32[]{:S(2)}) collective-permute-start(bf16[512,1408]{0,1:T(8,128)(2,1)} %fusion.12), channel_id=1, source_target_pairs={{0,16},{1,17},{2,18},{3,19},{4,20},{5,21},{6,22},{7,23},{8,24},{9,... | collective-permute-start | bytes 4325384 | tf_op jit(solution)/shard_map/ppermute | solution.py:88
  582.5 53.8 %collective-permute-start.61 = (bf16[128,2048]{0,1:T(8,128)(2,1)}, bf16[128,2048]{0,1:T(8,128)(2,1)}, u32[]{:S(2)}, u32[]{:S(2)}) collective-permute-start(bf16[128,2048]{0,1:T(8,128)(2,1)} %get-tuple-element.120), channel_id=1, source_target_pairs={{0,8},{1,9},{2,10},{3,11},{4,12},{5,13},{6,14},{7,15},{8,0},{9,1},... | collective-permute-start | bytes 1572872 | tf_op jit(solution)/shard_map/ppermute | solution.py:78
  702.5 113.6 %collective-permute-start.95 = (bf16[128,2816]{0,1:T(8,128)(2,1)}, bf16[128,2816]{0,1:T(8,128)(2,1)}, u32[]{:S(2)}, u32[]{:S(2)}) collective-permute-start(bf16[128,2816]{0,1:T(8,128)(2,1)} %get-tuple-element.138), channel_id=1, source_target_pairs={{0,2},{1,3},{2,0},{3,1},{4,6},{5,7},{6,4},{7,5},{8,10},{9,11},{10,... | collective-permute-start | bytes 2162696 | tf_op jit(solution)/shard_map/ppermute | solution.py:78
  762.0 125.0 %collective-permute-start.70 = (bf16[512,2048]{0,1:T(8,128)(2,1)}, bf16[512,2048]{0,1:T(8,128)(2,1)}, u32[]{:S(2)}, u32[]{:S(2)}) collective-permute-start(bf16[512,2048]{0,1:T(8,128)(2,1)} %pad_maximum_fusion.7), channel_id=1, source_target_pairs={{0,1},{1,0},{2,3},{3,2},{4,5},{5,4},{6,7},{7,6},{8,9},{9,8},{10,11... | collective-permute-start | bytes 6291464 | tf_op jit(solution)/shard_map/ppermute | solution.py:78
  762.2 108.4 %collective-permute-start.81 = (bf16[512,768]{1,0:T(8,128)(2,1)}, bf16[512,768]{1,0:T(8,128)(2,1)}, u32[]{:S(2)}, u32[]{:S(2)}) collective-permute-start(bf16[512,768]{1,0:T(8,128)(2,1)} %convolution_convert_fusion.2), channel_id=1, source_target_pairs={{0,4},{1,5},{2,6},{3,7},{4,0},{5,1},{6,2},{7,3},{8,12},{9,13},{10,... | collective-permute-start | bytes 2359304 | tf_op jit(solution)/shard_map/ppermute | solution.py:78
  (236 other events, 4177.0 us)

commit v2 on v1

--- a/solution.py
+++ b/solution.py
@@ -1,6 +1,11 @@
+import functools
+import math
+
 import jax
 import jax.numpy as jnp
 from jax import lax
+from jax.experimental import pallas as pl
+from jax.experimental.pallas import tpu as pltpu
 from jax.sharding import PartitionSpec as P
 
 HEADS = 32
@@ -72,6 +77,7 @@
         self.e = spot % 2
         self.x = side // 2
         self.c = side % 2
+        self.slot = jnp.reshape(self.b * 4 + side, (1,)).astype(jnp.int32)
 
     def flip(self, values, c=0, x=0, e=0, b=0):
         mask = c + 2 * x + self.seq * (e + 2 * b)
@@ -100,30 +106,46 @@
     )
 
 
-def to_relative(at, values):
-    width = values.shape[-1] // (at.outer * 4)
-    parts = []
-    for i in range(at.outer):
-        for j in range(2):
-            for k in range(2):
-                spot = (((at.a + i) % at.outer) * 2 + k) * 2 + (at.e ^ j)
-                parts.append(
-                    lax.dynamic_slice_in_dim(values, spot * width, width, values.ndim - 1)
-                )
-    return jnp.concatenate(parts, axis=-1)
-
-
-def to_absolute(at, values):
-    width = values.shape[-1] // (at.outer * 4)
-    parts = []
-    for i in range(at.outer):
-        for k in range(2):
-            for j in range(2):
-                spot = (((i - at.a) % at.outer) * 2 + (at.e ^ j)) * 2 + k
-                parts.append(
-                    lax.dynamic_slice_in_dim(values, spot * width, width, values.ndim - 1)
-                )
-    return jnp.concatenate(parts, axis=-1)
+def order_kernel(width, spots_ref, *refs):
+    half = len(refs) // 2
+    for ref, out in zip(refs[:half], refs[half:]):
+        for i in range(ref.shape[1] // width):
+            start = pl.multiple_of(spots_ref[i] * width, 128)
+            out[:, i * width : (i + 1) * width] = ref[:, pl.ds(start, width)]
+
+
+def reorder(spots, arrays):
+    width = arrays[0].shape[1] // len(spots)
+    if width % 128:
+        return [
+            jnp.concatenate(
+                [lax.dynamic_slice_in_dim(v, spot * width, width, 1) for spot in spots], axis=1
+            )
+            for v in arrays
+        ]
+    order = jnp.stack(spots).astype(jnp.int32)
+    outs = [(v.shape, v.dtype) for v in arrays]
+    return call(functools.partial(order_kernel, width), outs, order, *arrays)
+
+
+def to_relative(at, *arrays):
+    spots = [
+        (((at.a + i) % at.outer) * 2 + k) * 2 + (at.e ^ j)
+        for i in range(at.outer)
+        for j in range(2)
+        for k in range(2)
+    ]
+    return reorder(spots, arrays)
+
+
+def to_absolute(at, *arrays):
+    spots = [
+        (((i - at.a) % at.outer) * 2 + (at.e ^ j)) * 2 + k
+        for i in range(at.outer)
+        for k in range(2)
+        for j in range(2)
+    ]
+    return reorder(spots, arrays)
 
 
 def gather_tokens(at, values):
@@ -147,35 +169,119 @@
     return out
 
 
-def fetch(at, weights, parts):
-    pieces = []
-    for w, n in zip(weights, parts):
-        width = w.shape[1] // (8 * n)
-        for p in range(n):
-            pieces.append(
-                [w[:, (p * 8 + j) * width : (p * 8 + j + 1) * width] for j in range(8)]
-            )
-    def half(side):
-        return jnp.concatenate(
-            [
-                pick(side, piece[2 * g], piece[2 * g + 1])
-                for g in range(4)
-                for piece in pieces
-            ],
-            axis=1,
-        )
-
-    block = joined(at.c, half(at.c), at.flip(half(1 - at.c), c=1), 0)
-    wide = block.shape[1] // 4
-    quarter = [block[:, i * wide : (i + 1) * wide] for i in range(4)]
-    def side_of(side):
-        return jnp.concatenate(
-            [pick(side, quarter[0], quarter[1]), pick(side, quarter[2], quarter[3])], axis=1
-        )
-
-    block = joined(at.x, side_of(at.x), at.flip(side_of(1 - at.x), x=1), 0)
-    low, high = block[:, :wide], block[:, wide:]
-    block = joined(at.b, pick(at.b, low, high), at.flip(pick(at.b, high, low), b=1), 0)
+def call(kernel, outs, *args, flops=0):
+    size = sum(v.size * v.dtype.itemsize for v in args)
+    size += sum(math.prod(shape) * jnp.dtype(kind).itemsize for shape, kind in outs)
+    specs = [
+        pl.BlockSpec(memory_space=pltpu.SMEM if v.dtype == jnp.int32 else pltpu.VMEM)
+        for v in args
+    ]
+    return pl.pallas_call(
+        kernel,
+        out_shape=[jax.ShapeDtypeStruct(shape, kind) for shape, kind in outs],
+        in_specs=specs,
+        out_specs=[pl.BlockSpec(memory_space=pltpu.VMEM)] * len(outs),
+        compiler_params=pltpu.CompilerParams(vmem_limit_bytes=2 * size + 8 * 2**20),
+        cost_estimate=pl.CostEstimate(flops=flops, bytes_accessed=size, transcendentals=0),
+    )(*args)
+
+
+def block_at(ref, part, spot, width):
+    return ref[:, pl.ds(pl.multiple_of((part * 8 + spot) * width, 128), width)]
+
+
+def cut_kernel(parts, slot_ref, *refs):
+    slot = slot_ref[0]
+    weights, pieces = refs[: len(parts)], refs[len(parts) :]
+    col = 0
+    for ref, count in zip(weights, parts):
+        width = ref.shape[1] // (8 * count)
+        for p in range(count):
+            if width % 128 == 0:
+                for d in range(8):
+                    pieces[d][:, col : col + width] = block_at(ref, p, slot ^ d, width)
+            else:
+                for d in range(0, 8, 2):
+                    spot = slot ^ d
+                    start = (p * 4 + spot // 2) * 2 * width
+                    both = ref[:, pl.ds(pl.multiple_of(start, 128), 2 * width)]
+                    even = spot % 2 == 0
+                    low, high = both[:, :width], both[:, width:]
+                    pieces[d][:, col : col + width] = jnp.where(even, low, high)
+                    pieces[d + 1][:, col : col + width] = jnp.where(even, high, low)
+            col += width
+
+
+def place_kernel(slot_ref, *refs):
+    slot = slot_ref[0]
+    pieces, outs = refs[:8], refs[8:]
+    rows = pieces[0].shape[0]
+    for d in range(8):
+        start = pl.multiple_of((slot ^ d) * rows, rows)
+        col = 0
+        for out in outs:
+            out[pl.ds(start, rows), :] = pieces[d][:, col : col + out.shape[1]]
+            col += out.shape[1]
+
+
+def sum_cut_kernel(count, slot_ref, *refs):
+    slot = slot_ref[0]
+    terms, pieces = refs[:count], refs[count:]
+    rows = pieces[0].shape[0]
+    for d in range(8):
+        span = pl.ds(pl.multiple_of((slot ^ d) * rows, rows), rows)
+        total = terms[0][span, :].astype(F32)
+        for term in terms[1:]:
+            total = total + term[span, :].astype(F32)
+        pieces[d][...] = total.astype(BF16)
+
+
+def spread_kernel(counts, slot_ref, *refs):
+    slot = slot_ref[0]
+    pieces, outs = refs[:8], refs[8:]
+    col = 0
+    for out, count in zip(outs, counts):
+        width = out.shape[1] // (8 * count)
+        for p in range(count):
+            if width % 128 == 0:
+                for d in range(8):
+                    start = pl.multiple_of((p * 8 + (slot ^ d)) * width, 128)
+                    out[:, pl.ds(start, width)] = pieces[d][:, col : col + width].astype(F32)
+            else:
+                for d in range(0, 8, 2):
+                    spot = slot ^ d
+                    even = spot % 2 == 0
+                    one = pieces[d][:, col : col + width].astype(F32)
+                    two = pieces[d + 1][:, col : col + width].astype(F32)
+                    both = jnp.concatenate(
+                        [jnp.where(even, one, two), jnp.where(even, two, one)], axis=1
+                    )
+                    start = pl.multiple_of((p * 4 + spot // 2) * 2 * width, 128)
+                    out[:, pl.ds(start, 2 * width)] = both
+            col += width
+
+
+def exchange(at, pieces):
+    return [pieces[0]] + [
+        at.flip(pieces[d], b=d // 4, x=(d // 2) % 2, c=d % 2) for d in range(1, 8)
+    ]
+
+
+def fetch_group(at, weights, parts, splits):
+    rows = weights[0].shape[0]
+    wide = sum(w.shape[1] for w in weights) // 8
+    pieces = call(
+        functools.partial(cut_kernel, parts),
+        [((rows, wide), BF16)] * 8,
+        at.slot,
+        *weights,
+    )
+    return call(
+        place_kernel, [((8 * rows, n), BF16) for n in splits], at.slot, *exchange(at, pieces)
+    )
+
+
+def fetch_blocks(at, block):
     blocks = []
     for i in range(at.outer):
         here = block if i == 0 else at.shift(block, i)
@@ -184,49 +290,27 @@
     return blocks
 
 
-def deliver(at, make, parts):
+def deliver(at, make, counts, widths):
     outer = at.outer
     sent = [at.flip(make(2 * i + 1, BF16), e=1) for i in range(outer)]
-    total = None
-    for i in list(range(1, outer)) + [0]:
+    terms = []
+    for i in range(1, outer):
         here = make(2 * i, F32) + sent[i].astype(F32)
-        if i:
-            here = at.push(here.astype(BF16), i).astype(F32)
-        total = here if total is None else total + here
-    block = total.astype(BF16)
-    rows = block.shape[0] // 2
-    low, high = block[:rows], block[rows:]
-    block = joined(at.b, pick(at.b, low, high), at.flip(pick(at.b, high, low), b=1), 1)
-    rows = rows // 2
-    low, high = block[:rows], block[rows:]
-    own, other = pick(at.x, low, high), at.flip(pick(at.x, high, low), x=1)
-    wide = own.shape[1] // 2
-    block = jnp.concatenate(
-        [
-            joined(at.x, own[:, :wide], other[:, :wide], 1),
-            joined(at.x, own[:, wide:], other[:, wide:], 1),
-        ],
-        axis=1,
-    )
-    rows = rows // 2
-    low, high = block[:rows], block[rows:]
-    own, other = pick(at.c, low, high), at.flip(pick(at.c, high, low), c=1)
-    width = wide // parts
-    outs = []
-    for p in range(parts):
-        cols = []
-        for g in range(4):
-            at_col = (g * parts + p) * width
-            cols.append(
-                joined(
-                    at.c,
-                    own[:, at_col : at_col + width].astype(F32),
-                    other[:, at_col : at_col + width].astype(F32),
-                    1,
-                )
-            )
-        outs.append(jnp.concatenate(cols, axis=1))
-    return outs
+        terms.append(at.push(here.astype(BF16), i))
+    terms = [make(0, F32), sent[0]] + terms
+    rows = terms[0].shape[0] // 8
+    pieces = call(
+        functools.partial(sum_cut_kernel, len(terms)),
+        [((rows, terms[0].shape[1]), BF16)] * 8,
+        at.slot,
+        *terms,
+    )
+    return call(
+        functools.partial(spread_kernel, counts),
+        [((rows, n), F32) for n in widths],
+        at.slot,
+        *exchange(at, pieces),
+    )
 
 
 def fetch_small(at, values):
@@ -285,10 +369,14 @@
     step = width // (2 * at.outer)
     slot = at.b * 4 + at.x * 2 + at.c
 
-    inputs_low = to_relative(at, layer_input)
+    qkv_block, out_block = fetch_group(
+        at, [qkv_weight, out_weight], (3, 1), (3 * part, part)
+    )
+    qkv_blocks = fetch_blocks(at, qkv_block)
+    out_blocks = fetch_blocks(at, out_block)
+    inputs_low, cotangent_low = to_relative(at, layer_input, cotangent)
     inputs = inputs_low.astype(F32)
     inputs_all = gather_tokens(at, inputs_low)
-    qkv_blocks = fetch(at, [qkv_weight], [3])
     small = fetch_small(
         at, jnp.concatenate([qkv_bias, ln1_gain, ln1_bias, ln2_gain, ln2_bias])
     )
@@ -354,14 +442,15 @@
         jnp.einsum("bhtl,bhld->bhtd", probs_low, value, preferred_element_type=F32)
     ).astype(BF16)
 
-    out_blocks = fetch(at, [out_weight], [1])
     hidden = inputs + expand(attended, out_blocks)
     normed2 = layer_norm(hidden, gain_two, shift_two).astype(BF16)
     normed2_all = gather_tokens(at, normed2)
-    pair_blocks = fetch(at, [gate_weight, up_weight], [1, 1])
-    cotangent_low = to_relative(at, cotangent)
+    pair_block, down_block = fetch_group(
+        at, [gate_weight, up_weight, down_weight], (1, 1, 1), (2 * units, units)
+    )
+    pair_blocks = fetch_blocks(at, pair_block)
+    down_blocks = fetch_blocks(at, down_block)
     cotangent_all = gather_tokens(at, cotangent_low)
-    down_blocks = fetch(at, [down_weight], [1])
 
     gate_up = contract(normed2_all, pair_blocks)
     gate = gate_up[:, :units]
@@ -370,7 +459,7 @@
     silu = gate * sigmoid
     inner = (silu * up).astype(BF16)
     down_grads = deliver(
-        at, lambda i, kind: dot_rows(cut(cotangent_all, i), inner, kind), 1
+        at, lambda i, kind: dot_rows(cut(cotangent_all, i), inner, kind), (1,), (8 * units,)
     )
     inner_grad = contract(cotangent_all, down_blocks)
     gate_grad = inner_grad * up * sigmoid * (1.0 + gate * (1.0 - sigmoid))
@@ -378,16 +467,16 @@
     pair_low = jnp.concatenate([gate_grad.astype(BF16), up_grad.astype(BF16)], axis=1)
     normed2_grad = expand(pair_low, pair_blocks)
     pair_grads = deliver(
-        at, lambda i, kind: dot_rows(cut(normed2_all, i), pair_low, kind), 2
-    )
-    result = to_absolute(at, hidden + expand(inner, down_blocks))
+        at, lambda i, kind: dot_rows(cut(normed2_all, i), pair_low, kind), (1, 1), (8 * units,) * 2
+    )
+    result = (hidden + expand(inner, down_blocks)).astype(BF16)
 
     hidden_part, gain_two_grad, shift_two_grad = norm_back(hidden, gain_two, normed2_grad)
     hidden_grad = cotangent_low.astype(F32) + hidden_part
     branch_all = gather_tokens(at, hidden_grad.astype(BF16))
     attended_grad = by_sequence(contract(branch_all, out_blocks), heads_here).astype(BF16)
     out_grads = deliver(
-        at, lambda i, kind: dot_rows(cut(branch_all, i), attended, kind), 1
+        at, lambda i, kind: dot_rows(cut(branch_all, i), attended, kind), (1,), (8 * part,)
     )
     value_grad = jnp.einsum(
         "bhtl,bhtd->bhld", probs_low, attended_grad, preferred_element_type=F32
@@ -412,11 +501,11 @@
         axis=1,
     ).astype(BF16)
     qkv_grads = deliver(
-        at, lambda i, kind: dot_rows(cut(normed_all, i), mixed_low, kind), 3
+        at, lambda i, kind: dot_rows(cut(normed_all, i), mixed_low, kind), (3,), (24 * part,)
     )
     normed_grad = expand(mixed_low, qkv_blocks)
     input_part, gain_one_grad, shift_one_grad = norm_back(inputs, gain_one, normed_grad)
-    input_grad = to_absolute(at, hidden_grad + input_part)
+    result, input_grad = to_absolute(at, result, hidden_grad + input_part)
 
     bias_part = jnp.sum(mixed_low.astype(F32), axis=0).reshape(3, 1, part)
     own_slot = (jnp.arange(8) == slot).astype(F32)[None, :, None]
@@ -433,11 +522,11 @@
         return shares[bias_rows + i * rows : bias_rows + (i + 1) * rows]
 
     return (
-        result.astype(BF16),
+        result,
         input_grad,
         share(0),
         share(1),
-        jnp.concatenate(qkv_grads, axis=1),
+        qkv_grads[0],
         shares[:bias_rows],
         out_grads[0],
         share(2),

time: 955 us -> 769 us (0.81)
  waiting for transfers between devices: 414 us -> 306 us
  other arithmetic: 129 us -> 36.1 us
  matrix products: 151 us -> 131 us
  Pallas kernels: 0 us -> 18.9 us
  starting transfers between devices: 87.2 us -> 106 us
    ppermute x93 -> x111, waiting for transfers between devices: 371 us -> 232 us  [flip(): lax.ppermute(values, AXES, [(i, i ^ mask) for i in range(self.count)])]
    select_n x74 -> x13, other arithmetic: 45.1 us -> 0.13 us  [pick(): return jnp.where(bit == 0, first, second)]
    ppermute x93 -> x111, starting transfers between devices: 69.4 us -> 92.7 us  [flip(): lax.ppermute(values, AXES, [(i, i ^ mask) for i in range(self.count)])]
    ppermute x5, waiting for transfers between devices: 10.1 us -> 32.8 us  [shift(): lax.ppermute(values, AXES, [((i + steps * stride) % self.count, i) for i...]
    pallas_call x0 -> x14, Pallas kernels: none -> 18.9 us  [call(): pl.pallas_call(kernel, out_shape=[jax.ShapeDtypeStruct(shape, kind) for s...]
    convert_element_type x19 -> x0, other arithmetic: 15.6 us -> none  [the longest x14 10.9 us: deliver(): other[:, at_col:at_col + width].astype(F32)]
    unnamed x428 -> x368, local copies, waits for them, and re-layouts: 96.5 us -> 81.1 us
    unnamed x32 -> x3, other arithmetic: 15.6 us -> 3.04 us
  transfers between devices with their start and end apart: 103 -> 121, of which waited for: 46 -> 46; matrix products, arithmetic and copies ran while one was open for 43% -> 33% of each run, Pallas kernels for 0% -> 2%
where the time goes in v2:
time: 769 us; the launch traced here: 759 us
  waiting for transfers between devices  306 us (40%)
  local copies, waits for them, and re-layouts  157 us (20%)
  matrix products  131 us (17%)
  starting transfers between devices  106 us (14%)
  other arithmetic  36.1 us (5%)
  Pallas kernels  18.9 us (2%)
    ppermute x111, waiting for transfers between devices, flip(): lax.ppermute(values, AXES, [(i, i ^ mask) for i in range(self.count)])  232 us
    ppermute x111, starting transfers between devices, flip(): lax.ppermute(values, AXES, [(i, i ^ mask) for i in range(self.count)])  92.7 us
    unnamed x368, local copies, waits for them, and re-layouts  81.1 us
    ppermute x5, waiting for transfers between devices, push(): lax.ppermute(values, AXES, [(i, (i + steps * stride) % self.count) for i...  41 us
    dot_general x32, matrix products, dot_cols(): lax.dot_general(left, right, (((1,), (1,)), ((), ())), preferred_element_...  38.7 us
    dot_general x16, matrix products, dot(): return jnp.dot(left, right, preferred_element_type=F32)  38.6 us
    ppermute x5, waiting for transfers between devices, shift(): lax.ppermute(values, AXES, [((i + steps * stride) % self.count, i) for i...  32.8 us
    dot_general x16, matrix products, dot_rows(): lax.dot_general(left, right, (((0,), (0,)), ((), ())), preferred_element_...  32 us
  transfers between devices with their start and end apart: 121, of which 46 were waited for; matrix products, arithmetic and copies ran while one was open for 33% of the time, Pallas kernels for 2%

profile of v2, /device:TPU:0, one launch (start us, length us, event | category | flops | bytes accessed | tf_op | source)
XLA Modules:
  0.0 758.8 jit_solution(15427944539186818867)
XLA Ops:
  61.6 4.8 collective-permute-done.39.refs_3_
  69.8 8.9 %collective-permute-done.41.refs_5_ = bf16[64,2112]{1,0:T(8,128)(2,1)S(1)} collective-permute-done((bf16[64,2112]{1,0:T(8,128)(2,1)}, bf16[64,2112]{1,0:T(8,128)(2,1)S(1)}, u32[]{:S(2)}, u32[]{:S(2)}) %collective-permute-start.41) | collective-permute-done | bytes 270368 | tf_op jit(solution)/shard_map/ppermute | solution.py:84
  115.9 16.1 %collective-permute-done.55 = bf16[128,2048]{1,0:T(8,128)(2,1)S(1)} collective-permute-done((bf16[128,2048]{1,0:T(8,128)(2,1)S(1)}, bf16[128,2048]{1,0:T(8,128)(2,1)S(1)}, u32[]{:S(2)}, u32[]{:S(2)}) %collective-permute-start.55) | collective-permute-done | bytes 524320 | tf_op jit(solution)/shard_map/ppermute | solution.py:84
  136.6 4.7 collective-permute-done.21
  157.9 13.5 %collective-permute-done.22 = bf16[512,768]{1,0:T(8,128)(2,1)S(1)} collective-permute-done((bf16[512,768]{1,0:T(8,128)(2,1)S(1)}, bf16[512,768]{1,0:T(8,128)(2,1)S(1)}, u32[]{:S(2)}, u32[]{:S(2)}) %collective-permute-start.22) | collective-permute-done | bytes 786464 | tf_op jit(solution)/shard_map/ppermute | solution.py:84
  208.8 7.9 %fusion.162 = (f32[2,4,512]{2,1,0:T(4,128)S(1)}, f32[2,4,512,512]{2,3,1,0:T(8,128)}) fusion(pred[2,512,512]{1,2,0:T(8,128)(4,1)} %compare_and_fusion, bf16[2,4,512,48]{2,3,1,0:T(8,128)(2,1)S(1)} %slice.717, bf16[2,4,512,8]{2,3,1,0:T(8,128)(2,1)S(1)} %get-tuple-element.188, bf16[2,4,512,8]{2,3,1,0:T(8,128)(2,1)S(1)} %get-tuple-element.189, ...), kind=kOutput, calls=%fused_computation.347 | convolution fusion | flops 279970304 | bytes 9977856 | tf_op jit(solution)/shard_map/sub | solution.py:437
  238.8 26.1 %collective-permute-done.48 = bf16[512,704]{0,1:T(8,128)(2,1)S(1)} collective-permute-done((bf16[512,704]{0,1:T(8,128)(2,1)S(1)}, bf16[512,704]{0,1:T(8,128)(2,1)S(1)}, u32[]{:S(2)}, u32[]{:S(2)}) %collective-permute-start.48) | collective-permute-done | bytes 720928 | tf_op jit(solution)/shard_map/ppermute | solution.py:88
  273.0 4.6 collective-permute-done.28
  282.7 6.5 collective-permute-done.47
  298.5 9.2 %collective-permute-done.32 = bf16[128,2048]{1,0:T(8,128)(2,1)S(1)} collective-permute-done((bf16[128,2048]{1,0:T(8,128)(2,1)}, bf16[128,2048]{1,0:T(8,128)(2,1)S(1)}, u32[]{:S(2)}, u32[]{:S(2)}) %collective-permute-start.32) | collective-permute-done | bytes 524320 | tf_op jit(solution)/shard_map/ppermute | solution.py:84
  321.4 5.6 fusion.79
  327.0 32.1 %collective-permute-done.46 = bf16[512,1408]{1,0:T(8,128)(2,1)S(1)} collective-permute-done((bf16[512,1408]{1,0:T(8,128)(2,1)}, bf16[512,1408]{1,0:T(8,128)(2,1)S(1)}, u32[]{:S(2)}, u32[]{:S(2)}) %collective-permute-start.46) | collective-permute-done | bytes 1441824 | tf_op jit(solution)/shard_map/ppermute | solution.py:84
  359.1 5.7 add_add_fusion
  364.9 4.9 multiply_convert_fusion.1
  410.9 27.5 %collective-permute-done.112 = bf16[512,704]{0,1:T(8,128)(2,1)} collective-permute-done((bf16[512,704]{0,1:T(8,128)(2,1)}, bf16[512,704]{0,1:T(8,128)(2,1)}, u32[]{:S(2)}, u32[]{:S(2)}) %collective-permute-start.112) | collective-permute-done | bytes 720928 | tf_op jit(solution)/shard_map/ppermute | solution.py:84
  449.1 5.1 collective-permute-done.53
  454.3 17.6 %collective-permute-done.52 = bf16[128,2048]{1,0:T(8,128)(2,1)S(1)} collective-permute-done((bf16[128,2048]{1,0:T(8,128)(2,1)S(1)}, bf16[128,2048]{1,0:T(8,128)(2,1)S(1)}, u32[]{:S(2)}, u32[]{:S(2)}) %collective-permute-start.52) | collective-permute-done | bytes 524320 | tf_op jit(solution)/shard_map/ppermute | solution.py:84
  480.1 14.6 %collective-permute-done.111 = bf16[512,704]{0,1:T(8,128)(2,1)S(1)} collective-permute-done((bf16[512,704]{0,1:T(8,128)(2,1)S(1)}, bf16[512,704]{0,1:T(8,128)(2,1)S(1)}, u32[]{:S(2)}, u32[]{:S(2)}) %collective-permute-start.111) | collective-permute-done | bytes 720928 | tf_op jit(solution)/shard_map/ppermute | solution.py:84
  495.0 25.6 %collective-permute-done.113 = bf16[512,704]{0,1:T(8,128)(2,1)S(1)} collective-permute-done((bf16[512,704]{0,1:T(8,128)(2,1)S(1)}, bf16[512,704]{0,1:T(8,128)(2,1)S(1)}, u32[]{:S(2)}, u32[]{:S(2)}) %collective-permute-start.113) | collective-permute-done | bytes 720928 | tf_op jit(solution)/shard_map/ppermute | solution.py:94
  532.8 14.5 %collective-permute-done.103.refs_2_ = bf16[512,1408]{1,0:T(8,128)(2,1)} collective-permute-done((bf16[512,1408]{1,0:T(8,128)(2,1)}, bf16[512,1408]{1,0:T(8,128)(2,1)}, u32[]{:S(2)}, u32[]{:S(2)}) %collective-permute-start.103) | collective-permute-done | bytes 1441824 | tf_op jit(solution)/shard_map/ppermute | solution.py:94
  571.9 5.2 multiply_reduce_fusion
  577.1 4.8 multiply_convert_fusion
  662.5 15.5 %collective-permute-done.75 = bf16[128,2048]{1,0:T(8,128)(2,1)S(1)} collective-permute-done((bf16[128,2048]{1,0:T(8,128)(2,1)S(1)}, bf16[128,2048]{1,0:T(8,128)(2,1)S(1)}, u32[]{:S(2)}, u32[]{:S(2)}) %collective-permute-start.75) | collective-permute-done | bytes 524320 | tf_op jit(solution)/shard_map/ppermute | solution.py:84
  679.5 8.6 %collective-permute-done.74 = bf16[128,2048]{1,0:T(8,128)(2,1)S(1)} collective-permute-done((bf16[128,2048]{1,0:T(8,128)(2,1)S(1)}, bf16[128,2048]{1,0:T(8,128)(2,1)S(1)}, u32[]{:S(2)}, u32[]{:S(2)}) %collective-permute-start.74) | collective-permute-done | bytes 524320 | tf_op jit(solution)/shard_map/ppermute | solution.py:84
  (823 shorter events, 466.0 us)
Async XLA Ops:
  55.6 44.8 %collective-permute-start.1 = (bf16[128,2048]{1,0:T(8,128)(2,1)S(1)}, bf16[128,2048]{1,0:T(8,128)(2,1)}, u32[]{:S(2)}, u32[]{:S(2)}) collective-permute-start(bf16[128,2048]{1,0:T(8,128)(2,1)S(1)} %get-tuple-element.70), channel_id=1, source_target_pairs={{0,2},{1,3},{2,0},{3,1},{4,6},{5,7},{6,4},{7,5},{8,10},{9,11},{10,... | collective-permute-start | bytes 1572872 | tf_op jit(solution)/shard_map/ppermute | solution.py:84
  57.2 45.8 %collective-permute-start.2 = (bf16[128,2048]{1,0:T(8,128)(2,1)S(1)}, bf16[128,2048]{1,0:T(8,128)(2,1)}, u32[]{:S(2)}, u32[]{:S(2)}) collective-permute-start(bf16[128,2048]{1,0:T(8,128)(2,1)S(1)} %get-tuple-element.70), channel_id=1, source_target_pairs={{0,8},{1,9},{2,10},{3,11},{4,12},{5,13},{6,14},{7,15},{8,0},{9,1},... | collective-permute-start | bytes 1572872 | tf_op jit(solution)/shard_map/ppermute | solution.py:84
  103.0 124.8 %collective-permute-start.56 = (bf16[128,2048]{1,0:T(8,128)(2,1)S(1)}, bf16[128,2048]{1,0:T(8,128)(2,1)}, u32[]{:S(2)}, u32[]{:S(2)}) collective-permute-start(bf16[128,2048]{1,0:T(8,128)(2,1)S(1)} %get-tuple-element.91), channel_id=1, source_target_pairs={{0,10},{1,11},{2,8},{3,9},{4,14},{5,15},{6,12},{7,13},{8,2},{9,3},... | collective-permute-start | bytes 1572872 | tf_op jit(solution)/shard_map/ppermute | solution.py:84
  132.9 96.4 %collective-permute-start.57 = (bf16[128,2048]{1,0:T(8,128)(2,1)S(1)}, bf16[128,2048]{1,0:T(8,128)(2,1)}, u32[]{:S(2)}, u32[]{:S(2)}) collective-permute-start(bf16[128,2048]{1,0:T(8,128)(2,1)S(1)} %get-tuple-element.91), channel_id=1, source_target_pairs={{0,1},{1,0},{2,3},{3,2},{4,5},{5,4},{6,7},{7,6},{8,9},{9,8},{10,11... | collective-permute-start | bytes 1572872 | tf_op jit(solution)/shard_map/ppermute | solution.py:84
  156.2 70.7 %collective-permute-start.23 = (bf16[512,256]{1,0:T(8,128)(2,1)S(1)}, bf16[512,256]{1,0:T(8,128)(2,1)S(1)}, u32[]{:S(2)}, u32[]{:S(2)}) collective-permute-start(bf16[512,256]{1,0:T(8,128)(2,1)S(1)} %get-tuple-element.80), channel_id=1, source_target_pairs={{0,4},{1,5},{2,6},{3,7},{4,0},{5,1},{6,2},{7,3},{8,12},{9,13},{10,... | collective-permute-start | bytes 786440 | tf_op jit(solution)/shard_map/ppermute | solution.py:84
  157.8 152.2 %collective-permute-start.45 = (bf16[512,1408]{1,0:T(8,128)(2,1)}, bf16[512,1408]{1,0:T(8,128)(2,1)}, u32[]{:S(2)}, u32[]{:S(2)}) collective-permute-start(bf16[512,1408]{1,0:T(8,128)(2,1)} %get-tuple-element.89), channel_id=1, source_target_pairs={{16,0},{17,1},{18,2},{19,3},{20,4},{21,5},{22,6},{23,7},{24,8},{25... | collective-permute-start | bytes 4325384 | tf_op jit(solution)/shard_map/ppermute | solution.py:88
  171.5 53.6 %collective-permute-start.25 = (bf16[512,256]{1,0:T(8,128)(2,1)S(1)}, bf16[512,256]{1,0:T(8,128)(2,1)}, u32[]{:S(2)}, u32[]{:S(2)}) collective-permute-start(bf16[512,256]{1,0:T(8,128)(2,1)S(1)} %collective-permute-done.24), channel_id=1, source_target_pairs={{0,4},{1,5},{2,6},{3,7},{4,0},{5,1},{6,2},{7,3},{8,12},{9,13},{10,... | collective-permute-start | bytes 786440 | tf_op jit(solution)/shard_map/ppermute | solution.py:84
  230.6 90.8 %collective-permute-start.44 = (bf16[512,1408]{1,0:T(8,128)(2,1)}, bf16[512,1408]{1,0:T(8,128)(2,1)}, u32[]{:S(2)}, u32[]{:S(2)}) collective-permute-start(bf16[512,1408]{1,0:T(8,128)(2,1)} %get-tuple-element.89), channel_id=1, source_target_pairs={{0,4},{1,5},{2,6},{3,7},{4,0},{5,1},{6,2},{7,3},{8,12},{9,13},{10,... | collective-permute-start | bytes 4325384 | tf_op jit(solution)/shard_map/ppermute | solution.py:84
  309.9 54.9 %collective-permute-start.49 = (bf16[512,704]{0,1:T(8,128)(2,1)}, bf16[512,704]{0,1:T(8,128)(2,1)S(1)}, u32[]{:S(2)}, u32[]{:S(2)}) collective-permute-start(bf16[512,704]{0,1:T(8,128)(2,1)} %copy-done.115), channel_id=1, source_target_pairs={{0,4},{1,5},{2,6},{3,7},{4,0},{5,1},{6,2},{7,3},{8,12},{9,13},{10,... | collective-permute-start | bytes 2162696 | tf_op jit(solution)/shard_map/ppermute | solution.py:84
  311.5 47.6 %collective-permute-start.46 = (bf16[512,1408]{1,0:T(8,128)(2,1)}, bf16[512,1408]{1,0:T(8,128)(2,1)S(1)}, u32[]{:S(2)}, u32[]{:S(2)}) collective-permute-start(bf16[512,1408]{1,0:T(8,128)(2,1)} %collective-permute-done.45), channel_id=1, source_target_pairs={{0,4},{1,5},{2,6},{3,7},{4,0},{5,1},{6,2},{7,3},{8,12},{9,13},{10,... | collective-permute-start | bytes 4325384 | tf_op jit(solution)/shard_map/ppermute | solution.py:84
  389.2 49.5 %collective-permute-start.102 = (bf16[512,1408]{1,0:T(8,128)(2,1)S(1)}, bf16[512,1408]{1,0:T(8,128)(2,1)S(1)}, u32[]{:S(2)}, u32[]{:S(2)}) collective-permute-start(bf16[512,1408]{1,0:T(8,128)(2,1)S(1)} %convolution_convert_fusion), channel_id=1, source_target_pairs={{0,4},{1,5},{2,6},{3,7},{4,0},{5,1},{6,2},{7,3},{8,12},{9,13},{10,... | collective-permute-start | bytes 4325384 | tf_op jit(solution)/shard_map/ppermute | solution.py:84
  390.8 47.6 %collective-permute-start.112 = (bf16[512,704]{0,1:T(8,128)(2,1)}, bf16[512,704]{0,1:T(8,128)(2,1)}, u32[]{:S(2)}, u32[]{:S(2)}) collective-permute-start(bf16[512,704]{0,1:T(8,128)(2,1)} %convolution_convert_fusion.4), channel_id=1, source_target_pairs={{0,4},{1,5},{2,6},{3,7},{4,0},{5,1},{6,2},{7,3},{8,12},{9,13},{10,... | collective-permute-start | bytes 2162696 | tf_op jit(solution)/shard_map/ppermute | solution.py:84
  447.0 85.8 %collective-permute-start.101 = (bf16[512,1408]{1,0:T(8,128)(2,1)}, bf16[512,1408]{1,0:T(8,128)(2,1)}, u32[]{:S(2)}, u32[]{:S(2)}) collective-permute-start(bf16[512,1408]{1,0:T(8,128)(2,1)} %convolution_convert_fusion.1), channel_id=1, source_target_pairs={{0,4},{1,5},{2,6},{3,7},{4,0},{5,1},{6,2},{7,3},{8,12},{9,13},{10,... | collective-permute-start | bytes 4325384 | tf_op jit(solution)/shard_map/ppermute | solution.py:84
  448.6 46.1 %collective-permute-start.111 = (bf16[512,704]{0,1:T(8,128)(2,1)S(1)}, bf16[512,704]{0,1:T(8,128)(2,1)S(1)}, u32[]{:S(2)}, u32[]{:S(2)}) collective-permute-start(bf16[512,704]{0,1:T(8,128)(2,1)S(1)} %convolution_convert_fusion.5), channel_id=1, source_target_pairs={{0,4},{1,5},{2,6},{3,7},{4,0},{5,1},{6,2},{7,3},{8,12},{9,13},{10,... | collective-permute-start | bytes 2162696 | tf_op jit(solution)/shard_map/ppermute | solution.py:84
  454.2 66.4 %collective-permute-start.113 = (bf16[512,704]{0,1:T(8,128)(2,1)S(1)}, bf16[512,704]{0,1:T(8,128)(2,1)S(1)}, u32[]{:S(2)}, u32[]{:S(2)}) collective-permute-start(bf16[512,704]{0,1:T(8,128)(2,1)S(1)} %fusion.19), channel_id=1, source_target_pairs={{0,16},{1,17},{2,18},{3,19},{4,20},{5,21},{6,22},{7,23},{8,24},{9,... | collective-permute-start | bytes 2162696 | tf_op jit(solution)/shard_map/ppermute | solution.py:94
  471.9 75.4 %collective-permute-start.103 = (bf16[512,1408]{1,0:T(8,128)(2,1)}, bf16[512,1408]{1,0:T(8,128)(2,1)}, u32[]{:S(2)}, u32[]{:S(2)}) collective-permute-start(bf16[512,1408]{1,0:T(8,128)(2,1)} %fusion.12), channel_id=1, source_target_pairs={{0,16},{1,17},{2,18},{3,19},{4,20},{5,21},{6,22},{7,23},{8,24},{9,... | collective-permute-start | bytes 4325384 | tf_op jit(solution)/shard_map/ppermute | solution.py:94
  475.6 77.5 %collective-permute-start.65 = (bf16[128,2048]{1,0:T(8,128)(2,1)}, bf16[128,2048]{1,0:T(8,128)(2,1)}, u32[]{:S(2)}, u32[]{:S(2)}) collective-permute-start(bf16[128,2048]{1,0:T(8,128)(2,1)} %get-tuple-element.140), channel_id=1, source_target_pairs={{0,2},{1,3},{2,0},{3,1},{4,6},{5,7},{6,4},{7,5},{8,10},{9,11},{10,... | collective-permute-start | bytes 1572872 | tf_op jit(solution)/shard_map/ppermute | solution.py:84
  494.7 59.8 %collective-permute-start.66 = (bf16[128,2048]{1,0:T(8,128)(2,1)}, bf16[128,2048]{1,0:T(8,128)(2,1)}, u32[]{:S(2)}, u32[]{:S(2)}) collective-permute-start(bf16[128,2048]{1,0:T(8,128)(2,1)} %get-tuple-element.140), channel_id=1, source_target_pairs={{0,8},{1,9},{2,10},{3,11},{4,12},{5,13},{6,14},{7,15},{8,0},{9,1},... | collective-permute-start | bytes 1572872 | tf_op jit(solution)/shard_map/ppermute | solution.py:84
  532.8 100.0 %collective-permute-start.114 = (bf16[64,704]{1,0:T(8,128)(2,1)}, bf16[64,704]{1,0:T(8,128)(2,1)S(1)}, u32[]{:S(2)}, u32[]{:S(2)}) collective-permute-start(bf16[64,704]{1,0:T(8,128)(2,1)} %copy-done.80), channel_id=1, source_target_pairs={{0,1},{1,0},{2,3},{3,2},{4,5},{5,4},{6,7},{7,6},{8,9},{9,8},{10,11... | collective-permute-start | bytes 270344 | tf_op jit(solution)/shard_map/ppermute | solution.py:84
  547.3 86.9 %collective-permute-start.115 = (bf16[64,704]{1,0:T(8,128)(2,1)}, bf16[64,704]{1,0:T(8,128)(2,1)S(1)}, u32[]{:S(2)}, u32[]{:S(2)}) collective-permute-start(bf16[64,704]{1,0:T(8,128)(2,1)} %copy-done.79), channel_id=1, source_target_pairs={{0,2},{1,3},{2,0},{3,1},{4,6},{5,7},{6,4},{7,5},{8,10},{9,11},{10,... | collective-permute-start | bytes 270344 | tf_op jit(solution)/shard_map/ppermute | solution.py:84
  560.6 76.0 %collective-permute-start.116 = (bf16[64,704]{1,0:T(8,128)(2,1)}, bf16[64,704]{1,0:T(8,128)(2,1)S(1)}, u32[]{:S(2)}, u32[]{:S(2)}) collective-permute-start(bf16[64,704]{1,0:T(8,128)(2,1)} %copy-done.78), channel_id=1, source_target_pairs={{0,3},{1,2},{2,1},{3,0},{4,7},{5,6},{6,5},{7,4},{8,11},{9,10},{10,... | collective-permute-start | bytes 270344 | tf_op jit(solution)/shard_map/ppermute | solution.py:84
  644.7 43.4 %collective-permute-start.74 = (bf16[128,2048]{1,0:T(8,128)(2,1)S(1)}, bf16[128,2048]{1,0:T(8,128)(2,1)S(1)}, u32[]{:S(2)}, u32[]{:S(2)}) collective-permute-start(bf16[128,2048]{1,0:T(8,128)(2,1)S(1)} %get-tuple-element.162), channel_id=1, source_target_pairs={{0,8},{1,9},{2,10},{3,11},{4,12},{5,13},{6,14},{7,15},{8,0},{9,1},... | collective-permute-start | bytes 1572872 | tf_op jit(solution)/shard_map/ppermute | solution.py:84
  654.6 56.2 %collective-permute-start.81 = (bf16[512,768]{1,0:T(8,128)(2,1)}, bf16[512,768]{1,0:T(8,128)(2,1)S(1)}, u32[]{:S(2)}, u32[]{:S(2)}) collective-permute-start(bf16[512,768]{1,0:T(8,128)(2,1)} %convolution_convert_fusion.3), channel_id=1, source_target_pairs={{0,4},{1,5},{2,6},{3,7},{4,0},{5,1},{6,2},{7,3},{8,12},{9,13},{10,... | collective-permute-start | bytes 2359304 | tf_op jit(solution)/shard_map/ppermute | solution.py:84
  656.4 55.2 %collective-permute-start.83 = (bf16[512,768]{1,0:T(8,128)(2,1)}, bf16[512,768]{1,0:T(8,128)(2,1)S(1)}, u32[]{:S(2)}, u32[]{:S(2)}) collective-permute-start(bf16[512,768]{1,0:T(8,128)(2,1)} %add_convert_fusion), channel_id=1, source_target_pairs={{0,16},{1,17},{2,18},{3,19},{4,20},{5,21},{6,22},{7,23},{8,24},{9,... | collective-permute-start | bytes 2359304 | tf_op jit(solution)/shard_map/ppermute | solution.py:94
  (266 other events, 3173.6 us)

commit v3 on v1

v3 whole, which is shorter than its diff:
```python
import functools
import math

import jax
import jax.numpy as jnp
from jax import lax
from jax.experimental import pallas as pl
from jax.experimental.layout import Layout, with_layout_constraint
from jax.experimental.pallas import tpu as pltpu
from jax.sharding import PartitionSpec as P

HEADS = 32
HEAD_DIM = 64
AXES = ("fsdp", "seq")
F32 = jnp.float32
BF16 = jnp.bfloat16


def centered_of(values):
    centered = values - jnp.mean(values, axis=-1, keepdims=True)
    spread = jnp.mean(centered * centered, axis=-1, keepdims=True)
    return centered, lax.rsqrt(spread + 1e-05)


def norm_back(values, gain, grad):
    centered, scale = centered_of(values)
    hat = centered * scale
    lifted = grad * gain
    inner = jnp.mean(lifted * hat, axis=-1, keepdims=True)
    pulled = scale * (lifted - jnp.mean(lifted, axis=-1, keepdims=True) - hat * inner)
    return (
        pulled,
        jnp.sum(grad * hat, axis=0, keepdims=True),
        jnp.sum(grad, axis=0, keepdims=True),
    )


def rotary_tables(spots):
    inverse = 10000.0 ** (-jnp.arange(8).astype(F32) / 8.0)
    angle = inverse[:, None] * spots.astype(F32)[None]
    waves = jnp.concatenate([jnp.cos(angle), jnp.sin(angle)], axis=0)
    lane = jnp.arange(2 * HEAD_DIM) % HEAD_DIM
    row = jnp.arange(16)[:, None]
    turn = row - 8
    picks = [
        (row < 8) & (lane < 16) & (lane % 8 == row),
        (lane < 8) & (lane == turn),
        (lane >= 8) & (lane < 16) & (lane - 8 == turn),
    ]
    signs = (1.0, -1.0, 1.0)
    chosen = jnp.concatenate([p.astype(F32) * g for p, g in zip(picks, signs)], axis=1)
    rest = jnp.concatenate([(lane >= 16).astype(F32), jnp.zeros(4 * HEAD_DIM, F32)])
    table = lax.dot_general(
        waves, chosen, (((0,), (0,)), ((), ())), precision=lax.Precision.HIGHEST
    )
    return table + rest


def turned(values, table, sign):
    wide = values.shape[1]
    many = wide // (2 * HEAD_DIM)
    keep, later, earlier = (
        jnp.concatenate([table[:, i * 128 : (i + 1) * 128]] * many, axis=1) for i in range(3)
    )
    partner = pltpu.roll(values, wide - 8, 1) * later + pltpu.roll(values, 8, 1) * earlier
    return values * keep + sign * partner


def dot_rows(left, right, kind=F32):
    return lax.dot_general(
        left, right, (((0,), (0,)), ((), ())), preferred_element_type=F32
    ).astype(kind)


def dot_cols(left, right, kind=F32):
    return lax.dot_general(
        left, right, (((1,), (1,)), ((), ())), preferred_element_type=F32
    ).astype(kind)


def dot(left, right):
    return jnp.dot(left, right, preferred_element_type=F32)


class Places:
    def __init__(self):
        self.fsdp = lax.axis_size("fsdp")
        self.seq = lax.axis_size("seq")
        self.count = self.fsdp * self.seq
        self.outer = self.fsdp // 4
        spot = lax.axis_index("fsdp")
        side = lax.axis_index("seq")
        self.a = spot // 4
        self.b = (spot // 2) % 2
        self.e = spot % 2
        self.x = side // 2
        self.c = side % 2
        self.last = None
        high, low = 2 * self.seq, self.seq
        self.groups = [
            [(a * 4 + e) * low + b * high + i for b in range(2) for i in range(low)]
            for a in range(self.outer)
            for e in range(2)
        ]
        self.sides = [group[c::2] for group in self.groups for c in range(2)]

    def after(self, values):
        if self.last is None:
            return values
        values, self.last = lax.optimization_barrier((values, self.last))
        return values

    def move(self, values, pairs):
        if values.ndim == 2 and values.shape[1] % 128 and values.shape[0] > 8:
            values = with_layout_constraint(values, Layout((0, 1)))
            return with_layout_constraint(lax.ppermute(values, AXES, pairs), Layout((0, 1)))
        return lax.ppermute(values, AXES, pairs)

    def flip(self, values, c=0, x=0, e=0, b=0):
        mask = c + 2 * x + self.seq * (e + 2 * b)
        return self.move(values, [(i, i ^ mask) for i in range(self.count)])

    def shift(self, values, steps):
        stride = 4 * self.seq * steps
        return self.move(values, [((i + stride) % self.count, i) for i in range(self.count)])

    def push(self, values, steps):
        stride = 4 * self.seq * steps
        return self.move(values, [(i, (i + stride) % self.count) for i in range(self.count)])

    def swap(self, values, groups):
        parts = len(groups[0])
        view = values.reshape(parts, values.shape[0] // parts, values.shape[1])
        view = lax.all_to_all(view, AXES, 0, 0, axis_index_groups=groups, tiled=True)
        return view.reshape(values.shape)


class Window:
    def close(self, at):
        values, tree = jax.tree.flatten(self.__dict__)
        self.__dict__.update(jax.tree.unflatten(tree, lax.optimization_barrier(values)))
        at.last = None


def pick(bit, first, second):
    return jnp.where(bit == 0, first, second)


def joined(bit, own, other, axis):
    return pick(
        bit, jnp.concatenate([own, other], axis=axis), jnp.concatenate([other, own], axis=axis)
    )


def order_kernel(width, spots_ref, ref, *outs):
    for i in range(ref.shape[1] // width):
        start = pl.multiple_of(spots_ref[i] * width, 128)
        block = ref[:, pl.ds(start, width)]
        for out in outs:
            for k in range(out.shape[0] // ref.shape[0]):
                rows = slice(k * ref.shape[0], (k + 1) * ref.shape[0])
                out[rows, i * width : (i + 1) * width] = block


def reorder(at, spots, values, copies):
    width = values.shape[1] // len(spots)
    if width % 128:
        cols = [lax.dynamic_slice_in_dim(values, spot * width, width, 1) for spot in spots]
        ordered = jnp.concatenate(cols, axis=1)
        return [jnp.concatenate([ordered] * n, axis=0) for n in copies]
    order = jnp.stack(spots).astype(jnp.int32)
    rows, wide = values.shape
    outs = [((n * rows, wide), values.dtype) for n in copies]
    return call(at, functools.partial(order_kernel, width), outs, order, values, name="order")


def to_relative(at, values, copies):
    spots = [
        (((at.a + i) % at.outer) * 2 + k) * 2 + (at.e ^ j)
        for i in range(at.outer)
        for j in range(2)
        for k in range(2)
    ]
    return reorder(at, spots, values, copies)


def to_absolute(at, values):
    spots = [
        (((i - at.a) % at.outer) * 2 + (at.e ^ j)) * 2 + k
        for i in range(at.outer)
        for k in range(2)
        for j in range(2)
    ]
    return reorder(at, spots, values, [1])[0]


def rows_of(shape, rows, index=lambda i: i):
    return pl.BlockSpec((rows, shape[1]), lambda i: (index(i), 0))


def call(at, kernel, outs, *args, steps=1, tiles=None, out_tiles=None, scratch=(), name=None):
    def spec(shape, kind, k, given):
        if given and k in given:
            return given[k]
        if kind == jnp.int32:
            return pl.BlockSpec(memory_space=pltpu.SMEM)
        zeros = (0,) * len(shape)
        return pl.BlockSpec(shape, lambda i: zeros, pipeline_mode=pl.Buffered(1))

    size = 0
    for shapes, given in (
        ([(v.shape, v.dtype) for v in args], tiles),
        (list(outs), out_tiles),
        ([(v.shape, v.dtype) for v in scratch], None),
    ):
        for k, (shape, kind) in enumerate(shapes):
            block = given[k].block_shape if given and k in given else shape
            size += math.prod(block) * jnp.dtype(kind).itemsize * (1 + (block is not shape))
    least = min(range(len(args)), key=lambda i: args[i].size)
    in_specs = [spec(v.shape, v.dtype, k, tiles) for k, v in enumerate(args)]
    args = list(args)
    args[least] = at.after(args[least])
    results = pl.pallas_call(
        kernel,
        grid=(steps,),
        out_shape=[jax.ShapeDtypeStruct(shape, kind) for shape, kind in outs],
        in_specs=in_specs,
        out_specs=[spec(shape, kind, k, out_tiles) for k, (shape, kind) in enumerate(outs)],
        scratch_shapes=list(scratch),
        compiler_params=pltpu.CompilerParams(
            vmem_limit_bytes=min(size * 9 // 8 + 12 * 2**20, 60 * 2**20)
        ),
        cost_estimate=pl.CostEstimate(flops=0, bytes_accessed=0, transcendentals=0),
        name=name,
    )(*args)
    at.last = min(results, key=lambda v: v.size)
    return results


TILE = 256


def product(values, chunks):
    outs = []
    for blocks in chunks:
        depth = blocks[0].shape[0]
        total = dot(values[:, :depth], blocks[0][...])
        for i, block in enumerate(blocks[1:], 1):
            total = total + dot(values[:, i * depth : (i + 1) * depth], block[...])
        outs.append(total)
    return outs[0] if len(outs) == 1 else jnp.concatenate(outs, axis=1)


def in_chunks(refs, count):
    return [refs[i : i + count] for i in range(0, len(refs), count)]


def transposed_product(values, chunks, j):
    total, col = None, 0
    for blocks in chunks:
        width = blocks[j].shape[1]
        term = dot_cols(values[:, col : col + width], blocks[j][...])
        total = term if total is None else total + term
        col += width
    return total


def tile_of(i):
    return pl.ds(pl.multiple_of(i * TILE, TILE), TILE)


def near_far(near, far):
    half = near.shape[0] // TILE
    return {
        0: rows_of(near.shape, TILE, lambda i: jnp.minimum(i, half - 1)),
        1: rows_of(far.shape, TILE, lambda i: jnp.maximum(i - half, 0)),
    }


def tile_from(near, far):
    first = pl.program_id(0) < pl.num_programs(0) // 2
    return jnp.where(first, near[...], far[...])


def qkv_kernel(count, near, far, *refs):
    gain, shift, bias, table, normed, mixed = refs[-6:]
    centered, scale = centered_of(tile_from(near, far).astype(F32))
    normed[...] = (centered * scale * gain[...] + shift[...]).astype(BF16)
    turning = mixed.shape[1] * 2 // 3
    values = product(normed, in_chunks(refs[:-6], count)) + bias[...]
    mixed[:, :turning] = turned(values[:, :turning], table[...], 1.0).astype(BF16)
    mixed[:, turning:] = values[:, turning:].astype(BF16)


def attended_grad_kernel(count, near, far, *refs):
    whole, grads = refs[-2:]
    whole[...] = tile_from(near, far)
    grads[...] = product(whole, in_chunks(refs[:-2], count)).astype(BF16)


def head_of(ref, group, head, start):
    part = ref.shape[1] // 3
    low = group * part + head * HEAD_DIM
    return ref[pl.ds(pl.multiple_of(start, TILE), TILE), low : low + HEAD_DIM]


def both_halves(ref, group, head, start, half):
    return jnp.concatenate(
        [head_of(ref, group, head, start), head_of(ref, group, head, start + half)], axis=0
    )


def allowed_at(row, col, sequence, turn):
    spot = pl.ds(pl.multiple_of(turn * TILE, TILE), TILE)
    ours = jnp.where(sequence == 0, row[0:1, spot], row[1:2, spot])
    theirs = jnp.where(sequence == 0, col[:, 0:1], col[:, 1:2])
    return (theirs == ours) & (col[:, 2:3] <= row[2:3, spot])


def scores_of(key, query, allowed):
    return jnp.where(allowed, dot_cols(key, query) * 0.125, -1e30)


def attend_kernel(mixed, row, col, attended, sums):
    half = mixed.shape[0] // 2
    heads = attended.shape[1] // HEAD_DIM

    @pl.loop(0, 4)
    def _(i):
        sequence, turn = i // 2, i % 2
        allowed = allowed_at(row, col, sequence, turn)
        start = turn * half + sequence * TILE
        span = pl.ds(pl.multiple_of(start, TILE), TILE)
        for h in range(heads):
            key = both_halves(mixed, 1, h, sequence * TILE, half)
            value = both_halves(mixed, 2, h, sequence * TILE, half)
            scores = scores_of(key, head_of(mixed, 0, h, start), allowed)
            top = jnp.max(scores, axis=0, keepdims=True)
            expo = jnp.exp(scores - top)
            total = jnp.sum(expo, axis=0, keepdims=True)
            probs = (expo * (1.0 / total)).astype(BF16)
            out = jnp.transpose(dot_rows(value, probs))
            attended[span, h * HEAD_DIM : (h + 1) * HEAD_DIM] = out.astype(BF16)
            sums[pl.ds(i * heads + h, 1), :] = top + jnp.log(total)


def attend_back_kernel(
    grads, mixed, sums, table, row, col, low, bias, query_sum, key_sum, value_sum
):
    half = mixed.shape[0] // 2
    part = grads.shape[1]
    heads = part // HEAD_DIM

    for sequence in range(2):
        for turn in range(2):
            i = sequence * 2 + turn
            allowed = allowed_at(row, col, sequence, turn)
            start = turn * half + sequence * TILE
            span = pl.ds(start, TILE)
            for h in range(heads):
                cols = slice(h * HEAD_DIM, (h + 1) * HEAD_DIM)
                query = head_of(mixed, 0, h, start)
                key = both_halves(mixed, 1, h, sequence * TILE, half)
                value = both_halves(mixed, 2, h, sequence * TILE, half)
                grad = grads[span, cols]
                scores = scores_of(key, query, allowed)
                probs = jnp.exp(scores - sums[i * heads + h : i * heads + h + 1, :])
                probs_grad = dot_cols(value, grad)
                value_grad = dot(probs.astype(BF16), grad)
                center = jnp.sum(probs * probs_grad, axis=0, keepdims=True)
                scores_low = (probs * (probs_grad - center)).astype(BF16)
                key_grad = dot(scores_low, query)
                query_sum[span, cols] = jnp.transpose(dot_rows(key, scores_low))
                for k in range(2):
                    keys = pl.ds(k * half + sequence * TILE, TILE)
                    rows = slice(k * TILE, (k + 1) * TILE)
                    if turn == 0:
                        key_sum[keys, cols] = key_grad[rows]
                        value_sum[keys, cols] = value_grad[rows]
                    else:
                        key_sum[keys, cols] += key_grad[rows]
                        value_sum[keys, cols] += value_grad[rows]

    bias[...] = jnp.zeros_like(bias)

    @pl.loop(0, mixed.shape[0] // TILE)
    def _(i):
        span = tile_of(i)
        factors = table[span, :]
        for k, ref in enumerate((query_sum, key_sum, value_sum)):
            values = ref[span, :]
            if k < 2:
                values = turned(values * 0.125, factors, -1.0)
            values = values.astype(BF16)
            low[span, k * part : (k + 1) * part] = values
            bias[:, k * part : (k + 1) * part] += jnp.sum(
                values.astype(F32), axis=0, keepdims=True
            )


def expand_kernel(count, values, *refs):
    *blocks, out = refs
    chunks = in_chunks(blocks, count)
    width = blocks[0].shape[0]
    for j in range(count):
        total = transposed_product(values, chunks, j)
        out[:, j * width : (j + 1) * width] = total.astype(out.dtype)


def total_of(terms):
    rows = terms.shape[0] // 4
    total = terms[:rows, :].astype(F32)
    for i in range(1, 4):
        total = total + terms[i * rows : (i + 1) * rows, :].astype(F32)
    return total


def four(out, values):
    rows = values.shape[0]
    for i in range(4):
        out[i * rows : (i + 1) * rows, :] = values


def hidden_kernel(inputs, gain, shift, terms, hidden, normed):
    values = inputs[...].astype(F32) + total_of(terms)
    hidden[...] = values
    centered, scale = centered_of(values)
    four(normed, (centered * scale * gain[...] + shift[...]).astype(BF16))


def result_kernel(hidden, terms, out):
    out[...] = (hidden[...] + total_of(terms)).astype(BF16)


def branch_kernel(hidden, cotangent, gain, terms, grad, low, gain_grad, shift_grad):
    pulled, gain_grad[...], shift_grad[...] = norm_back(hidden[...], gain[...], total_of(terms))
    values = cotangent[...].astype(F32) + pulled
    grad[...] = values
    four(low, values.astype(BF16))


def input_kernel(inputs, hidden_grad, gain, terms, grad, gain_grad, shift_grad):
    pulled, gain_grad[...], shift_grad[...] = norm_back(
        inputs[...].astype(F32), gain[...], total_of(terms)
    )
    grad[...] = hidden_grad[...] + pulled


def mlp_kernel(count, near, far, *refs):
    *blocks, normed, inner, gate_factor, up_factor = refs
    units = inner.shape[1]
    normed[...] = tile_from(near, far)
    values = product(normed, in_chunks(blocks, count))
    gate, up = values[:, :units], values[:, units:]
    sigmoid = 1.0 / (1.0 + jnp.exp(-gate))
    silu = gate * sigmoid
    inner[...] = (silu * up).astype(BF16)
    gate_factor[...] = up * sigmoid * (1.0 + gate * (1.0 - sigmoid))
    up_factor[...] = silu


def mlp_back_kernel(count, grads, *refs):
    *blocks, gate_factor, up_factor, pair = refs
    values = product(grads, in_chunks(blocks, count))
    pair[...] = jnp.concatenate(
        [(values * gate_factor[...]).astype(BF16), (values * up_factor[...]).astype(BF16)],
        axis=1,
    )


def segments(widths, chunks):
    out = []
    at_part = at_chunk = part = chunk = 0
    while part < len(widths):
        size = min(widths[part] - at_part, chunks[chunk] - at_chunk)
        out.append((part, at_part, chunk, at_chunk, size))
        at_part, at_chunk = at_part + size, at_chunk + size
        if at_part == widths[part]:
            part, at_part = part + 1, 0
        if at_chunk == chunks[chunk]:
            chunk, at_chunk = chunk + 1, 0
    return out


def part_list(refs, counts):
    return [
        (ref, p, ref.shape[1] // (8 * count)) for ref, count in zip(refs, counts) for p in range(count)
    ]


def cut_kernel(counts, *refs):
    weights, outs = refs[: len(counts)], refs[len(counts) :]
    rows = weights[0].shape[0]
    parts = part_list(weights, counts)
    cuts = segments([width for _, _, width in parts], [out.shape[1] for out in outs])
    for part, begin, chunk, col, size in cuts:
        ref, p, width = parts[part]
        for j in range(8):
            start = (p * 8 + j) * width + begin
            outs[chunk][j * rows : (j + 1) * rows, col : col + size] = ref[:, start : start + size]


def spread_kernel(counts, *refs):
    chunks, outs = refs[: -len(counts)], refs[-len(counts) :]
    rows = outs[0].shape[0]
    parts = part_list(outs, counts)
    cuts = segments([width for _, _, width in parts], [chunk.shape[1] for chunk in chunks])
    for part, begin, chunk, col, size in cuts:
        ref, p, width = parts[part]
        for j in range(8):
            start = (p * 8 + j) * width + begin
            piece = chunks[chunk][j * rows : (j + 1) * rows, col : col + size]
            ref[:, start : start + size] = piece.astype(F32)


def sum_kernel(*refs):
    *terms, out = refs
    total = terms[0][...].astype(F32)
    for term in terms[1:]:
        total = total + term[...].astype(F32)
    out[...] = total.astype(BF16)


def cut_rows(at, weights, counts, chunks):
    rows = weights[0].shape[0]
    return call(
        at,
        functools.partial(cut_kernel, counts),
        [((8 * rows, n), BF16) for n in chunks],
        *weights,
        name="cut",
    )


def split_kernel(whole, *outs):
    col = 0
    for out in outs:
        out[...] = whole[:, col : col + out.shape[1]]
        col += out.shape[1]


def cross_block(at, block):
    return [block] + [at.shift(block, i) for i in range(1, at.outer)]


def merge_blocks(across, beside):
    return [block for pair in zip(across, beside) for block in pair]


def send_block(at, block):
    return [block] + [at.shift(block, i) for i in range(1, at.outer)]


def grad_kernel(count, begin, values, grads, *refs):
    addends, outs = refs[:count], refs[count:]
    each = pl.num_programs(0) // len(outs)
    for k, out in enumerate(outs):

        @pl.when(pl.program_id(0) // each == k)
        def _():
            total = dot_rows(values[...], grads[:, begin : begin + out.shape[1]])
            if k < count:
                total = total + addends[k][...].astype(F32)
            out[...] = total.astype(out.dtype)


def grad_blocks(at, way, spots, kind, addends=()):
    values, grads, begin, size = way
    tokens, wide = values.shape
    width = wide // (2 * at.outer)
    tile = min(TILE, width)
    each = width // tile

    def column(i):
        spot = spots[0]
        for k in range(1, len(spots)):
            spot = jnp.where(i // each == k, spots[k], spot)
        return spot * each + i % each

    def row_of(k):
        return lambda i: jnp.clip(i - k * each, 0, each - 1)

    shape = (width, size)
    tiles = {0: pl.BlockSpec((tokens, tile), lambda i: (0, column(i)))}
    for k in range(len(addends)):
        tiles[2 + k] = rows_of(shape, tile, row_of(k))
    return call(
        at,
        functools.partial(grad_kernel, len(addends), begin),
        [(shape, kind)] * len(spots),
        values,
        grads,
        *addends,
        steps=len(spots) * each,
        tiles=tiles,
        out_tiles={k: rows_of(shape, tile, row_of(k)) for k in range(len(spots))},
        name="grad",
    )


def grad_beside(at, way):
    order = list(range(1, at.outer)) + [0]
    return grad_blocks(at, way, [2 * i + 1 for i in order], BF16)


def grad_own(at, way):
    return grad_blocks(at, way, [0], F32)[0]


def grad_across(at, way, sent):
    if at.outer == 1:
        return []
    return grad_blocks(at, way, [2 * i for i in range(1, at.outer)], BF16, sent[: at.outer - 1])


def push_all(at, made):
    return [at.push(v, i) for i, v in enumerate(made, 1)]


def flip_all(at, made):
    return [at.flip(v, e=1) for v in made]


def grad_spread(at, chunks, counts, widths):
    rows = chunks[0].shape[0] // 8
    return call(
        at,
        functools.partial(spread_kernel, counts),
        [((rows, n), F32) for n in widths],
        *chunks,
        name="spread",
    )


def join_kernel(near, far, out):
    out[...] = tile_from(near, far)


def joined_rows(at, near, far):
    shape = (2 * near.shape[0], near.shape[1])
    (out,) = call(
        at,
        join_kernel,
        [(shape, BF16)],
        near,
        far,
        steps=shape[0] // TILE,
        tiles=near_far(near, far),
        out_tiles={0: rows_of(shape, TILE)},
        name="join",
    )
    return out


def expand(at, values, chunks, side, kind):
    half = values.shape[0] // 2
    blocks = [block for chunk in chunks for block in chunk]
    count = len(chunks[0])
    shape = (half, blocks[0].shape[0] * count)
    steps = half // TILE
    (out,) = call(
        at,
        functools.partial(expand_kernel, count),
        [(shape, kind)],
        values,
        *blocks,
        steps=steps,
        tiles={0: rows_of(values.shape, TILE, lambda i: i + side * steps)},
        out_tiles={0: rows_of(shape, TILE)},
        name="expand",
    )
    return out


def add(at, *terms):
    shape = terms[0].shape
    tile = min(TILE, shape[0])
    (total,) = call(
        at,
        sum_kernel,
        [(shape, BF16)],
        *terms,
        steps=shape[0] // tile,
        tiles={k: rows_of(shape, tile) for k in range(len(terms))},
        out_tiles={0: rows_of(shape, tile)},
        name="add",
    )
    return total


def fetch_small(at, values):
    block = values[None]
    block = joined(at.c, block, at.flip(block, c=1), 0)
    block = joined(at.x, block, at.flip(block, x=1), 0)
    block = joined(at.b, block, at.flip(block, b=1), 0)
    whole = jnp.stack([block] + [at.shift(block, i) for i in range(1, at.outer)])
    return jnp.stack([whole, at.flip(whole, e=1)], axis=1)


def deliver_small(at, values):
    whole = values[:, 0] + at.flip(values[:, 1], e=1)
    block = whole[0]
    for i in range(1, at.outer):
        block = block + at.push(whole[i], i)
    for bit, name in ((at.b, "b"), (at.x, "x"), (at.c, "c")):
        rows = block.shape[0] // 2
        low, high = block[:rows], block[rows:]
        block = pick(bit, low, high) + at.flip(pick(bit, high, low), **{name: 1})
    return block[0]


def order_tokens(at, values):
    seqs, length = values.shape
    view = values.reshape(seqs, 2, 2, length // 4)
    view = pick(at.c, view, view[:, :, ::-1])
    return jnp.swapaxes(view, 1, 2).reshape(seqs, length)


def body(
    layer_input,
    segment_ids,
    positions,
    ln1_gain,
    ln1_bias,
    qkv_weight,
    qkv_bias,
    out_weight,
    ln2_gain,
    ln2_bias,
    gate_weight,
    up_weight,
    down_weight,
    cotangent,
):
    at = Places()
    width = layer_input.shape[1]
    rows = qkv_weight.shape[0]
    bias_rows = qkv_bias.shape[0]
    length = segment_ids.shape[1]
    heads_here = HEADS // 8
    part = width // 8
    units = gate_weight.shape[1] // 8
    slot = at.b * 4 + at.x * 2 + at.c

    tokens = 2 * length
    count = 2 * at.outer
    near = layer_input.shape[0]

    first = 2 * units // 256 * 128
    second = 2 * units - first
    v = Window()
    thin, wide = (tokens, units), (tokens, 2 * units)

    (cut_now,) = cut_rows(at, [qkv_weight, out_weight], (3, 1), (4 * part,))
    v.front = at.swap(cut_now, at.groups)
    v.inputs, v.inputs_four = to_relative(at, layer_input, [1, 4])
    v.first_cut, v.second_cut = cut_rows(at, [gate_weight, up_weight], (1, 1), (first, second))
    (v.down_cut,) = cut_rows(at, [down_weight], (1,), (units,))
    v.cotangent, v.cotangent_four = to_relative(at, cotangent, [1, 4])
    v.small = jnp.concatenate([qkv_bias, ln1_gain, ln1_bias, ln2_gain, ln2_bias])
    spots = jnp.concatenate([segment_ids, positions[None]], axis=0)[None]
    v.spots = joined(at.b, spots, at.flip(spots, b=1), 0)
    v.close(at)

    v.qkv, v.out = call(
        at,
        split_kernel,
        [((8 * rows, 3 * part), BF16), ((8 * rows, part), BF16)],
        v.front,
        name="split",
    )
    del v.front
    v.qkv_across = cross_block(at, v.qkv)
    v.qkv_beside = [at.flip(v.qkv, e=1)]
    v.near = at.swap(v.inputs_four, at.sides)
    v.first = at.swap(v.first_cut, at.groups)
    v.small = fetch_small(at, v.small)
    segments_here = order_tokens(at, v.spots[:, 0])
    places = order_tokens(at, v.spots[:, 1])
    index = order_tokens(at, jnp.arange(length)[None])
    v.row = jnp.concatenate([segments_here, index], axis=0).astype(F32)
    v.col = jnp.transpose(v.row)
    places = places.reshape(2, 2, length // 2).swapaxes(0, 1).reshape(2 * length)
    v.table = rotary_tables(places)
    v.close(at)

    v.qkv_beside += flip_all(at, v.qkv_across[1:])
    v.far = at.flip(v.near, c=1)
    v.out_across = cross_block(at, v.out)
    v.out_beside = [at.flip(v.out, e=1)]
    v.cotangent_near = at.swap(v.cotangent_four, at.sides)

    def vector(i):
        start = bias_rows + i * rows
        return v.small[..., start : start + rows].reshape(1, width).astype(F32)

    v.gains = [vector(i) for i in range(4)]
    bias = v.small[..., :bias_rows]
    bias = pick(at.e, bias, bias[:, ::-1])
    bias = jnp.roll(bias, at.a, axis=0)
    bias = bias.reshape(at.outer, 2, 2, 4, bias_rows).swapaxes(1, 2).reshape(3, 8, part)
    bias = lax.dynamic_index_in_dim(bias, slot, 1, keepdims=False)
    v.bias = bias.reshape(1, 3 * part).astype(F32)
    v.close(at)
    v.qkv_blocks = [merge_blocks(v.qkv_across, v.qkv_beside)]
    del v.qkv_across, v.qkv_beside, v.qkv, v.small, v.spots, v.inputs_four, v.cotangent_four, v.first_cut

    v.first_across = cross_block(at, v.first)
    v.first_beside = [at.flip(v.first, e=1)]
    v.out_beside += flip_all(at, v.out_across[1:])
    v.cotangent_far = at.flip(v.cotangent_near, c=1)
    v.second = at.swap(v.second_cut, at.groups)
    v.down = at.swap(v.down_cut, at.groups)
    v.normed, v.mixed = call(
        at,
        functools.partial(qkv_kernel, count),
        [((tokens, width), BF16), ((tokens, 3 * part), BF16)],
        v.near,
        v.far,
        *v.qkv_blocks[0],
        v.gains[0],
        v.gains[1],
        v.bias,
        v.table,
        steps=tokens // TILE,
        tiles=near_far(v.near, v.far) | {5 + count: rows_of(v.table.shape, TILE)},
        out_tiles={0: rows_of((tokens, width), TILE), 1: rows_of((tokens, 3 * part), TILE)},
        name="qkv",
    )
    v.attended, v.sums = call(
        at,
        attend_kernel,
        [((tokens, part), BF16), ((4 * heads_here, TILE), F32)],
        v.mixed,
        v.row,
        v.col,
        name="attend",
    )
    v.out_blocks = [merge_blocks(v.out_across, v.out_beside)]
    v.other = expand(at, v.attended, v.out_blocks, 1, BF16)
    v.own = expand(at, v.attended, v.out_blocks, 0, F32)
    v.close(at)
    del v.out_across, v.out_beside, v.out, v.second_cut, v.down_cut

    v.other = at.flip(v.other, c=1)
    v.cotangent_all = joined_rows(at, v.cotangent_near, v.cotangent_far)
    v.close(at)
    del v.cotangent_near, v.cotangent_far

    v.terms = at.swap(add(at, v.own, v.other), at.sides)
    v.second_across = cross_block(at, v.second)
    v.second_beside = [at.flip(v.second, e=1)]
    v.first_beside += flip_all(at, v.first_across[1:])
    v.close(at)
    del v.own, v.other

    v.hidden, normed2_four = call(
        at,
        hidden_kernel,
        [((near, width), F32), ((4 * near, width), BF16)],
        v.inputs,
        v.gains[2],
        v.gains[3],
        v.terms,
        name="hidden",
    )
    v.near = at.swap(normed2_four, at.sides)
    v.down_across = cross_block(at, v.down)
    v.down_beside = [at.flip(v.down, e=1)]
    v.second_beside += flip_all(at, v.second_across[1:])
    v.close(at)
    v.pair_blocks = [
        merge_blocks(v.first_across, v.first_beside),
        merge_blocks(v.second_across, v.second_beside),
    ]
    del v.first_across, v.first_beside, v.second_across, v.second_beside, v.first, v.second

    v.far = at.flip(v.near, c=1)
    v.down_beside += flip_all(at, v.down_across[1:])
    v.normed2, v.inner, v.gate_factor, v.up_factor = call(
        at,
        functools.partial(mlp_kernel, count),
        [((tokens, width), BF16), (thin, BF16), (thin, F32), (thin, F32)],
        v.near,
        v.far,
        *v.pair_blocks[0],
        *v.pair_blocks[1],
        steps=tokens // TILE,
        tiles=near_far(v.near, v.far),
        out_tiles={0: rows_of((tokens, width), TILE)}
        | {k: rows_of(thin, TILE) for k in range(1, 4)},
        name="mlp",
    )
    v.down_made = grad_beside(at, (v.cotangent_all, v.inner, 0, units))
    v.close(at)
    v.down_blocks = [merge_blocks(v.down_across, v.down_beside)]
    del v.down_across, v.down_beside, v.down, v.near, v.far

    v.down_sent = flip_all(at, v.down_made[:-1])
    (v.pair_low,) = call(
        at,
        functools.partial(mlp_back_kernel, count),
        [(wide, BF16)],
        v.cotangent_all,
        *v.down_blocks[0],
        v.gate_factor,
        v.up_factor,
        steps=tokens // TILE,
        tiles={
            0: rows_of((tokens, width), TILE),
            1 + count: rows_of(thin, TILE),
            2 + count: rows_of(thin, TILE),
        },
        out_tiles={0: rows_of(wide, TILE)},
        name="mlp_back",
    )
    v.other = expand(at, v.pair_low, v.pair_blocks, 1, BF16)
    v.own = expand(at, v.pair_low, v.pair_blocks, 0, F32)
    v.down_own = grad_own(at, (v.cotangent_all, v.inner, 0, units))
    v.close(at)

    v.other = at.flip(v.other, c=1)
    v.down_cross = grad_across(at, (v.cotangent_all, v.inner, 0, units), v.down_sent)
    v.first_made = grad_beside(at, (v.normed2, v.pair_low, 0, first))
    v.close(at)

    v.terms = at.swap(add(at, v.own, v.other), at.sides)
    v.down_far = push_all(at, v.down_cross)
    v.down_sent += flip_all(at, v.down_made[-1:])
    v.first_sent = flip_all(at, v.first_made[:-1])
    v.second_made = grad_beside(at, (v.normed2, v.pair_low, first, second))
    v.first_own = grad_own(at, (v.normed2, v.pair_low, 0, first))
    v.second_own = grad_own(at, (v.normed2, v.pair_low, first, second))
    v.result_other = expand(at, v.inner, v.down_blocks, 1, BF16)
    v.result_own = expand(at, v.inner, v.down_blocks, 0, F32)
    v.close(at)
    del v.down_cross, v.down_made, v.own, v.other

    v.hidden_grad, branch_four, v.gain_two_grad, v.shift_two_grad = call(
        at,
        branch_kernel,
        [((near, width), F32), ((4 * near, width), BF16)] + [((1, width), F32)] * 2,
        v.hidden,
        v.cotangent,
        v.gains[2],
        v.terms,
        name="branch",
    )
    v.near = at.swap(branch_four, at.sides)
    v.first_far = push_all(at, grad_across(at, (v.normed2, v.pair_low, 0, first), v.first_sent))
    v.first_sent += flip_all(at, v.first_made[-1:])
    v.second_sent = flip_all(at, v.second_made[:-1])
    v.result_other = at.flip(v.result_other, c=1)
    v.down_total = add(at, v.down_own, v.down_sent[-1], *v.down_far)
    v.close(at)
    del v.first_made, v.down_own, v.down_sent, v.down_far

    v.far = at.flip(v.near, c=1)
    v.second_far = push_all(
        at, grad_across(at, (v.normed2, v.pair_low, first, second), v.second_sent)
    )
    v.second_sent += flip_all(at, v.second_made[-1:])
    v.down_pieces = at.swap(v.down_total, at.groups)
    v.branch, v.attended_grad = call(
        at,
        functools.partial(attended_grad_kernel, count),
        [((tokens, width), BF16), ((tokens, part), BF16)],
        v.near,
        v.far,
        *v.out_blocks[0],
        steps=tokens // TILE,
        tiles=near_far(v.near, v.far),
        out_tiles={0: rows_of((tokens, width), TILE), 1: rows_of((tokens, part), TILE)},
        name="attended_grad",
    )
    v.mixed_low, v.bias_part = call(
        at,
        attend_back_kernel,
        [((tokens, 3 * part), BF16), ((1, 3 * part), F32)],
        v.attended_grad,
        v.mixed,
        v.sums,
        v.table,
        v.row,
        v.col,
        scratch=[pltpu.VMEM((tokens, part), F32)] * 3,
        name="attend_back",
    )
    v.qkv_made = grad_beside(at, (v.normed, v.mixed_low, 0, 3 * part))
    v.other = expand(at, v.mixed_low, v.qkv_blocks, 1, BF16)
    v.own = expand(at, v.mixed_low, v.qkv_blocks, 0, F32)
    v.out_made = grad_beside(at, (v.branch, v.attended, 0, part))
    v.first_total = add(at, v.first_own, v.first_sent[-1], *v.first_far)
    v.result_terms = add(at, v.result_own, v.result_other)
    v.close(at)
    del v.near, v.far, v.second_made, v.attended_grad, v.down_total, v.result_own, v.result_other
    del v.first_own, v.first_sent, v.first_far

    v.other = at.flip(v.other, c=1)
    v.qkv_sent = flip_all(at, v.qkv_made[:-1])
    v.out_sent = flip_all(at, v.out_made)
    v.result_terms = at.swap(v.result_terms, at.sides)
    v.qkv_own = grad_own(at, (v.normed, v.mixed_low, 0, 3 * part))
    v.out_own = grad_own(at, (v.branch, v.attended, 0, part))
    v.second_total = add(at, v.second_own, v.second_sent[-1], *v.second_far)
    (v.down_grad,) = grad_spread(at, [v.down_pieces], (1,), (8 * units,))
    v.close(at)
    del v.second_own, v.second_sent, v.second_far, v.down_pieces

    v.qkv_far = push_all(at, grad_across(at, (v.normed, v.mixed_low, 0, 3 * part), v.qkv_sent))
    v.terms = at.swap(add(at, v.own, v.other), at.sides)
    v.qkv_sent += flip_all(at, v.qkv_made[-1:])
    v.first_pieces = at.swap(v.first_total, at.groups)
    v.out_cross = grad_across(at, (v.branch, v.attended, 0, part), v.out_sent)
    (v.result,) = call(
        at, result_kernel, [((near, width), BF16)], v.hidden, v.result_terms, name="result"
    )
    v.result = to_absolute(at, v.result)
    v.close(at)

    v.qkv_pieces = at.swap(add(at, v.qkv_own, v.qkv_sent[-1], *v.qkv_far), at.groups)
    v.out_far = push_all(at, v.out_cross)
    v.second_pieces = at.swap(v.second_total, at.groups)
    v.input_grad, v.gain_one_grad, v.shift_one_grad = call(
        at,
        input_kernel,
        [((near, width), F32)] + [((1, width), F32)] * 2,
        v.inputs,
        v.hidden_grad,
        v.gains[0],
        v.terms,
        name="inputs",
    )
    v.close(at)
    v.out_pieces = at.swap(add(at, v.out_own, v.out_sent[-1], *v.out_far), at.groups)
    input_grad = to_absolute(at, v.input_grad)
    gate_wgrad, up_wgrad = grad_spread(
        at, [v.first_pieces, v.second_pieces], (1, 1), (8 * units,) * 2
    )
    (qkv_wgrad,) = grad_spread(at, [v.qkv_pieces], (3,), (24 * part,))
    (out_wgrad,) = grad_spread(at, [v.out_pieces], (1,), (8 * part,))
    result, down_grad, bias_part = v.result, v.down_grad, v.bias_part
    gain_one_grad, shift_one_grad = v.gain_one_grad, v.shift_one_grad
    gain_two_grad, shift_two_grad = v.gain_two_grad, v.shift_two_grad

    bias_part = bias_part.reshape(3, 1, part)
    own_slot = (jnp.arange(8) == slot).astype(F32)[None, :, None]
    bias_whole = (bias_part * own_slot).reshape(at.outer, 2, 2, 4, bias_rows).swapaxes(1, 2)
    bias_whole = jnp.roll(bias_whole, -at.a, axis=0)
    bias_whole = pick(at.e, bias_whole, bias_whole[:, ::-1]).reshape(at.outer, 2, 8, bias_rows)
    grads = [
        v.reshape(at.outer, 2, 8, rows)
        for v in (gain_one_grad, shift_one_grad, gain_two_grad, shift_two_grad)
    ]
    shares = deliver_small(at, jnp.concatenate([bias_whole] + grads, axis=-1))

    def share(i):
        return shares[bias_rows + i * rows : bias_rows + (i + 1) * rows]

    return (
        result,
        input_grad,
        share(0),
        share(1),
        qkv_wgrad,
        shares[:bias_rows],
        out_wgrad,
        share(2),
        share(3),
        gate_wgrad,
        up_wgrad,
        down_grad,
    )


def solution(mesh):
    both = ("fsdp", "seq")
    wide = P(both, None)
    flat = P(both)
    return jax.shard_map(
        body,
        mesh=mesh,
        in_specs=(
            wide, P("fsdp", None), P("fsdp"), flat, flat, wide, flat,
            wide, flat, flat, wide, wide, wide, wide,
        ),
        out_specs=(wide, wide, flat, flat, wide, flat, wide, flat, flat, wide, wide, wide),
        check_vma=False,
    )
```

time: 955 us -> 720 us (0.75)
  matrix products: 151 us -> 1.45 us
  waiting for transfers between devices: 414 us -> 272 us
  Pallas kernels: 0 us -> 141 us
  other arithmetic: 129 us -> 9.26 us
  starting transfers between devices: 87.2 us -> 140 us
  local copies, waits for them, and re-layouts: 160 us -> 141 us
    ppermute x103 -> x49, waiting for transfers between devices: 414 us -> 230 us  [the longest x43 171 us: move(): return lax.ppermute(values, AXES, pairs)]
    dot_general x69 -> x1, matrix products: 143 us -> 1.45 us  [rotary_tables(): lax.dot_general(waves, chosen, (((0,), (0,)), ((), ())), precision=lax.Pr...]
    pallas_call x0 -> x55, Pallas kernels: none -> 141 us  [call(): pl.pallas_call(kernel, grid=(steps,), out_shape=[jax.ShapeDtypeStruct(sha...]
    all_to_all x0 -> x17, starting transfers between devices: none -> 76.8 us  [swap(): lax.all_to_all(view, AXES, 0, 0, axis_index_groups=groups, tiled=True)]
    select_n x74 -> x11, other arithmetic: 45.1 us -> 0.11 us  [pick(): return jnp.where(bit == 0, first, second)]
    all_to_all x0 -> x17, waiting for transfers between devices: none -> 41.5 us  [swap(): lax.all_to_all(view, AXES, 0, 0, axis_index_groups=groups, tiled=True)]
    ppermute x103 -> x49, starting transfers between devices: 87.2 us -> 63.6 us  [the longest x43 57 us: move(): return lax.ppermute(values, AXES, pairs)]
    convert_element_type x23 -> x5, other arithmetic: 24.1 us -> 1.99 us  [the longest x1 1.76 us: body(): v.row = jnp.concatenate([segments_here, index], axis=0).astype(F32)]
  transfers between devices with their start and end apart: 103 -> 66, of which waited for: 46 -> 32; matrix products, arithmetic and copies ran while one was open for 43% -> 3% of each run, Pallas kernels for 0% -> 17%
where the time goes in v3:
time: 720 us; the launch traced here: 708 us
  waiting for transfers between devices  272 us (38%)
  local copies, waits for them, and re-layouts  141 us (20%)
  Pallas kernels  141 us (20%)
  starting transfers between devices  140 us (19%)
  other arithmetic  9.26 us (1%)
    ppermute x43, waiting for transfers between devices, move(): return lax.ppermute(values, AXES, pairs)  171 us
    pallas_call x55, Pallas kernels, call(): pl.pallas_call(kernel, grid=(steps,), out_shape=[jax.ShapeDtypeStruct(sha...  141 us
    unnamed x326, local copies, waits for them, and re-layouts  116 us
    all_to_all x17, starting transfers between devices, swap(): lax.all_to_all(view, AXES, 0, 0, axis_index_groups=groups, tiled=True)  76.8 us
    ppermute x6, waiting for transfers between devices, move(): lax.ppermute(values, AXES, pairs)  59 us
    ppermute x43, starting transfers between devices, move(): return lax.ppermute(values, AXES, pairs)  57 us
    all_to_all x17, waiting for transfers between devices, swap(): lax.all_to_all(view, AXES, 0, 0, axis_index_groups=groups, tiled=True)  41.5 us
  transfers between devices with their start and end apart: 66, of which 32 were waited for; matrix products, arithmetic and copies ran while one was open for 3% of the time, Pallas kernels for 17%

profile of v3, /device:TPU:0, one launch (start us, length us, event | category | flops | bytes accessed | tf_op | source)
XLA Modules:
  0.0 707.9 jit_solution(14350616567359761169)
XLA Ops:
  27.3 10.1 %all-to-all-done.1 = bf16[8,64,640]{2,1,0:T(8,128)(2,1)S(1)} async-done(((bf16[8,64,640]{2,1,0:T(8,128)(2,1)}), bf16[8,64,640]{2,1,0:T(8,128)(2,1)S(1)}, u32[]{:S(2)}, u32[]{:S(2)}) %all-to-all-start.1) | async-done | bytes 655392 | tf_op jit(solution)/shard_map/all_to_all | solution.py:134
  51.2 7.1 collective-permute-done.4
  58.3 10.1 %collective-permute-start.5 = (bf16[4,448]{1,0:T(4,128)(2,1)S(1)}, bf16[4,448]{1,0:T(4,128)(2,1)S(1)}, u32[]{:S(2)}, u32[]{:S(2)}) collective-permute-start(bf16[4,448]{1,0:T(4,128)(2,1)S(1)} %maximum_select_fusion.2), channel_id=1, source_target_pairs={{0,8},{1,9},{2,10},{3,11},{4,12},{5,13},{6,14},{7,15},{8,0},{9,1},... | collective-permute-start | bytes 10760 | tf_op jit(solution)/shard_map/ppermute | solution.py:117
  69.3 14.5 %collective-permute-done.5 = bf16[4,448]{1,0:T(4,128)(2,1)S(1)} collective-permute-done((bf16[4,448]{1,0:T(4,128)(2,1)S(1)}, bf16[4,448]{1,0:T(4,128)(2,1)S(1)}, u32[]{:S(2)}, u32[]{:S(2)}) %collective-permute-start.5) | collective-permute-done | bytes 3616 | tf_op jit(solution)/shard_map/ppermute | solution.py:117
  102.0 20.5 %collective-permute-done.10.refs_1_ = bf16[512,256]{1,0:T(8,128)(2,1)S(1)} collective-permute-done((bf16[512,256]{1,0:T(8,128)(2,1)S(1)}, bf16[512,256]{1,0:T(8,128)(2,1)S(1)}, u32[]{:S(2)}, u32[]{:S(2)}) %collective-permute-start.10) | collective-permute-done | bytes 262176 | tf_op jit(solution)/shard_map/ppermute | solution.py:117
  130.7 11.1 %all-to-all-done.4 = bf16[8,64,704]{2,1,0:T(8,128)(2,1)S(1)} async-done(((bf16[8,64,704]{2,1,0:T(8,128)(2,1)}), bf16[8,64,704]{2,1,0:T(8,128)(2,1)S(1)}, u32[]{:S(2)}, u32[]{:S(2)}) %all-to-all-start.4) | async-done | bytes 720928 | tf_op jit(solution)/shard_map/all_to_all | solution.py:134
  150.4 9.2 %qkv.1 = (bf16[1024,2048]{1,0:T(8,128)(2,1)S(1)}, bf16[1024,768]{1,0:T(8,128)(2,1)S(1)}) custom-call(bf16[512,2048]{1,0:T(8,128)(2,1)} %bitcast.20.near, bf16[512,2048]{1,0:T(8,128)(2,1)} %collective-permute-done.8.far, bf16[512,768]{1,0:T(8,128)(2,1)S(1)} %copy-done.56, bf16[512,768]{1,0:T(8,128)(2,1)} %collective-permute-done.2.refs_1_, ...), custom_call_target="tpu_custom_call" | custom-call | tf_op jit(solution)/shard_map/qkv/pallas_call | solution.py:223
  166.2 9.2 %attend.1 = (bf16[1024,256]{1,0:T(8,128)(2,1)S(1)}, f32[16,256]{1,0:T(8,128)S(1)}) custom-call(bf16[1024,768]{1,0:T(8,128)(2,1)S(1)} %copy-done.66, f32[3,512]{1,0:T(4,128)S(1)} %copy.102.row, f32[512,3]{1,0:T(8,128)S(1)} %copy-done.96), custom_call_target="tpu_custom_call" | custom-call | tf_op jit(solution)/shard_map/attend/pallas_call | solution.py:223
  200.1 29.8 %collective-permute-done.17.refs_3_ = bf16[512,640]{1,0:T(8,128)(2,1)S(1)} collective-permute-done((bf16[512,640]{1,0:T(8,128)(2,1)}, bf16[512,640]{1,0:T(8,128)(2,1)S(1)}, u32[]{:S(2)}, u32[]{:S(2)}) %collective-permute-start.17) | collective-permute-done | bytes 655392 | tf_op jit(solution)/shard_map/ppermute | solution.py:117
  229.9 6.4 collective-permute-done.18.refs_6_
  253.7 30.5 %collective-permute-done.21 = bf16[512,704]{0,1:T(8,128)(2,1)S(1)} collective-permute-done((bf16[512,704]{0,1:T(8,128)(2,1)}, bf16[512,704]{0,1:T(8,128)(2,1)S(1)}, u32[]{:S(2)}, u32[]{:S(2)}) %collective-permute-start.21) | collective-permute-done | bytes 720928 | tf_op jit(solution)/shard_map/ppermute | solution.py:116
  292.6 17.8 %collective-permute-done.23 = bf16[512,704]{0,1:T(8,128)(2,1)} collective-permute-done((bf16[512,704]{0,1:T(8,128)(2,1)}, bf16[512,704]{0,1:T(8,128)(2,1)}, u32[]{:S(2)}, u32[]{:S(2)}) %collective-permute-start.23) | collective-permute-done | bytes 720928 | tf_op jit(solution)/shard_map/ppermute | solution.py:116
  313.7 11.8 %mlp.1 = (bf16[1024,2048]{1,0:T(8,128)(2,1)S(1)}, bf16[1024,704]{1,0:T(8,128)(2,1)S(1)}, f32[1024,704]{1,0:T(8,128)S(1)}, f32[1024,704]{1,0:T(8,128)S(1)}) custom-call(bf16[512,2048]{1,0:T(8,128)(2,1)} %bitcast.41.near, bf16[512,2048]{1,0:T(8,128)(2,1)} %collective-permute-done.24.far, bf16[512,640]{1,0:T(8,128)(2,1)S(1)} %bitcast.123, ...), custom_call_target="tpu_custom_call" | custom-call | tf_op jit(solution)/shard_map/mlp/pallas_call | solution.py:223
  349.9 5.5 expand.10
  356.7 5.6 expand.11.refs_0_
  415.1 8.4 %collective-permute-done.27 = bf16[512,704]{0,1:T(8,128)(2,1)} collective-permute-done((bf16[512,704]{0,1:T(8,128)(2,1)}, bf16[512,704]{0,1:T(8,128)(2,1)}, u32[]{:S(2)}, u32[]{:S(2)}) %collective-permute-start.27) | collective-permute-done | bytes 720928 | tf_op jit(solution)/shard_map/ppermute | solution.py:116
  434.7 6.0 all-to-all-start.9
  450.1 24.8 %collective-permute-done.31.refs_1_ = bf16[512,640]{1,0:T(8,128)(2,1)S(1)} collective-permute-done((bf16[512,640]{1,0:T(8,128)(2,1)}, bf16[512,640]{1,0:T(8,128)(2,1)S(1)}, u32[]{:S(2)}, u32[]{:S(2)}) %collective-permute-start.31) | collective-permute-done | bytes 655392 | tf_op jit(solution)/shard_map/ppermute | solution.py:117
  480.2 6.1 all-to-all-start.10
  505.1 9.8 %attend_back.1 = (bf16[1024,768]{1,0:T(8,128)(2,1)S(1)}, f32[1,768]{1,0:T(1,128)S(1)}) custom-call(bf16[1024,256]{1,0:T(8,128)(2,1)S(1)} %copy-done.137, bf16[1024,768]{1,0:T(8,128)(2,1)S(1)} %copy-done.67, f32[16,256]{1,0:T(8,128)S(1)} %get-tuple-element.877.sums, f32[1024,384]{1,0:T(8,128)S(1)} %copy-done.37, f32[3,512]{1,0:T(4,128)S(1)} %copy.115.row, ...), custom_call_target="tpu_custom_call" | custom-call | tf_op jit(solution)/shard_map/attend_back/pallas_call | solution.py:223
  556.1 11.6 %collective-permute-done.38.refs_0_ = bf16[512,256]{1,0:T(8,128)(2,1)S(1)} collective-permute-done((bf16[512,256]{1,0:T(8,128)(2,1)}, bf16[512,256]{1,0:T(8,128)(2,1)S(1)}, u32[]{:S(2)}, u32[]{:S(2)}) %collective-permute-start.38) | collective-permute-done | bytes 262176 | tf_op jit(solution)/shard_map/ppermute | solution.py:117
  604.3 30.1 %collective-permute-done.41.refs_2_ = bf16[512,768]{1,0:T(8,128)(2,1)} collective-permute-done((bf16[512,768]{1,0:T(8,128)(2,1)}, bf16[512,768]{1,0:T(8,128)(2,1)}, u32[]{:S(2)}, u32[]{:S(2)}) %collective-permute-start.41) | collective-permute-done | bytes 786464 | tf_op jit(solution)/shard_map/ppermute | solution.py:117
  642.4 9.3 %all-to-all-done.15 = bf16[8,64,768]{2,1,0:T(8,128)(2,1)S(1)} async-done(((bf16[8,64,768]{2,1,0:T(8,128)(2,1)}), bf16[8,64,768]{2,1,0:T(8,128)(2,1)S(1)}, u32[]{:S(2)}, u32[]{:S(2)}) %all-to-all-start.15) | async-done | bytes 786464 | tf_op jit(solution)/shard_map/all_to_all | solution.py:134
  663.2 7.3 %collective-permute-done.43.refs_2_ = bf16[512,256]{1,0:T(8,128)(2,1)} collective-permute-done((bf16[512,256]{1,0:T(8,128)(2,1)}, bf16[512,256]{1,0:T(8,128)(2,1)}, u32[]{:S(2)}, u32[]{:S(2)}) %collective-permute-start.43) | collective-permute-done | bytes 262176 | tf_op jit(solution)/shard_map/ppermute | solution.py:117
  (590 shorter events, 392.7 us)
Async XLA Ops:
  37.4 54.8 %all-to-all-start.2 = ((bf16[4,128,2048]{2,1,0:T(8,128)(2,1)}), bf16[4,128,2048]{2,1,0:T(8,128)(2,1)}, u32[]{:S(2)}, u32[]{:S(2)}) async-start(bf16[4,128,2048]{2,1,0:T(8,128)(2,1)} %bitcast.138), calls=%async_computation.2 | async-start | bytes 4194304 | tf_op jit(solution)/shard_map/all_to_all | solution.py:134
  42.2 50.0 %collective-permute-start.2 = (bf16[512,768]{1,0:T(8,128)(2,1)S(1)}, bf16[512,768]{1,0:T(8,128)(2,1)}, u32[]{:S(2)}, u32[]{:S(2)}) collective-permute-start(bf16[512,768]{1,0:T(8,128)(2,1)S(1)} %get-tuple-element.896.refs_0_), channel_id=1, source_target_pairs={{0,4},{1,5},{2,6},{3,7},{4,0},{5,1},{6,2},{7,3},{8,12},{9,13},{10,... | collective-permute-start | bytes 2359304 | tf_op jit(solution)/shard_map/ppermute | solution.py:117
  43.8 48.4 %collective-permute-start.1 = (bf16[512,768]{1,0:T(8,128)(2,1)S(1)}, bf16[512,768]{1,0:T(8,128)(2,1)}, u32[]{:S(2)}, u32[]{:S(2)}) collective-permute-start(bf16[512,768]{1,0:T(8,128)(2,1)S(1)} %get-tuple-element.896.refs_0_), channel_id=1, source_target_pairs={{16,0},{17,1},{18,2},{19,3},{20,4},{21,5},{22,6},{23,7},{24,8},{25... | collective-permute-start | bytes 2359304 | tf_op jit(solution)/shard_map/ppermute | solution.py:117
  130.1 53.6 %collective-permute-start.12 = (bf16[512,2048]{1,0:T(8,128)(2,1)}, bf16[512,2048]{1,0:T(8,128)(2,1)}, u32[]{:S(2)}, u32[]{:S(2)}) collective-permute-start(bf16[512,2048]{1,0:T(8,128)(2,1)} %bitcast.33.near), channel_id=1, source_target_pairs={{0,1},{1,0},{2,3},{3,2},{4,5},{5,4},{6,7},{7,6},{8,9},{9,8},{10,11... | collective-permute-start | bytes 6291464 | tf_op jit(solution)/shard_map/ppermute | solution.py:117
  141.8 41.9 %all-to-all-start.5 = ((bf16[8,64,768]{2,1,0:T(8,128)(2,1)}), bf16[8,64,768]{2,1,0:T(8,128)(2,1)S(1)}, u32[]{:S(2)}, u32[]{:S(2)}) async-start(bf16[8,64,768]{2,1,0:T(8,128)(2,1)} %bitcast.142), calls=%async_computation.5 | async-start | bytes 1572864 | tf_op jit(solution)/shard_map/all_to_all | solution.py:134
  145.4 38.4 %collective-permute-start.14 = (bf16[512,640]{1,0:T(8,128)(2,1)}, bf16[512,640]{1,0:T(8,128)(2,1)}, u32[]{:S(2)}, u32[]{:S(2)}) collective-permute-start(bf16[512,640]{1,0:T(8,128)(2,1)} %bitcast.121), channel_id=1, source_target_pairs={{0,4},{1,5},{2,6},{3,7},{4,0},{5,1},{6,2},{7,3},{8,12},{9,13},{10,... | collective-permute-start | bytes 1966088 | tf_op jit(solution)/shard_map/ppermute | solution.py:117
  146.5 37.2 %collective-permute-start.13 = (bf16[512,640]{1,0:T(8,128)(2,1)}, bf16[512,640]{1,0:T(8,128)(2,1)}, u32[]{:S(2)}, u32[]{:S(2)}) collective-permute-start(bf16[512,640]{1,0:T(8,128)(2,1)} %bitcast.122), channel_id=1, source_target_pairs={{16,0},{17,1},{18,2},{19,3},{20,4},{21,5},{22,6},{23,7},{24,8},{25... | collective-permute-start | bytes 1966088 | tf_op jit(solution)/shard_map/ppermute | solution.py:117
  191.3 47.2 %all-to-all-start.6 = ((bf16[4,128,2048]{2,1,0:T(8,128)(2,1)}), bf16[4,128,2048]{2,1,0:T(8,128)(2,1)}, u32[]{:S(2)}, u32[]{:S(2)}) async-start(bf16[4,128,2048]{2,1,0:T(8,128)(2,1)} %bitcast.129), calls=%async_computation.6 | async-start | bytes 4194304 | tf_op jit(solution)/shard_map/all_to_all | solution.py:134
  195.8 34.1 %collective-permute-start.19 = (bf16[512,768]{1,0:T(8,128)(2,1)S(1)}, bf16[512,768]{1,0:T(8,128)(2,1)S(1)}, u32[]{:S(2)}, u32[]{:S(2)}) collective-permute-start(bf16[512,768]{1,0:T(8,128)(2,1)S(1)} %bitcast.116), channel_id=1, source_target_pairs={{0,4},{1,5},{2,6},{3,7},{4,0},{5,1},{6,2},{7,3},{8,12},{9,13},{10,... | collective-permute-start | bytes 2359304 | tf_op jit(solution)/shard_map/ppermute | solution.py:117
  197.4 38.9 %collective-permute-start.18 = (bf16[512,768]{1,0:T(8,128)(2,1)S(1)}, bf16[512,768]{1,0:T(8,128)(2,1)}, u32[]{:S(2)}, u32[]{:S(2)}) collective-permute-start(bf16[512,768]{1,0:T(8,128)(2,1)S(1)} %bitcast.117), channel_id=1, source_target_pairs={{16,0},{17,1},{18,2},{19,3},{20,4},{21,5},{22,6},{23,7},{24,8},{25... | collective-permute-start | bytes 2359304 | tf_op jit(solution)/shard_map/ppermute | solution.py:117
  244.3 46.0 %all-to-all-start.7 = ((bf16[4,128,2048]{2,1,0:T(8,128)(2,1)}), bf16[4,128,2048]{2,1,0:T(8,128)(2,1)}, u32[]{:S(2)}, u32[]{:S(2)}) async-start(bf16[4,128,2048]{2,1,0:T(8,128)(2,1)} %bitcast.140), calls=%async_computation.7 | async-start | bytes 4194304 | tf_op jit(solution)/shard_map/all_to_all | solution.py:134
  249.2 39.8 %collective-permute-start.22 = (bf16[512,768]{1,0:T(8,128)(2,1)}, bf16[512,768]{1,0:T(8,128)(2,1)}, u32[]{:S(2)}, u32[]{:S(2)}) collective-permute-start(bf16[512,768]{1,0:T(8,128)(2,1)} %collective-permute-done.18.refs_6_), channel_id=1, source_target_pairs={{0,4},{1,5},{2,6},{3,7},{4,0},{5,1},{6,2},{7,3},{8,12},{9,13},{10,... | collective-permute-start | bytes 2359304 | tf_op jit(solution)/shard_map/ppermute | solution.py:117
  252.5 35.2 %collective-permute-start.20 = (bf16[512,704]{0,1:T(8,128)(2,1)}, bf16[512,704]{0,1:T(8,128)(2,1)}, u32[]{:S(2)}, u32[]{:S(2)}) collective-permute-start(bf16[512,704]{0,1:T(8,128)(2,1)} %copy.103), channel_id=1, source_target_pairs={{16,0},{17,1},{18,2},{19,3},{20,4},{21,5},{22,6},{23,7},{24,8},{25... | collective-permute-start | bytes 2162696 | tf_op jit(solution)/shard_map/ppermute | solution.py:116
  379.6 46.8 %all-to-all-start.8 = ((bf16[4,128,2048]{2,1,0:T(8,128)(2,1)}), bf16[4,128,2048]{2,1,0:T(8,128)(2,1)}, u32[]{:S(2)}, u32[]{:S(2)}) async-start(bf16[4,128,2048]{2,1,0:T(8,128)(2,1)} %bitcast.128), calls=%async_computation.8 | async-start | bytes 4194304 | tf_op jit(solution)/shard_map/all_to_all | solution.py:134
  434.7 45.6 %all-to-all-start.9 = ((bf16[4,128,2048]{2,1,0:T(8,128)(2,1)}), bf16[4,128,2048]{2,1,0:T(8,128)(2,1)}, u32[]{:S(2)}, u32[]{:S(2)}) async-start(bf16[4,128,2048]{2,1,0:T(8,128)(2,1)} %bitcast.139), calls=%async_computation.9 | async-start | bytes 4194304 | tf_op jit(solution)/shard_map/all_to_all | solution.py:134
  440.7 38.2 %collective-permute-start.32 = (bf16[512,2048]{1,0:T(8,128)(2,1)}, bf16[512,2048]{1,0:T(8,128)(2,1)S(1)}, u32[]{:S(2)}, u32[]{:S(2)}) collective-permute-start(bf16[512,2048]{1,0:T(8,128)(2,1)} %copy-done.106), channel_id=1, source_target_pairs={{0,1},{1,0},{2,3},{3,2},{4,5},{5,4},{6,7},{7,6},{8,9},{9,8},{10,11... | collective-permute-start | bytes 6291464 | tf_op jit(solution)/shard_map/ppermute | solution.py:117
  440.7 37.3 %collective-permute-start.33 = (bf16[512,768]{1,0:T(8,128)(2,1)}, bf16[512,768]{1,0:T(8,128)(2,1)S(1)}, u32[]{:S(2)}, u32[]{:S(2)}) collective-permute-start(bf16[512,768]{1,0:T(8,128)(2,1)} %copy-done.150), channel_id=1, source_target_pairs={{0,4},{1,5},{2,6},{3,7},{4,0},{5,1},{6,2},{7,3},{8,12},{9,13},{10,... | collective-permute-start | bytes 2359304 | tf_op jit(solution)/shard_map/ppermute | solution.py:117
  480.2 56.8 %all-to-all-start.10 = ((bf16[8,64,704]{2,1,0:T(8,128)(2,1)}), bf16[8,64,704]{2,1,0:T(8,128)(2,1)}, u32[]{:S(2)}, u32[]{:S(2)}) async-start(bf16[8,64,704]{2,1,0:T(8,128)(2,1)} %bitcast.134), calls=%async_computation.10 | async-start | bytes 1572864 | tf_op jit(solution)/shard_map/all_to_all | solution.py:134
  491.9 45.2 %collective-permute-start.35 = (bf16[512,768]{1,0:T(8,128)(2,1)}, bf16[512,768]{1,0:T(8,128)(2,1)}, u32[]{:S(2)}, u32[]{:S(2)}) collective-permute-start(bf16[512,768]{1,0:T(8,128)(2,1)} %grad.23), channel_id=1, source_target_pairs={{0,16},{1,17},{2,18},{3,19},{4,20},{5,21},{6,22},{7,23},{8,24},{9,... | collective-permute-start | bytes 2359304 | tf_op jit(solution)/shard_map/ppermute | solution.py:117
  493.7 43.4 %collective-permute-start.36 = (bf16[512,768]{1,0:T(8,128)(2,1)}, bf16[512,768]{1,0:T(8,128)(2,1)}, u32[]{:S(2)}, u32[]{:S(2)}) collective-permute-start(bf16[512,768]{1,0:T(8,128)(2,1)} %get-tuple-element.910), channel_id=1, source_target_pairs={{0,4},{1,5},{2,6},{3,7},{4,0},{5,1},{6,2},{7,3},{8,12},{9,13},{10,... | collective-permute-start | bytes 2359304 | tf_op jit(solution)/shard_map/ppermute | solution.py:117
  537.1 38.7 %all-to-all-start.11 = ((bf16[4,128,2048]{2,1,0:T(8,128)(2,1)}), bf16[4,128,2048]{2,1,0:T(8,128)(2,1)}, u32[]{:S(2)}, u32[]{:S(2)}) async-start(bf16[4,128,2048]{2,1,0:T(8,128)(2,1)} %bitcast.127), calls=%async_computation.11 | async-start | bytes 4194304 | tf_op jit(solution)/shard_map/all_to_all | solution.py:134
  590.2 46.3 %all-to-all-start.13 = ((bf16[4,128,2048]{2,1,0:T(8,128)(2,1)}), bf16[4,128,2048]{2,1,0:T(8,128)(2,1)}, u32[]{:S(2)}, u32[]{:S(2)}) async-start(bf16[4,128,2048]{2,1,0:T(8,128)(2,1)} %bitcast.126), calls=%async_computation.13 | async-start | bytes 4194304 | tf_op jit(solution)/shard_map/all_to_all | solution.py:134
  594.7 39.7 %collective-permute-start.41 = (bf16[512,768]{1,0:T(8,128)(2,1)}, bf16[512,768]{1,0:T(8,128)(2,1)}, u32[]{:S(2)}, u32[]{:S(2)}) collective-permute-start(bf16[512,768]{1,0:T(8,128)(2,1)} %grad.28), channel_id=1, source_target_pairs={{0,16},{1,17},{2,18},{3,19},{4,20},{5,21},{6,22},{7,23},{8,24},{9,... | collective-permute-start | bytes 2359304 | tf_op jit(solution)/shard_map/ppermute | solution.py:117
  596.1 38.3 %collective-permute-start.42 = (bf16[512,768]{1,0:T(8,128)(2,1)}, bf16[512,768]{1,0:T(8,128)(2,1)}, u32[]{:S(2)}, u32[]{:S(2)}) collective-permute-start(bf16[512,768]{1,0:T(8,128)(2,1)} %get-tuple-element.959), channel_id=1, source_target_pairs={{0,4},{1,5},{2,6},{3,7},{4,0},{5,1},{6,2},{7,3},{8,12},{9,13},{10,... | collective-permute-start | bytes 2359304 | tf_op jit(solution)/shard_map/ppermute | solution.py:117
  (204 other events, 2055.8 us)

commit v4 on v3

--- a/solution.py
+++ b/solution.py
@@ -5,7 +5,6 @@
 import jax.numpy as jnp
 from jax import lax
 from jax.experimental import pallas as pl
-from jax.experimental.layout import Layout, with_layout_constraint
 from jax.experimental.pallas import tpu as pltpu
 from jax.sharding import PartitionSpec as P
 
@@ -111,9 +110,6 @@
         return values
 
     def move(self, values, pairs):
-        if values.ndim == 2 and values.shape[1] % 128 and values.shape[0] > 8:
-            values = with_layout_constraint(values, Layout((0, 1)))
-            return with_layout_constraint(lax.ppermute(values, AXES, pairs), Layout((0, 1)))
         return lax.ppermute(values, AXES, pairs)
 
     def flip(self, values, c=0, x=0, e=0, b=0):
@@ -127,6 +123,11 @@
     def push(self, values, steps):
         stride = 4 * self.seq * steps
         return self.move(values, [(i, (i + stride) % self.count) for i in range(self.count)])
+
+    def push_beside(self, values, steps):
+        stride = 4 * self.seq * steps
+        pairs = [(i, (i + stride) % self.count ^ self.seq) for i in range(self.count)]
+        return self.move(values, pairs)
 
     def swap(self, values, groups):
         parts = len(groups[0])
@@ -191,11 +192,24 @@
         for k in range(2)
         for j in range(2)
     ]
-    return reorder(at, spots, values, [1])[0]
+    return reorder(at, spots, values, [1])
 
 
 def rows_of(shape, rows, index=lambda i: i):
     return pl.BlockSpec((rows, shape[1]), lambda i: (index(i), 0))
+
+
+def need(args, outs, scratch, tiles, out_tiles):
+    total = 6 * 2**20
+    for shapes, given in (
+        ([(v.shape, v.dtype) for v in args], tiles),
+        (list(outs), out_tiles),
+        ([(v.shape, v.dtype) for v in scratch], None),
+    ):
+        for k, (shape, kind) in enumerate(shapes):
+            block = given[k].block_shape if given and k in given else shape
+            total += math.prod(block) * jnp.dtype(kind).itemsize * (1 + (block is not shape)) * 9 // 8
+    return total
 
 
 def call(at, kernel, outs, *args, steps=1, tiles=None, out_tiles=None, scratch=(), name=None):
@@ -207,15 +221,6 @@
         zeros = (0,) * len(shape)
         return pl.BlockSpec(shape, lambda i: zeros, pipeline_mode=pl.Buffered(1))
 
-    size = 0
-    for shapes, given in (
-        ([(v.shape, v.dtype) for v in args], tiles),
-        (list(outs), out_tiles),
-        ([(v.shape, v.dtype) for v in scratch], None),
-    ):
-        for k, (shape, kind) in enumerate(shapes):
-            block = given[k].block_shape if given and k in given else shape
-            size += math.prod(block) * jnp.dtype(kind).itemsize * (1 + (block is not shape))
     least = min(range(len(args)), key=lambda i: args[i].size)
     in_specs = [spec(v.shape, v.dtype, k, tiles) for k, v in enumerate(args)]
     args = list(args)
@@ -228,7 +233,7 @@
         out_specs=[spec(shape, kind, k, out_tiles) for k, (shape, kind) in enumerate(outs)],
         scratch_shapes=list(scratch),
         compiler_params=pltpu.CompilerParams(
-            vmem_limit_bytes=min(size * 9 // 8 + 12 * 2**20, 60 * 2**20)
+            vmem_limit_bytes=max(need(args, outs, scratch, tiles, out_tiles), 20 * 2**20)
         ),
         cost_estimate=pl.CostEstimate(flops=0, bytes_accessed=0, transcendentals=0),
         name=name,
@@ -269,33 +274,35 @@
     return pl.ds(pl.multiple_of(i * TILE, TILE), TILE)
 
 
-def near_far(near, far):
-    half = near.shape[0] // TILE
-    return {
-        0: rows_of(near.shape, TILE, lambda i: jnp.minimum(i, half - 1)),
-        1: rows_of(far.shape, TILE, lambda i: jnp.maximum(i - half, 0)),
-    }
-
-
-def tile_from(near, far):
-    first = pl.program_id(0) < pl.num_programs(0) // 2
-    return jnp.where(first, near[...], far[...])
-
-
-def qkv_kernel(count, near, far, *refs):
-    gain, shift, bias, table, normed, mixed = refs[-6:]
-    centered, scale = centered_of(tile_from(near, far).astype(F32))
+def gathered(pieces, out):
+    rows = pieces[0].shape[0]
+    for i in range(4):
+
+        @pl.when(pl.program_id(0) == i)
+        def _():
+            out[:rows, :] = pieces[2 * i][...]
+            out[rows:, :] = pieces[2 * i + 1][...]
+
+
+def qkv_kernel(count, *refs):
+    pieces, blocks = refs[:8], refs[8:-7]
+    gain, shift, bias, table, normed, mixed, tile = refs[-7:]
+    gathered(pieces, tile)
+    centered, scale = centered_of(tile[...].astype(F32))
     normed[...] = (centered * scale * gain[...] + shift[...]).astype(BF16)
     turning = mixed.shape[1] * 2 // 3
-    values = product(normed, in_chunks(refs[:-6], count)) + bias[...]
-    mixed[:, :turning] = turned(values[:, :turning], table[...], 1.0).astype(BF16)
+    values = product(normed, in_chunks(blocks, count)) + bias[...]
+    both = turned(values[:, :turning], table[...], 1.0).astype(BF16)
+    mixed[:, : turning // 2] = both[:, : turning // 2] * 0.125
+    mixed[:, turning // 2 : turning] = both[:, turning // 2 :]
     mixed[:, turning:] = values[:, turning:].astype(BF16)
 
 
-def attended_grad_kernel(count, near, far, *refs):
+def attended_grad_kernel(count, *refs):
+    pieces, blocks = refs[:8], refs[8:-2]
     whole, grads = refs[-2:]
-    whole[...] = tile_from(near, far)
-    grads[...] = product(whole, in_chunks(refs[:-2], count)).astype(BF16)
+    gathered(pieces, whole)
+    grads[...] = product(whole, in_chunks(blocks, count)).astype(BF16)
 
 
 def head_of(ref, group, head, start):
@@ -318,7 +325,7 @@
 
 
 def scores_of(key, query, allowed):
-    return jnp.where(allowed, dot_cols(key, query) * 0.125, -1e30)
+    return jnp.where(allowed, dot_cols(key, query), -1e30)
 
 
 def attend_kernel(mixed, row, col, attended, sums):
@@ -338,8 +345,7 @@
             top = jnp.max(scores, axis=0, keepdims=True)
             expo = jnp.exp(scores - top)
             total = jnp.sum(expo, axis=0, keepdims=True)
-            probs = (expo * (1.0 / total)).astype(BF16)
-            out = jnp.transpose(dot_rows(value, probs))
+            out = jnp.transpose(dot_rows(value, (expo * (1.0 / total)).astype(BF16)))
             attended[span, h * HEAD_DIM : (h + 1) * HEAD_DIM] = out.astype(BF16)
             sums[pl.ds(i * heads + h, 1), :] = top + jnp.log(total)
 
@@ -389,8 +395,10 @@
         factors = table[span, :]
         for k, ref in enumerate((query_sum, key_sum, value_sum)):
             values = ref[span, :]
+            if k == 0:
+                values = values * 0.125
             if k < 2:
-                values = turned(values * 0.125, factors, -1.0)
+                values = turned(values, factors, -1.0)
             values = values.astype(BF16)
             low[span, k * part : (k + 1) * part] = values
             bias[:, k * part : (k + 1) * part] += jnp.sum(
@@ -408,60 +416,60 @@
 
 
 def total_of(terms):
-    rows = terms.shape[0] // 4
-    total = terms[:rows, :].astype(F32)
-    for i in range(1, 4):
-        total = total + terms[i * rows : (i + 1) * rows, :].astype(F32)
+    total = terms[0][...].astype(F32)
+    for term in terms[1:]:
+        total = total + term[...].astype(F32)
     return total
 
 
-def four(out, values):
-    rows = values.shape[0]
-    for i in range(4):
-        out[i * rows : (i + 1) * rows, :] = values
-
-
-def hidden_kernel(inputs, gain, shift, terms, hidden, normed):
+def hidden_kernel(inputs, gain, shift, *refs):
+    *terms, hidden, normed = refs
     values = inputs[...].astype(F32) + total_of(terms)
     hidden[...] = values
     centered, scale = centered_of(values)
-    four(normed, (centered * scale * gain[...] + shift[...]).astype(BF16))
-
-
-def result_kernel(hidden, terms, out):
+    normed[...] = (centered * scale * gain[...] + shift[...]).astype(BF16)
+
+
+def result_kernel(hidden, *refs):
+    *terms, out = refs
     out[...] = (hidden[...] + total_of(terms)).astype(BF16)
 
 
-def branch_kernel(hidden, cotangent, gain, terms, grad, low, gain_grad, shift_grad):
+def branch_kernel(hidden, cotangent, gain, *refs):
+    *terms, grad, low, gain_grad, shift_grad = refs
     pulled, gain_grad[...], shift_grad[...] = norm_back(hidden[...], gain[...], total_of(terms))
     values = cotangent[...].astype(F32) + pulled
     grad[...] = values
-    four(low, values.astype(BF16))
-
-
-def input_kernel(inputs, hidden_grad, gain, terms, grad, gain_grad, shift_grad):
+    low[...] = values.astype(BF16)
+
+
+def input_kernel(inputs, hidden_grad, gain, *refs):
+    *terms, grad, gain_grad, shift_grad = refs
     pulled, gain_grad[...], shift_grad[...] = norm_back(
         inputs[...].astype(F32), gain[...], total_of(terms)
     )
     grad[...] = hidden_grad[...] + pulled
 
 
-def mlp_kernel(count, near, far, *refs):
-    *blocks, normed, inner, gate_factor, up_factor = refs
-    units = inner.shape[1]
-    normed[...] = tile_from(near, far)
+def mlp_kernel(count, *refs):
+    pieces, blocks = refs[:8], refs[8:-4]
+    normed, inner, gate_factor, up_factor = refs[-4:]
+    units = gate_factor.shape[1]
+    gathered(pieces, normed)
     values = product(normed, in_chunks(blocks, count))
     gate, up = values[:, :units], values[:, units:]
     sigmoid = 1.0 / (1.0 + jnp.exp(-gate))
     silu = gate * sigmoid
-    inner[...] = (silu * up).astype(BF16)
+    inner[:, :units] = (silu * up).astype(BF16)
+    if inner.shape[1] > units:
+        inner[:, units:] = jnp.zeros((inner.shape[0], inner.shape[1] - units), BF16)
     gate_factor[...] = up * sigmoid * (1.0 + gate * (1.0 - sigmoid))
     up_factor[...] = silu
 
 
 def mlp_back_kernel(count, grads, *refs):
     *blocks, gate_factor, up_factor, pair = refs
-    values = product(grads, in_chunks(blocks, count))
+    values = product(grads, in_chunks(blocks, count))[:, : gate_factor.shape[1]]
     pair[...] = jnp.concatenate(
         [(values * gate_factor[...]).astype(BF16), (values * up_factor[...]).astype(BF16)],
         axis=1,
@@ -489,56 +497,66 @@
 
 
 def cut_kernel(counts, *refs):
-    weights, outs = refs[: len(counts)], refs[len(counts) :]
+    *weights, out = refs
     rows = weights[0].shape[0]
-    parts = part_list(weights, counts)
-    cuts = segments([width for _, _, width in parts], [out.shape[1] for out in outs])
-    for part, begin, chunk, col, size in cuts:
-        ref, p, width = parts[part]
+    col = 0
+    for ref, p, width in part_list(weights, counts):
         for j in range(8):
-            start = (p * 8 + j) * width + begin
-            outs[chunk][j * rows : (j + 1) * rows, col : col + size] = ref[:, start : start + size]
-
-
-def spread_kernel(counts, *refs):
+            start = (p * 8 + j) * width
+            out[j * rows : (j + 1) * rows, col : col + width] = ref[:, start : start + width]
+        col += width
+    if col < out.shape[1]:
+        out[:, col:] = jnp.zeros((out.shape[0], out.shape[1] - col), BF16)
+
+
+def spread_kernel(counts, strips, *refs):
     chunks, outs = refs[: -len(counts)], refs[-len(counts) :]
     rows = outs[0].shape[0]
     parts = part_list(outs, counts)
-    cuts = segments([width for _, _, width in parts], [chunk.shape[1] for chunk in chunks])
-    for part, begin, chunk, col, size in cuts:
+    cuts = segments([width for _, _, width in parts], [width for _, _, width in strips])
+    for part, begin, strip, col, size in cuts:
         ref, p, width = parts[part]
+        chunk, first, _ = strips[strip]
         for j in range(8):
             start = (p * 8 + j) * width + begin
-            piece = chunks[chunk][j * rows : (j + 1) * rows, col : col + size]
+            piece = chunks[chunk][j * rows : (j + 1) * rows, first + col : first + col + size]
             ref[:, start : start + size] = piece.astype(F32)
 
 
-def sum_kernel(*refs):
+def sum_kernel(counts, *refs):
     *terms, out = refs
-    total = terms[0][...].astype(F32)
-    for term in terms[1:]:
-        total = total + term[...].astype(F32)
-    out[...] = total.astype(BF16)
-
-
-def cut_rows(at, weights, counts, chunks):
-    rows = weights[0].shape[0]
-    return call(
+    col = 0
+    for count in counts:
+        mine, terms = terms[:count], terms[count:]
+        total = mine[0][...].astype(F32)
+        for term in mine[1:]:
+            total = total + term[...].astype(F32)
+        out[:, col : col + total.shape[1]] = total.astype(BF16)
+        col += total.shape[1]
+
+
+def cut_rows(at, weights, counts, wide):
+    (out,) = call(
         at,
         functools.partial(cut_kernel, counts),
-        [((8 * rows, n), BF16) for n in chunks],
+        [((8 * weights[0].shape[0], wide), BF16)],
         *weights,
         name="cut",
     )
-
-
-def split_kernel(whole, *outs):
-    col = 0
+    return out
+
+
+def split_kernel(col, whole, *outs):
     for out in outs:
         out[...] = whole[:, col : col + out.shape[1]]
         col += out.shape[1]
 
 
+def split(at, whole, begin, widths):
+    outs = [((whole.shape[0], n), BF16) for n in widths]
+    return call(at, functools.partial(split_kernel, begin), outs, whole, name="split")
+
+
 def cross_block(at, block):
     return [block] + [at.shift(block, i) for i in range(1, at.outer)]
 
@@ -551,22 +569,26 @@
     return [block] + [at.shift(block, i) for i in range(1, at.outer)]
 
 
-def grad_kernel(count, begin, values, grads, *refs):
-    addends, outs = refs[:count], refs[count:]
+def grad_kernel(count, ways, *refs):
+    many = 2 * len(ways)
+    pairs, addends, outs = refs[:many], refs[many : many + count], refs[many + count :]
     each = pl.num_programs(0) // len(outs)
     for k, out in enumerate(outs):
 
         @pl.when(pl.program_id(0) // each == k)
         def _():
-            total = dot_rows(values[...], grads[:, begin : begin + out.shape[1]])
-            if k < count:
-                total = total + addends[k][...].astype(F32)
-            out[...] = total.astype(out.dtype)
-
-
-def grad_blocks(at, way, spots, kind, addends=()):
-    values, grads, begin, size = way
-    tokens, wide = values.shape
+            col = 0
+            for i, (begin, size) in enumerate(ways):
+                values, grads = pairs[2 * i : 2 * i + 2]
+                total = dot_rows(values[...], grads[:, begin : begin + size])
+                if k < count:
+                    total = total + addends[k][:, col : col + size].astype(F32)
+                out[:, col : col + size] = total.astype(out.dtype)
+                col += size
+
+
+def grad_blocks(at, ways, spots, kind, addends=()):
+    tokens, wide = ways[0][0].shape
     width = wide // (2 * at.outer)
     tile = min(TILE, width)
     each = width // tile
@@ -580,16 +602,15 @@
     def row_of(k):
         return lambda i: jnp.clip(i - k * each, 0, each - 1)
 
-    shape = (width, size)
-    tiles = {0: pl.BlockSpec((tokens, tile), lambda i: (0, column(i)))}
+    shape = (width, sum(way[3] for way in ways))
+    tiles = {2 * i: pl.BlockSpec((tokens, tile), lambda i: (0, column(i))) for i in range(len(ways))}
     for k in range(len(addends)):
-        tiles[2 + k] = rows_of(shape, tile, row_of(k))
+        tiles[2 * len(ways) + k] = rows_of(shape, tile, row_of(k))
     return call(
         at,
-        functools.partial(grad_kernel, len(addends), begin),
+        functools.partial(grad_kernel, len(addends), tuple(way[2:] for way in ways)),
         [(shape, kind)] * len(spots),
-        values,
-        grads,
+        *[v for way in ways for v in way[:2]],
         *addends,
         steps=len(spots) * each,
         tiles=tiles,
@@ -598,16 +619,16 @@
     )
 
 
-def grad_beside(at, way):
+def grad_beside(at, *way):
     order = list(range(1, at.outer)) + [0]
     return grad_blocks(at, way, [2 * i + 1 for i in order], BF16)
 
 
-def grad_own(at, way):
+def grad_own(at, *way):
     return grad_blocks(at, way, [0], F32)[0]
 
 
-def grad_across(at, way, sent):
+def grad_across(at, sent, *way):
     if at.outer == 1:
         return []
     return grad_blocks(at, way, [2 * i for i in range(1, at.outer)], BF16, sent[: at.outer - 1])
@@ -621,35 +642,93 @@
     return [at.flip(v, e=1) for v in made]
 
 
-def grad_spread(at, chunks, counts, widths):
+def grad_spread(at, chunks, counts, strips, widths):
     rows = chunks[0].shape[0] // 8
     return call(
         at,
-        functools.partial(spread_kernel, counts),
+        functools.partial(spread_kernel, counts, strips),
         [((rows, n), F32) for n in widths],
         *chunks,
         name="spread",
     )
 
 
-def join_kernel(near, far, out):
-    out[...] = tile_from(near, far)
+def join_kernel(place, near, far, out):
+    rows = near.shape[0] // 4
+    for half, ref in enumerate((near, far)):
+        for d in range(4):
+            start = pl.multiple_of((place[0] ^ d) * rows, rows)
+            low = (half * 4 + d) * rows
+            out[low : low + rows, :] = ref[pl.ds(start, rows), :]
 
 
 def joined_rows(at, near, far):
+    place = jnp.reshape(at.b * 2 + at.x, (1,)).astype(jnp.int32)
     shape = (2 * near.shape[0], near.shape[1])
-    (out,) = call(
-        at,
-        join_kernel,
-        [(shape, BF16)],
-        near,
-        far,
-        steps=shape[0] // TILE,
-        tiles=near_far(near, far),
-        out_tiles={0: rows_of(shape, TILE)},
-        name="join",
-    )
+    (out,) = call(at, join_kernel, [(shape, BF16)], place, near, far, name="join")
     return out
+
+
+def spread_tokens(at, values):
+    low = at.flip(values, b=1)
+    beside = at.flip(values, x=1)
+    return [values, beside, low, at.flip(low, x=1)]
+
+
+def send_pieces(at, pieces):
+    return [pieces[0], at.flip(pieces[1], x=1), pieces[2], at.flip(pieces[3], x=1)]
+
+
+def pass_pieces(at, pieces):
+    return [pieces[0], pieces[1], at.flip(add(at, pieces[2:]), b=1)]
+
+
+def expand_add_kernel(count, values, *refs):
+    blocks, other, outs = refs[:-5], refs[-5], refs[-4:]
+    chunks = in_chunks(blocks, count)
+    width = blocks[0].shape[0]
+    rows = outs[0].shape[0]
+    for j in range(count):
+        cols = slice(j * width, (j + 1) * width)
+        total = transposed_product(values, chunks, j) + other[:, cols].astype(F32)
+        total = total.astype(BF16)
+        for i in range(2):
+
+            @pl.when(pl.program_id(0) == i)
+            def _():
+                outs[2 * i][:, cols] = total[:rows]
+                outs[2 * i + 1][:, cols] = total[rows:]
+
+
+def expand_pieces(at, values, chunks, other):
+    blocks = [block for chunk in chunks for block in chunk]
+    shape = (other.shape[0] // 4, other.shape[1])
+    return call(
+        at,
+        functools.partial(expand_add_kernel, len(chunks[0])),
+        [(shape, BF16)] * 4,
+        values,
+        *blocks,
+        other,
+        steps=other.shape[0] // TILE,
+        tiles={
+            0: rows_of(values.shape, TILE),
+            1 + len(blocks): rows_of(other.shape, TILE),
+        },
+        name="expand_add",
+    )
+
+
+def add_pieces_kernel(own, other, *outs):
+    rows = outs[0].shape[0]
+    for d, out in enumerate(outs):
+        span = slice(d * rows, (d + 1) * rows)
+        out[...] = (own[span, :] + other[span, :].astype(F32)).astype(BF16)
+
+
+def add_pieces(at, own, other):
+    shape = (own.shape[0] // 4, own.shape[1])
+    return call(at, add_pieces_kernel, [(shape, BF16)] * 4, own, other, name="pieces")
 
 
 def expand(at, values, chunks, side, kind):
@@ -672,46 +751,36 @@
     return out
 
 
-def add(at, *terms):
-    shape = terms[0].shape
-    tile = min(TILE, shape[0])
+def add(at, *sums):
+    rows = sums[0][0].shape[0]
+    tile = min(TILE, rows)
+    terms = [v for each in sums for v in each]
+    shape = (rows, sum(each[0].shape[1] for each in sums))
     (total,) = call(
         at,
-        sum_kernel,
+        functools.partial(sum_kernel, tuple(len(each) for each in sums)),
         [(shape, BF16)],
         *terms,
-        steps=shape[0] // tile,
-        tiles={k: rows_of(shape, tile) for k in range(len(terms))},
+        steps=rows // tile,
+        tiles={k: rows_of(v.shape, tile) for k, v in enumerate(terms)},
         out_tiles={0: rows_of(shape, tile)},
         name="add",
     )
     return total
 
 
-def fetch_small(at, values):
-    block = values[None]
-    block = joined(at.c, block, at.flip(block, c=1), 0)
-    block = joined(at.x, block, at.flip(block, x=1), 0)
-    block = joined(at.b, block, at.flip(block, b=1), 0)
-    whole = jnp.stack([block] + [at.shift(block, i) for i in range(1, at.outer)])
-    return jnp.stack([whole, at.flip(whole, e=1)], axis=1)
-
-
-def deliver_small(at, values):
-    whole = values[:, 0] + at.flip(values[:, 1], e=1)
-    block = whole[0]
+def send_small(at, values):
+    total = values[0, 0] + at.flip(values[0, 1], e=1)
     for i in range(1, at.outer):
-        block = block + at.push(whole[i], i)
-    for bit, name in ((at.b, "b"), (at.x, "x"), (at.c, "c")):
-        rows = block.shape[0] // 2
-        low, high = block[:rows], block[rows:]
-        block = pick(bit, low, high) + at.flip(pick(bit, high, low), **{name: 1})
-    return block[0]
+        total = total + at.push(values[i, 0], i)
+        total = total + at.push_beside(values[i, 1], i)
+    return total
 
 
 def order_tokens(at, values):
     seqs, length = values.shape
     view = values.reshape(seqs, 2, 2, length // 4)
+    view = pick(at.x, view, view[:, ::-1])
     view = pick(at.c, view, view[:, :, ::-1])
     return jnp.swapaxes(view, 1, 2).reshape(seqs, length)
 
@@ -746,49 +815,47 @@
     count = 2 * at.outer
     near = layer_input.shape[0]
 
-    first = 2 * units // 256 * 128
-    second = 2 * units - first
+    second = 2 * units // 256 * 128
+    first = 2 * units - second
     v = Window()
+    padded = (units + 127) // 128 * 128
     thin, wide = (tokens, units), (tokens, 2 * units)
 
-    (cut_now,) = cut_rows(at, [qkv_weight, out_weight], (3, 1), (4 * part,))
-    v.front = at.swap(cut_now, at.groups)
-    v.inputs, v.inputs_four = to_relative(at, layer_input, [1, 4])
-    v.first_cut, v.second_cut = cut_rows(at, [gate_weight, up_weight], (1, 1), (first, second))
-    (v.down_cut,) = cut_rows(at, [down_weight], (1,), (units,))
+    v.front = at.swap(cut_rows(at, [qkv_weight, out_weight], (3, 1), 4 * part), at.groups)
+    v.small = jnp.concatenate([at.after(qkv_bias), ln1_gain, ln1_bias, ln2_gain, ln2_bias])[None]
+    v.small = joined(at.c, v.small, at.flip(v.small, c=1), 0)
+    v.small = joined(at.x, v.small, at.flip(v.small, x=1), 0)
+    (v.inputs,) = to_relative(at, layer_input, [1])
+    v.later = cut_rows(at, [gate_weight, up_weight, down_weight], (1, 1, 1), 2 * units + padded)
     v.cotangent, v.cotangent_four = to_relative(at, cotangent, [1, 4])
-    v.small = jnp.concatenate([qkv_bias, ln1_gain, ln1_bias, ln2_gain, ln2_bias])
     spots = jnp.concatenate([segment_ids, positions[None]], axis=0)[None]
-    v.spots = joined(at.b, spots, at.flip(spots, b=1), 0)
-    v.close(at)
-
-    v.qkv, v.out = call(
-        at,
-        split_kernel,
-        [((8 * rows, 3 * part), BF16), ((8 * rows, part), BF16)],
-        v.front,
-        name="split",
-    )
+    v.spots = jnp.concatenate([spots, at.flip(spots, b=1)], axis=0)
+    v.close(at)
+
+    v.qkv, v.out = split(at, v.front, 0, (3 * part, part))
     del v.front
     v.qkv_across = cross_block(at, v.qkv)
     v.qkv_beside = [at.flip(v.qkv, e=1)]
-    v.near = at.swap(v.inputs_four, at.sides)
-    v.first = at.swap(v.first_cut, at.groups)
-    v.small = fetch_small(at, v.small)
+    v.tokens = spread_tokens(at, v.inputs)
+    v.turned = [at.flip(v.tokens[1], c=1)]
+    v.small = joined(at.b, v.small, at.flip(v.small, b=1), 0)
+    v.small = jnp.stack([v.small] + [at.shift(v.small, i) for i in range(1, at.outer)])
     segments_here = order_tokens(at, v.spots[:, 0])
     places = order_tokens(at, v.spots[:, 1])
     index = order_tokens(at, jnp.arange(length)[None])
-    v.row = jnp.concatenate([segments_here, index], axis=0).astype(F32)
-    v.col = jnp.transpose(v.row)
+    v.row = jnp.concatenate([segments_here, index, jnp.zeros((5, length), index.dtype)], axis=0)
+    v.row = v.row.astype(F32)
+    v.col = jnp.pad(jnp.transpose(v.row), ((0, 0), (0, 120)))
     places = places.reshape(2, 2, length // 2).swapaxes(0, 1).reshape(2 * length)
     v.table = rotary_tables(places)
     v.close(at)
 
     v.qkv_beside += flip_all(at, v.qkv_across[1:])
-    v.far = at.flip(v.near, c=1)
+    v.turned = [at.flip(v.tokens[0], c=1), *v.turned] + [at.flip(t, c=1) for t in v.tokens[2:]]
     v.out_across = cross_block(at, v.out)
-    v.out_beside = [at.flip(v.out, e=1)]
-    v.cotangent_near = at.swap(v.cotangent_four, at.sides)
+    v.later = at.swap(v.later, at.groups)
+
+    v.small = jnp.stack([v.small, at.flip(v.small, e=1)], axis=1)
 
     def vector(i):
         start = bias_rows + i * rows
@@ -803,28 +870,28 @@
     v.bias = bias.reshape(1, 3 * part).astype(F32)
     v.close(at)
     v.qkv_blocks = [merge_blocks(v.qkv_across, v.qkv_beside)]
-    del v.qkv_across, v.qkv_beside, v.qkv, v.small, v.spots, v.inputs_four, v.cotangent_four, v.first_cut
-
+    del v.qkv_across, v.qkv_beside, v.qkv, v.small, v.spots
+
+    (v.first,) = split(at, v.later, 0, (first,))
     v.first_across = cross_block(at, v.first)
     v.first_beside = [at.flip(v.first, e=1)]
-    v.out_beside += flip_all(at, v.out_across[1:])
-    v.cotangent_far = at.flip(v.cotangent_near, c=1)
-    v.second = at.swap(v.second_cut, at.groups)
-    v.down = at.swap(v.down_cut, at.groups)
+    v.out_beside = flip_all(at, v.out_across)
+    v.cotangent_near = at.swap(v.cotangent_four, at.sides)
     v.normed, v.mixed = call(
         at,
         functools.partial(qkv_kernel, count),
         [((tokens, width), BF16), ((tokens, 3 * part), BF16)],
-        v.near,
-        v.far,
+        *v.tokens,
+        *v.turned,
         *v.qkv_blocks[0],
         v.gains[0],
         v.gains[1],
         v.bias,
         v.table,
         steps=tokens // TILE,
-        tiles=near_far(v.near, v.far) | {5 + count: rows_of(v.table.shape, TILE)},
+        tiles={11 + count: rows_of(v.table.shape, TILE)},
         out_tiles={0: rows_of((tokens, width), TILE), 1: rows_of((tokens, 3 * part), TILE)},
+        scratch=[pltpu.VMEM((TILE, width), BF16)],
         name="qkv",
     )
     v.attended, v.sums = call(
@@ -838,33 +905,36 @@
     )
     v.out_blocks = [merge_blocks(v.out_across, v.out_beside)]
     v.other = expand(at, v.attended, v.out_blocks, 1, BF16)
-    v.own = expand(at, v.attended, v.out_blocks, 0, F32)
-    v.close(at)
-    del v.out_across, v.out_beside, v.out, v.second_cut, v.down_cut
+    v.second, v.down = split(at, v.later, first, (second, padded))
+    v.close(at)
+    del v.later
+    del v.out_across, v.out_beside, v.out, v.cotangent_four
 
     v.other = at.flip(v.other, c=1)
+    v.cotangent_far = at.flip(v.cotangent_near, c=1)
+    v.pieces = expand_pieces(at, v.attended, v.out_blocks, v.other)
+    v.close(at)
+
+    v.terms = pass_pieces(at, send_pieces(at, v.pieces))
     v.cotangent_all = joined_rows(at, v.cotangent_near, v.cotangent_far)
-    v.close(at)
-    del v.cotangent_near, v.cotangent_far
-
-    v.terms = at.swap(add(at, v.own, v.other), at.sides)
     v.second_across = cross_block(at, v.second)
     v.second_beside = [at.flip(v.second, e=1)]
     v.first_beside += flip_all(at, v.first_across[1:])
     v.close(at)
-    del v.own, v.other
-
-    v.hidden, normed2_four = call(
+    del v.other, v.pieces, v.cotangent_near, v.cotangent_far
+
+    v.hidden, normed2 = call(
         at,
         hidden_kernel,
-        [((near, width), F32), ((4 * near, width), BF16)],
+        [((near, width), F32), ((near, width), BF16)],
         v.inputs,
         v.gains[2],
         v.gains[3],
-        v.terms,
+        *v.terms,
         name="hidden",
     )
-    v.near = at.swap(normed2_four, at.sides)
+    v.tokens = spread_tokens(at, normed2)
+    v.turned = [at.flip(v.tokens[1], c=1)]
     v.down_across = cross_block(at, v.down)
     v.down_beside = [at.flip(v.down, e=1)]
     v.second_beside += flip_all(at, v.second_across[1:])
@@ -875,26 +945,26 @@
     ]
     del v.first_across, v.first_beside, v.second_across, v.second_beside, v.first, v.second
 
-    v.far = at.flip(v.near, c=1)
+    v.turned = [at.flip(v.tokens[0], c=1), *v.turned] + [at.flip(t, c=1) for t in v.tokens[2:]]
     v.down_beside += flip_all(at, v.down_across[1:])
     v.normed2, v.inner, v.gate_factor, v.up_factor = call(
         at,
         functools.partial(mlp_kernel, count),
-        [((tokens, width), BF16), (thin, BF16), (thin, F32), (thin, F32)],
-        v.near,
-        v.far,
+        [((tokens, width), BF16), ((tokens, padded), BF16), (thin, F32), (thin, F32)],
+        *v.tokens,
+        *v.turned,
         *v.pair_blocks[0],
         *v.pair_blocks[1],
         steps=tokens // TILE,
-        tiles=near_far(v.near, v.far),
         out_tiles={0: rows_of((tokens, width), TILE)}
-        | {k: rows_of(thin, TILE) for k in range(1, 4)},
+        | {1: rows_of((tokens, padded), TILE)}
+        | {k: rows_of(thin, TILE) for k in (2, 3)},
         name="mlp",
     )
-    v.down_made = grad_beside(at, (v.cotangent_all, v.inner, 0, units))
+    v.down_made = grad_beside(at, (v.cotangent_all, v.inner, 0, padded))
     v.close(at)
     v.down_blocks = [merge_blocks(v.down_across, v.down_beside)]
-    del v.down_across, v.down_beside, v.down, v.near, v.far
+    del v.down_across, v.down_beside, v.down, v.tokens, v.turned
 
     v.down_sent = flip_all(at, v.down_made[:-1])
     (v.pair_low,) = call(
@@ -916,63 +986,73 @@
     )
     v.other = expand(at, v.pair_low, v.pair_blocks, 1, BF16)
     v.own = expand(at, v.pair_low, v.pair_blocks, 0, F32)
-    v.down_own = grad_own(at, (v.cotangent_all, v.inner, 0, units))
+    v.down_own = grad_own(at, (v.cotangent_all, v.inner, 0, padded))
     v.close(at)
 
     v.other = at.flip(v.other, c=1)
-    v.down_cross = grad_across(at, (v.cotangent_all, v.inner, 0, units), v.down_sent)
-    v.first_made = grad_beside(at, (v.normed2, v.pair_low, 0, first))
-    v.close(at)
-
-    v.terms = at.swap(add(at, v.own, v.other), at.sides)
+    v.down_cross = grad_across(at, v.down_sent, (v.cotangent_all, v.inner, 0, padded))
+    v.first_made = grad_beside(at, (v.normed2, v.pair_low, first, second))
+    v.pieces = add_pieces(at, v.own, v.other)
+    v.close(at)
+
+    v.terms = pass_pieces(at, send_pieces(at, v.pieces))
     v.down_far = push_all(at, v.down_cross)
     v.down_sent += flip_all(at, v.down_made[-1:])
     v.first_sent = flip_all(at, v.first_made[:-1])
-    v.second_made = grad_beside(at, (v.normed2, v.pair_low, first, second))
-    v.first_own = grad_own(at, (v.normed2, v.pair_low, 0, first))
-    v.second_own = grad_own(at, (v.normed2, v.pair_low, first, second))
+    v.second_made = grad_beside(at, (v.normed2, v.pair_low, 0, first))
+    v.first_own = grad_own(at, (v.normed2, v.pair_low, first, second))
+    v.second_own = grad_own(at, (v.normed2, v.pair_low, 0, first))
     v.result_other = expand(at, v.inner, v.down_blocks, 1, BF16)
     v.result_own = expand(at, v.inner, v.down_blocks, 0, F32)
     v.close(at)
     del v.down_cross, v.down_made, v.own, v.other
 
-    v.hidden_grad, branch_four, v.gain_two_grad, v.shift_two_grad = call(
+    v.hidden_grad, branch, v.gain_two_grad, v.shift_two_grad = call(
         at,
         branch_kernel,
-        [((near, width), F32), ((4 * near, width), BF16)] + [((1, width), F32)] * 2,
+        [((near, width), F32), ((near, width), BF16)] + [((1, width), F32)] * 2,
         v.hidden,
         v.cotangent,
         v.gains[2],
-        v.terms,
+        *v.terms,
         name="branch",
     )
-    v.near = at.swap(branch_four, at.sides)
-    v.first_far = push_all(at, grad_across(at, (v.normed2, v.pair_low, 0, first), v.first_sent))
+    v.tokens = spread_tokens(at, branch)
+    v.turned = [at.flip(v.tokens[1], c=1)]
+    v.first_far = push_all(at, grad_across(at, v.first_sent, (v.normed2, v.pair_low, first, second)))
     v.first_sent += flip_all(at, v.first_made[-1:])
     v.second_sent = flip_all(at, v.second_made[:-1])
+    v.close(at)
+    del v.first_made, v.pieces
+
+    v.turned = [at.flip(v.tokens[0], c=1), *v.turned] + [at.flip(t, c=1) for t in v.tokens[2:]]
     v.result_other = at.flip(v.result_other, c=1)
-    v.down_total = add(at, v.down_own, v.down_sent[-1], *v.down_far)
-    v.close(at)
-    del v.first_made, v.down_own, v.down_sent, v.down_far
-
-    v.far = at.flip(v.near, c=1)
-    v.second_far = push_all(
-        at, grad_across(at, (v.normed2, v.pair_low, first, second), v.second_sent)
-    )
+    v.early = add(
+        at,
+        [v.down_own, v.down_sent[-1], *v.down_far],
+        [v.first_own, v.first_sent[-1], *v.first_far],
+    )
+    v.second_cross = grad_across(at, v.second_sent, (v.normed2, v.pair_low, 0, first))
+    v.pieces = add_pieces(at, v.result_own, v.result_other)
+    v.close(at)
+    del v.first_own, v.first_sent, v.first_far, v.down_own, v.down_sent, v.down_far
+    del v.result_own, v.result_other
+
+    v.early = at.swap(v.early, at.groups)
+    v.second_far = push_all(at, v.second_cross)
     v.second_sent += flip_all(at, v.second_made[-1:])
-    v.down_pieces = at.swap(v.down_total, at.groups)
     v.branch, v.attended_grad = call(
         at,
         functools.partial(attended_grad_kernel, count),
         [((tokens, width), BF16), ((tokens, part), BF16)],
-        v.near,
-        v.far,
+        *v.tokens,
+        *v.turned,
         *v.out_blocks[0],
         steps=tokens // TILE,
-        tiles=near_far(v.near, v.far),
         out_tiles={0: rows_of((tokens, width), TILE), 1: rows_of((tokens, part), TILE)},
         name="attended_grad",
     )
+    v.out_sent = flip_all(at, grad_beside(at, (v.branch, v.attended, 0, part)))
     v.mixed_low, v.bias_part = call(
         at,
         attend_back_kernel,
@@ -988,71 +1068,77 @@
     )
     v.qkv_made = grad_beside(at, (v.normed, v.mixed_low, 0, 3 * part))
     v.other = expand(at, v.mixed_low, v.qkv_blocks, 1, BF16)
-    v.own = expand(at, v.mixed_low, v.qkv_blocks, 0, F32)
-    v.out_made = grad_beside(at, (v.branch, v.attended, 0, part))
-    v.first_total = add(at, v.first_own, v.first_sent[-1], *v.first_far)
-    v.result_terms = add(at, v.result_own, v.result_other)
-    v.close(at)
-    del v.near, v.far, v.second_made, v.attended_grad, v.down_total, v.result_own, v.result_other
-    del v.first_own, v.first_sent, v.first_far
-
+    v.close(at)
+    del v.tokens, v.turned, v.second_made, v.second_cross, v.attended_grad
+
+    v.late = at.swap(add(at, [v.second_own, v.second_sent[-1], *v.second_far]), at.groups)
+    v.out_far = push_all(at, grad_across(at, v.out_sent, (v.branch, v.attended, 0, part)))
     v.other = at.flip(v.other, c=1)
     v.qkv_sent = flip_all(at, v.qkv_made[:-1])
-    v.out_sent = flip_all(at, v.out_made)
-    v.result_terms = at.swap(v.result_terms, at.sides)
+    result_pieces = send_pieces(at, v.pieces)
     v.qkv_own = grad_own(at, (v.normed, v.mixed_low, 0, 3 * part))
     v.out_own = grad_own(at, (v.branch, v.attended, 0, part))
-    v.second_total = add(at, v.second_own, v.second_sent[-1], *v.second_far)
-    (v.down_grad,) = grad_spread(at, [v.down_pieces], (1,), (8 * units,))
-    v.close(at)
-    del v.second_own, v.second_sent, v.second_far, v.down_pieces
-
-    v.qkv_far = push_all(at, grad_across(at, (v.normed, v.mixed_low, 0, 3 * part), v.qkv_sent))
-    v.terms = at.swap(add(at, v.own, v.other), at.sides)
+    v.result_terms = pass_pieces(at, result_pieces)
+    v.pieces = expand_pieces(at, v.mixed_low, v.qkv_blocks, v.other)
+    v.qkv_cross = grad_across(at, v.qkv_sent, (v.normed, v.mixed_low, 0, 3 * part))
+    v.close(at)
+    del v.second_own, v.second_sent, v.second_far
+
+    v.qkv_far = push_all(at, v.qkv_cross)
+    v.terms = pass_pieces(at, send_pieces(at, v.pieces))
     v.qkv_sent += flip_all(at, v.qkv_made[-1:])
-    v.first_pieces = at.swap(v.first_total, at.groups)
-    v.out_cross = grad_across(at, (v.branch, v.attended, 0, part), v.out_sent)
     (v.result,) = call(
-        at, result_kernel, [((near, width), BF16)], v.hidden, v.result_terms, name="result"
-    )
-    v.result = to_absolute(at, v.result)
-    v.close(at)
-
-    v.qkv_pieces = at.swap(add(at, v.qkv_own, v.qkv_sent[-1], *v.qkv_far), at.groups)
-    v.out_far = push_all(at, v.out_cross)
-    v.second_pieces = at.swap(v.second_total, at.groups)
-    v.input_grad, v.gain_one_grad, v.shift_one_grad = call(
+        at, result_kernel, [((near, width), BF16)], v.hidden, *v.result_terms, name="result"
+    )
+    (v.result,) = to_absolute(at, v.result)
+    (v.down_grad,) = grad_spread(at, [v.early], (1,), ((0, 0, units),), (8 * units,))
+    v.close(at)
+    del v.other, v.qkv_made, v.pieces
+
+    v.back = at.swap(
+        add(
+            at,
+            [v.qkv_own, v.qkv_sent[-1], *v.qkv_far],
+            [v.out_own, v.out_sent[-1], *v.out_far],
+        ),
+        at.groups,
+    )
+    v.input_grad, gain_one_grad, shift_one_grad = call(
         at,
         input_kernel,
         [((near, width), F32)] + [((1, width), F32)] * 2,
         v.inputs,
         v.hidden_grad,
         v.gains[0],
-        v.terms,
+        *v.terms,
         name="inputs",
     )
-    v.close(at)
-    v.out_pieces = at.swap(add(at, v.out_own, v.out_sent[-1], *v.out_far), at.groups)
-    input_grad = to_absolute(at, v.input_grad)
     gate_wgrad, up_wgrad = grad_spread(
-        at, [v.first_pieces, v.second_pieces], (1, 1), (8 * units,) * 2
-    )
-    (qkv_wgrad,) = grad_spread(at, [v.qkv_pieces], (3,), (24 * part,))
-    (out_wgrad,) = grad_spread(at, [v.out_pieces], (1,), (8 * part,))
-    result, down_grad, bias_part = v.result, v.down_grad, v.bias_part
-    gain_one_grad, shift_one_grad = v.gain_one_grad, v.shift_one_grad
-    gain_two_grad, shift_two_grad = v.gain_two_grad, v.shift_two_grad
-
-    bias_part = bias_part.reshape(3, 1, part)
+        at,
+        [v.early, v.late],
+        (1, 1),
+        ((1, 0, first), (0, padded, second)),
+        (8 * units,) * 2,
+    )
+    (input_grad,) = to_absolute(at, v.input_grad)
+    v.done = [gate_wgrad, up_wgrad, input_grad]
+    bias_part = v.bias_part.reshape(3, 1, part)
     own_slot = (jnp.arange(8) == slot).astype(F32)[None, :, None]
     bias_whole = (bias_part * own_slot).reshape(at.outer, 2, 2, 4, bias_rows).swapaxes(1, 2)
     bias_whole = jnp.roll(bias_whole, -at.a, axis=0)
     bias_whole = pick(at.e, bias_whole, bias_whole[:, ::-1]).reshape(at.outer, 2, 8, bias_rows)
     grads = [
-        v.reshape(at.outer, 2, 8, rows)
-        for v in (gain_one_grad, shift_one_grad, gain_two_grad, shift_two_grad)
+        g.reshape(at.outer, 2, 8, rows)
+        for g in (gain_one_grad, shift_one_grad, v.gain_two_grad, v.shift_two_grad)
     ]
-    shares = deliver_small(at, jnp.concatenate([bias_whole] + grads, axis=-1))
+    v.small = send_small(at, jnp.concatenate([bias_whole] + grads, axis=-1))
+    v.close(at)
+    gate_wgrad, up_wgrad, input_grad = v.done
+    result, down_grad = v.result, v.down_grad
+    shares = jnp.sum(at.swap(v.small, at.groups), axis=0)
+    qkv_wgrad, out_wgrad = grad_spread(
+        at, [v.back], (3, 1), ((0, 0, 4 * part),), (24 * part, 8 * part)
+    )
 
     def share(i):
         return shares[bias_rows + i * rows : bias_rows + (i + 1) * rows]

time: 720 us -> 552 us (0.77)
  local copies, waits for them, and re-layouts: 141 us -> 72.5 us
  waiting for transfers between devices: 272 us -> 215 us
  starting transfers between devices: 140 us -> 111 us
  Pallas kernels: 141 us -> 132 us
    unnamed x326 -> x216, local copies, waits for them, and re-layouts: 116 us -> 55.4 us
    ppermute x6 -> x0, waiting for transfers between devices: 59 us -> none  [move(): lax.ppermute(values, AXES, pairs)]
    all_to_all x17 -> x7, starting transfers between devices: 76.8 us -> 28.6 us  [swap(): lax.all_to_all(view, AXES, 0, 0, axis_index_groups=groups, tiled=True)]
    ppermute x43 -> x77, waiting for transfers between devices: 171 us -> 211 us  [move(): return lax.ppermute(values, AXES, pairs)]
    all_to_all x17 -> x7, waiting for transfers between devices: 41.5 us -> 4.52 us  [swap(): lax.all_to_all(view, AXES, 0, 0, axis_index_groups=groups, tiled=True)]
    ppermute x43 -> x77, starting transfers between devices: 57 us -> 82.5 us  [move(): return lax.ppermute(values, AXES, pairs)]
    ppermute x6 -> x0, local copies, waits for them, and re-layouts: 11.7 us -> none  [move(): lax.ppermute(values, AXES, pairs)]
    pallas_call x55, Pallas kernels: 141 us -> 132 us  [call(): pl.pallas_call(kernel, grid=(steps,), out_shape=[jax.ShapeDtypeStruct(sha...]
  transfers between devices with their start and end apart: 66 -> 84, of which waited for: 32 -> 33; matrix products, arithmetic and copies ran while one was open for 3% -> 5% of each run, Pallas kernels for 17% -> 23%
where the time goes in v4:
time: 552 us; the launch traced here: 545 us
  waiting for transfers between devices  215 us (39%)
  Pallas kernels  132 us (24%)
  starting transfers between devices  111 us (20%)
  local copies, waits for them, and re-layouts  72.5 us (13%)
  other arithmetic  8.74 us (2%)
    ppermute x77, waiting for transfers between devices, move(): return lax.ppermute(values, AXES, pairs)  211 us
    pallas_call x55, Pallas kernels, call(): pl.pallas_call(kernel, grid=(steps,), out_shape=[jax.ShapeDtypeStruct(sha...  132 us
    ppermute x77, starting transfers between devices, move(): return lax.ppermute(values, AXES, pairs)  82.5 us
    unnamed x216, local copies, waits for them, and re-layouts  55.4 us
    all_to_all x7, starting transfers between devices, swap(): lax.all_to_all(view, AXES, 0, 0, axis_index_groups=groups, tiled=True)  28.6 us
  transfers between devices with their start and end apart: 84, of which 33 were waited for; matrix products, arithmetic and copies ran while one was open for 5% of the time, Pallas kernels for 23%

profile of v4, /device:TPU:0, one launch (start us, length us, event | category | flops | bytes accessed | tf_op | source)
XLA Modules:
  0.0 544.7 jit_solution(7877105968622801561)
XLA Ops:
  38.0 10.0 %collective-permute-done.8.refs_2_ = bf16[128,2048]{1,0:T(8,128)(2,1)S(1)} collective-permute-done((bf16[128,2048]{1,0:T(8,128)(2,1)S(1)}, bf16[128,2048]{1,0:T(8,128)(2,1)S(1)}, u32[]{:S(2)}, u32[]{:S(2)}) %collective-permute-start.8) | collective-permute-done | bytes 524320 | tf_op jit(solution)/shard_map/ppermute | solution.py:113
  59.0 7.8 %collective-permute-done.6 = bf16[8,448]{1,0:T(8,128)(2,1)S(1)} collective-permute-done((bf16[8,448]{1,0:T(8,128)(2,1)S(1)}, bf16[8,448]{1,0:T(8,128)(2,1)S(1)}, u32[]{:S(2)}, u32[]{:S(2)}) %collective-permute-start.6) | collective-permute-done | bytes 7200 | tf_op jit(solution)/shard_map/ppermute | solution.py:113
  77.2 16.5 %collective-permute-done.11 = bf16[2,8,448]{2,1,0:T(8,128)(2,1)} collective-permute-done((bf16[2,8,448]{2,1,0:T(8,128)(2,1)S(1)}, bf16[2,8,448]{2,1,0:T(8,128)(2,1)}, u32[]{:S(2)}, u32[]{:S(2)}) %collective-permute-start.11) | collective-permute-done | bytes 14368 | tf_op jit(solution)/shard_map/ppermute | solution.py:113
  122.2 8.4 %qkv.1 = (bf16[1024,2048]{1,0:T(8,128)(2,1)S(1)}, bf16[1024,768]{1,0:T(8,128)(2,1)S(1)}) custom-call(bf16[128,2048]{1,0:T(8,128)(2,1)S(1)} %order.4.refs_0_.inputs, bf16[128,2048]{1,0:T(8,128)(2,1)} %collective-permute-done.7.refs_1_, bf16[128,2048]{1,0:T(8,128)(2,1)S(1)} %copy-done.81, bf16[128,2048]{1,0:T(8,128)(2,1)S(1)} %copy-done.83, ...), custom_call_target="tpu_custom_call" | custom-call | tf_op jit(solution)/shard_map/qkv/pallas_call | solution.py:228
  138.5 9.2 %attend.1 = (bf16[1024,256]{1,0:T(8,128)(2,1)S(1)}, f32[16,256]{1,0:T(8,128)S(1)}) custom-call(bf16[1024,768]{1,0:T(8,128)(2,1)S(1)} %copy-done.34, f32[8,512]{1,0:T(8,128)S(1)} %copy-done.89, f32[512,128]{1,0:T(8,128)S(1)} %copy-done.43), custom_call_target="tpu_custom_call" | custom-call | tf_op jit(solution)/shard_map/attend/pallas_call | solution.py:228
  171.2 9.5 %collective-permute-done.23.refs_1_ = bf16[128,2048]{1,0:T(8,128)(2,1)S(1)} collective-permute-done((bf16[128,2048]{1,0:T(8,128)(2,1)S(1)}, bf16[128,2048]{1,0:T(8,128)(2,1)S(1)}, u32[]{:S(2)}, u32[]{:S(2)}) %collective-permute-start.23) | collective-permute-done | bytes 524320 | tf_op jit(solution)/shard_map/ppermute | solution.py:113
  191.3 9.7 %collective-permute-done.26.refs_13_.refs_5_ = bf16[512,640]{1,0:T(8,128)(2,1)S(1)} collective-permute-done((bf16[512,640]{1,0:T(8,128)(2,1)S(1)}, bf16[512,640]{1,0:T(8,128)(2,1)S(1)}, u32[]{:S(2)}, u32[]{:S(2)}) %collective-permute-start.26) | collective-permute-done | bytes 655392 | tf_op jit(solution)/shard_map/ppermute | solution.py:113
  201.0 5.2 collective-permute-done.28.refs_2_
  214.4 12.6 %collective-permute-done.33.refs_2_ = bf16[128,2048]{1,0:T(8,128)(2,1)S(1)} collective-permute-done((bf16[128,2048]{1,0:T(8,128)(2,1)S(1)}, bf16[128,2048]{1,0:T(8,128)(2,1)S(1)}, u32[]{:S(2)}, u32[]{:S(2)}) %collective-permute-start.33) | collective-permute-done | bytes 524320 | tf_op jit(solution)/shard_map/ppermute | solution.py:113
  230.0 10.5 %collective-permute-done.31.refs_15_.refs_7_ = bf16[512,640]{1,0:T(8,128)(2,1)S(1)} collective-permute-done((bf16[512,640]{1,0:T(8,128)(2,1)}, bf16[512,640]{1,0:T(8,128)(2,1)S(1)}, u32[]{:S(2)}, u32[]{:S(2)}) %collective-permute-start.31) | collective-permute-done | bytes 655392 | tf_op jit(solution)/shard_map/ppermute | solution.py:113
  240.5 5.6 %collective-permute-done.29.refs_2_ = bf16[512,768]{1,0:T(8,128)(2,1)S(1)} collective-permute-done((bf16[512,768]{1,0:T(8,128)(2,1)S(1)}, bf16[512,768]{1,0:T(8,128)(2,1)S(1)}, u32[]{:S(2)}, u32[]{:S(2)}) %collective-permute-start.29) | collective-permute-done | bytes 786464 | tf_op jit(solution)/shard_map/ppermute | solution.py:113
  249.8 10.4 %mlp.1 = (bf16[1024,2048]{1,0:T(8,128)(2,1)S(1)}, bf16[1024,768]{1,0:T(8,128)(2,1)S(1)}, f32[1024,704]{1,0:T(8,128)S(1)}, f32[1024,704]{1,0:T(8,128)S(1)}) custom-call(bf16[128,2048]{1,0:T(8,128)(2,1)S(1)} %get-tuple-element.751.refs_0_, bf16[128,2048]{1,0:T(8,128)(2,1)S(1)} %collective-permute-done.32.refs_1_, ...), custom_call_target="tpu_custom_call" | custom-call | tf_op jit(solution)/shard_map/mlp/pallas_call | solution.py:228
  269.7 5.2 expand.7
  274.9 5.2 expand.8.own
  291.7 10.7 %collective-permute-done.44.refs_1_ = bf16[128,2048]{1,0:T(8,128)(2,1)S(1)} collective-permute-done((bf16[128,2048]{1,0:T(8,128)(2,1)S(1)}, bf16[128,2048]{1,0:T(8,128)(2,1)S(1)}, u32[]{:S(2)}, u32[]{:S(2)}) %collective-permute-start.44) | collective-permute-done | bytes 524320 | tf_op jit(solution)/shard_map/ppermute | solution.py:113
  313.7 8.1 %collective-permute-done.45.refs_2_ = bf16[512,640]{1,0:T(8,128)(2,1)S(1)} collective-permute-done((bf16[512,640]{1,0:T(8,128)(2,1)S(1)}, bf16[512,640]{1,0:T(8,128)(2,1)S(1)}, u32[]{:S(2)}, u32[]{:S(2)}) %collective-permute-start.45) | collective-permute-done | bytes 655392 | tf_op jit(solution)/shard_map/ppermute | solution.py:113
  325.4 7.1 %collective-permute-done.47.refs_2_ = bf16[128,2048]{1,0:T(8,128)(2,1)S(1)} collective-permute-done((bf16[128,2048]{1,0:T(8,128)(2,1)S(1)}, bf16[128,2048]{1,0:T(8,128)(2,1)S(1)}, u32[]{:S(2)}, u32[]{:S(2)}) %collective-permute-start.47) | collective-permute-done | bytes 524320 | tf_op jit(solution)/shard_map/ppermute | solution.py:113
  340.6 13.1 %collective-permute-done.52.refs_2_ = bf16[128,2048]{1,0:T(8,128)(2,1)S(1)} collective-permute-done((bf16[128,2048]{1,0:T(8,128)(2,1)S(1)}, bf16[128,2048]{1,0:T(8,128)(2,1)S(1)}, u32[]{:S(2)}, u32[]{:S(2)}) %collective-permute-start.52) | collective-permute-done | bytes 524320 | tf_op jit(solution)/shard_map/ppermute | solution.py:113
  353.7 11.9 %collective-permute-done.49.refs_4_ = bf16[512,640]{1,0:T(8,128)(2,1)S(1)} collective-permute-done((bf16[512,640]{1,0:T(8,128)(2,1)S(1)}, bf16[512,640]{1,0:T(8,128)(2,1)S(1)}, u32[]{:S(2)}, u32[]{:S(2)}) %collective-permute-start.49) | collective-permute-done | bytes 655392 | tf_op jit(solution)/shard_map/ppermute | solution.py:113
  396.8 9.4 %attend_back.1 = (bf16[1024,768]{1,0:T(8,128)(2,1)S(1)}, f32[1,768]{1,0:T(1,128)S(1)}) custom-call(bf16[1024,256]{1,0:T(8,128)(2,1)S(1)} %copy-done.65, bf16[1024,768]{1,0:T(8,128)(2,1)S(1)} %copy-done.35, f32[16,256]{1,0:T(8,128)S(1)} %copy-done.93, f32[1024,384]{1,0:T(8,128)S(1)} %copy-done.6, f32[8,512]{1,0:T(8,128)S(1)} %copy.99.row, ...), custom_call_target="tpu_custom_call" | custom-call | tf_op jit(solution)/shard_map/attend_back/pallas_call | solution.py:228
  438.2 12.0 %collective-permute-done.65.refs_1_ = bf16[128,2048]{1,0:T(8,128)(2,1)S(1)} collective-permute-done((bf16[128,2048]{1,0:T(8,128)(2,1)}, bf16[128,2048]{1,0:T(8,128)(2,1)S(1)}, u32[]{:S(2)}, u32[]{:S(2)}) %collective-permute-start.65) | collective-permute-done | bytes 524320 | tf_op jit(solution)/shard_map/ppermute | solution.py:113
  459.4 8.6 %collective-permute-done.64.refs_5_ = bf16[512,256]{1,0:T(8,128)(2,1)S(1)} collective-permute-done((bf16[512,256]{1,0:T(8,128)(2,1)S(1)}, bf16[512,256]{1,0:T(8,128)(2,1)S(1)}, u32[]{:S(2)}, u32[]{:S(2)}) %collective-permute-start.64) | collective-permute-done | bytes 262176 | tf_op jit(solution)/shard_map/ppermute | solution.py:113
  477.4 8.0 %collective-permute-done.69.refs_1_ = bf16[128,2048]{1,0:T(8,128)(2,1)S(1)} collective-permute-done((bf16[128,2048]{1,0:T(8,128)(2,1)}, bf16[128,2048]{1,0:T(8,128)(2,1)S(1)}, u32[]{:S(2)}, u32[]{:S(2)}) %collective-permute-start.69) | collective-permute-done | bytes 524320 | tf_op jit(solution)/shard_map/ppermute | solution.py:113
  495.6 12.1 %collective-permute-done.70.refs_2_ = bf16[512,768]{1,0:T(8,128)(2,1)} collective-permute-done((bf16[512,768]{1,0:T(8,128)(2,1)S(1)}, bf16[512,768]{1,0:T(8,128)(2,1)}, u32[]{:S(2)}, u32[]{:S(2)}) %collective-permute-start.70) | collective-permute-done | bytes 786464 | tf_op jit(solution)/shard_map/ppermute | solution.py:113
  (507 shorter events, 315.3 us)
Async XLA Ops:
  28.7 38.1 %collective-permute-start.4 = (bf16[512,768]{1,0:T(8,128)(2,1)S(1)}, bf16[512,768]{1,0:T(8,128)(2,1)S(1)}, u32[]{:S(2)}, u32[]{:S(2)}) collective-permute-start(bf16[512,768]{1,0:T(8,128)(2,1)S(1)} %get-tuple-element.1072.refs_8_.refs_0_), channel_id=1, source_target_pairs={{0,4},{1,5},{2,6},{3,7},{4,0},{5,1},{6,2},{7,3},{8,12},{9,13},{10,... | collective-permute-start | bytes 2359304 | tf_op jit(solution)/shard_map/ppermute | solution.py:113
  30.2 37.5 %collective-permute-start.3 = (bf16[512,768]{1,0:T(8,128)(2,1)S(1)}, bf16[512,768]{1,0:T(8,128)(2,1)S(1)}, u32[]{:S(2)}, u32[]{:S(2)}) collective-permute-start(bf16[512,768]{1,0:T(8,128)(2,1)S(1)} %get-tuple-element.1072.refs_8_.refs_0_), channel_id=1, source_target_pairs={{16,0},{17,1},{18,2},{19,3},{20,4},{21,5},{22,6},{23,7},{24,8},{25... | collective-permute-start | bytes 2359304 | tf_op jit(solution)/shard_map/ppermute | solution.py:113
  69.5 37.4 %all-to-all-start.1 = ((bf16[8,64,2176]{2,1,0:T(8,128)(2,1)}), bf16[8,64,2176]{2,1,0:T(8,128)(2,1)S(1)}, u32[]{:S(2)}, u32[]{:S(2)}) async-start(bf16[8,64,2176]{2,1,0:T(8,128)(2,1)} %bitcast.88), calls=%async_computation.1 | async-start | bytes 4456448 | tf_op jit(solution)/shard_map/all_to_all | solution.py:135
  73.2 33.7 %collective-permute-start.13 = (bf16[512,768]{1,0:T(8,128)(2,1)}, bf16[512,768]{1,0:T(8,128)(2,1)S(1)}, u32[]{:S(2)}, u32[]{:S(2)}) collective-permute-start(bf16[512,768]{1,0:T(8,128)(2,1)} %copy-done.23), channel_id=1, source_target_pairs={{0,4},{1,5},{2,6},{3,7},{4,0},{5,1},{6,2},{7,3},{8,12},{9,13},{10,... | collective-permute-start | bytes 2359304 | tf_op jit(solution)/shard_map/ppermute | solution.py:113
  107.8 47.4 %all-to-all-start.2 = ((bf16[4,128,2048]{2,1,0:T(8,128)(2,1)}), bf16[4,128,2048]{2,1,0:T(8,128)(2,1)}, u32[]{:S(2)}, u32[]{:S(2)}) async-start(bf16[4,128,2048]{2,1,0:T(8,128)(2,1)} %bitcast.92), calls=%async_computation.2 | async-start | bytes 4194304 | tf_op jit(solution)/shard_map/all_to_all | solution.py:135
  112.5 41.4 %collective-permute-start.20 = (bf16[512,768]{1,0:T(8,128)(2,1)S(1)}, bf16[512,768]{1,0:T(8,128)(2,1)}, u32[]{:S(2)}, u32[]{:S(2)}) collective-permute-start(bf16[512,768]{1,0:T(8,128)(2,1)S(1)} %split.4.refs_8_.refs_0_), channel_id=1, source_target_pairs={{0,4},{1,5},{2,6},{3,7},{4,0},{5,1},{6,2},{7,3},{8,12},{9,13},{10,... | collective-permute-start | bytes 2359304 | tf_op jit(solution)/shard_map/ppermute | solution.py:113
  113.1 40.8 %collective-permute-start.19 = (bf16[512,768]{1,0:T(8,128)(2,1)S(1)}, bf16[512,768]{1,0:T(8,128)(2,1)}, u32[]{:S(2)}, u32[]{:S(2)}) collective-permute-start(bf16[512,768]{1,0:T(8,128)(2,1)S(1)} %split.4.refs_8_.refs_0_), channel_id=1, source_target_pairs={{16,0},{17,1},{18,2},{19,3},{20,4},{21,5},{22,6},{23,7},{24,8},{25... | collective-permute-start | bytes 2359304 | tf_op jit(solution)/shard_map/ppermute | solution.py:113
  114.7 33.6 %collective-permute-start.17 = (bf16[512,256]{1,0:T(8,128)(2,1)}, bf16[512,256]{1,0:T(8,128)(2,1)}, u32[]{:S(2)}, u32[]{:S(2)}) collective-permute-start(bf16[512,256]{1,0:T(8,128)(2,1)} %get-tuple-element.1009.refs_0_.refs_8_), channel_id=1, source_target_pairs={{0,4},{1,5},{2,6},{3,7},{4,0},{5,1},{6,2},{7,3},{8,12},{9,13},{10,... | collective-permute-start | bytes 786440 | tf_op jit(solution)/shard_map/ppermute | solution.py:113
  116.2 32.1 %collective-permute-start.18 = (bf16[512,256]{1,0:T(8,128)(2,1)}, bf16[512,256]{1,0:T(8,128)(2,1)}, u32[]{:S(2)}, u32[]{:S(2)}) collective-permute-start(bf16[512,256]{1,0:T(8,128)(2,1)} %collective-permute-done.12.refs_2_.refs_10_), channel_id=1, source_target_pairs={{0,4},{1,5},{2,6},{3,7},{4,0},{5,1},{6,2},{7,3},{8,12},{9,13},{10,... | collective-permute-start | bytes 786440 | tf_op jit(solution)/shard_map/ppermute | solution.py:113
  167.4 33.6 %collective-permute-start.24 = (bf16[512,768]{1,0:T(8,128)(2,1)}, bf16[512,768]{1,0:T(8,128)(2,1)S(1)}, u32[]{:S(2)}, u32[]{:S(2)}) collective-permute-start(bf16[512,768]{1,0:T(8,128)(2,1)} %collective-permute-done.19.refs_10_.refs_2_), channel_id=1, source_target_pairs={{0,4},{1,5},{2,6},{3,7},{4,0},{5,1},{6,2},{7,3},{8,12},{9,13},{10,... | collective-permute-start | bytes 2359304 | tf_op jit(solution)/shard_map/ppermute | solution.py:113
  168.4 32.6 %collective-permute-start.26 = (bf16[512,640]{1,0:T(8,128)(2,1)S(1)}, bf16[512,640]{1,0:T(8,128)(2,1)S(1)}, u32[]{:S(2)}, u32[]{:S(2)}) collective-permute-start(bf16[512,640]{1,0:T(8,128)(2,1)S(1)} %copy-done.39), channel_id=1, source_target_pairs={{0,4},{1,5},{2,6},{3,7},{4,0},{5,1},{6,2},{7,3},{8,12},{9,13},{10,... | collective-permute-start | bytes 1966088 | tf_op jit(solution)/shard_map/ppermute | solution.py:113
  210.5 35.6 %collective-permute-start.29 = (bf16[512,768]{1,0:T(8,128)(2,1)S(1)}, bf16[512,768]{1,0:T(8,128)(2,1)S(1)}, u32[]{:S(2)}, u32[]{:S(2)}) collective-permute-start(bf16[512,768]{1,0:T(8,128)(2,1)S(1)} %copy-done.15), channel_id=1, source_target_pairs={{16,0},{17,1},{18,2},{19,3},{20,4},{21,5},{22,6},{23,7},{24,8},{25... | collective-permute-start | bytes 2359304 | tf_op jit(solution)/shard_map/ppermute | solution.py:113
  288.0 37.4 %collective-permute-start.42 = (bf16[512,768]{1,0:T(8,128)(2,1)S(1)}, bf16[512,768]{1,0:T(8,128)(2,1)S(1)}, u32[]{:S(2)}, u32[]{:S(2)}) collective-permute-start(bf16[512,768]{1,0:T(8,128)(2,1)S(1)} %grad.17), channel_id=1, source_target_pairs={{0,16},{1,17},{2,18},{3,19},{4,20},{5,21},{6,22},{7,23},{8,24},{9,... | collective-permute-start | bytes 2359304 | tf_op jit(solution)/shard_map/ppermute | solution.py:113
  288.0 37.4 %collective-permute-start.43 = (bf16[512,768]{1,0:T(8,128)(2,1)S(1)}, bf16[512,768]{1,0:T(8,128)(2,1)S(1)}, u32[]{:S(2)}, u32[]{:S(2)}) collective-permute-start(bf16[512,768]{1,0:T(8,128)(2,1)S(1)} %get-tuple-element.879), channel_id=1, source_target_pairs={{0,4},{1,5},{2,6},{3,7},{4,0},{5,1},{6,2},{7,3},{8,12},{9,13},{10,... | collective-permute-start | bytes 2359304 | tf_op jit(solution)/shard_map/ppermute | solution.py:113
  289.7 32.1 %collective-permute-start.45 = (bf16[512,640]{1,0:T(8,128)(2,1)S(1)}, bf16[512,640]{1,0:T(8,128)(2,1)S(1)}, u32[]{:S(2)}, u32[]{:S(2)}) collective-permute-start(bf16[512,640]{1,0:T(8,128)(2,1)S(1)} %get-tuple-element.881), channel_id=1, source_target_pairs={{0,4},{1,5},{2,6},{3,7},{4,0},{5,1},{6,2},{7,3},{8,12},{9,13},{10,... | collective-permute-start | bytes 1966088 | tf_op jit(solution)/shard_map/ppermute | solution.py:113
  334.0 32.9 %collective-permute-start.50 = (bf16[512,768]{1,0:T(8,128)(2,1)S(1)}, bf16[512,768]{1,0:T(8,128)(2,1)S(1)}, u32[]{:S(2)}, u32[]{:S(2)}) collective-permute-start(bf16[512,768]{1,0:T(8,128)(2,1)S(1)} %get-tuple-element.948), channel_id=1, source_target_pairs={{0,4},{1,5},{2,6},{3,7},{4,0},{5,1},{6,2},{7,3},{8,12},{9,13},{10,... | collective-permute-start | bytes 2359304 | tf_op jit(solution)/shard_map/ppermute | solution.py:113
  376.1 42.6 %all-to-all-start.3 = ((bf16[8,64,1408]{2,1,0:T(8,128)(2,1)}), bf16[8,64,1408]{2,1,0:T(8,128)(2,1)}, u32[]{:S(2)}, u32[]{:S(2)}) async-start(bf16[8,64,1408]{2,1,0:T(8,128)(2,1)} %bitcast.33), calls=%async_computation.3 | async-start | bytes 2883584 | tf_op jit(solution)/shard_map/all_to_all | solution.py:135
  380.5 38.1 %collective-permute-start.61 = (bf16[512,768]{1,0:T(8,128)(2,1)}, bf16[512,768]{1,0:T(8,128)(2,1)}, u32[]{:S(2)}, u32[]{:S(2)}) collective-permute-start(bf16[512,768]{1,0:T(8,128)(2,1)} %grad.23), channel_id=1, source_target_pairs={{0,16},{1,17},{2,18},{3,19},{4,20},{5,21},{6,22},{7,23},{8,24},{9,... | collective-permute-start | bytes 2359304 | tf_op jit(solution)/shard_map/ppermute | solution.py:113
  382.1 36.5 %collective-permute-start.62 = (bf16[512,768]{1,0:T(8,128)(2,1)}, bf16[512,768]{1,0:T(8,128)(2,1)}, u32[]{:S(2)}, u32[]{:S(2)}) collective-permute-start(bf16[512,768]{1,0:T(8,128)(2,1)} %copy-done.96), channel_id=1, source_target_pairs={{0,4},{1,5},{2,6},{3,7},{4,0},{5,1},{6,2},{7,3},{8,12},{9,13},{10,... | collective-permute-start | bytes 2359304 | tf_op jit(solution)/shard_map/ppermute | solution.py:113
  418.6 34.6 %collective-permute-start.63 = (bf16[512,2048]{1,0:T(8,128)(2,1)}, bf16[512,2048]{1,0:T(8,128)(2,1)}, u32[]{:S(2)}, u32[]{:S(2)}) collective-permute-start(bf16[512,2048]{1,0:T(8,128)(2,1)} %copy-done.47), channel_id=1, source_target_pairs={{0,1},{1,0},{2,3},{3,2},{4,5},{5,4},{6,7},{7,6},{8,9},{9,8},{10,11... | collective-permute-start | bytes 6291464 | tf_op jit(solution)/shard_map/ppermute | solution.py:113
  422.5 47.8 %all-to-all-start.4 = ((bf16[8,64,768]{2,1,0:T(8,128)(2,1)}), bf16[8,64,768]{2,1,0:T(8,128)(2,1)}, u32[]{:S(2)}, u32[]{:S(2)}) async-start(bf16[8,64,768]{2,1,0:T(8,128)(2,1)} %bitcast.91), calls=%async_computation.4 | async-start | bytes 1572864 | tf_op jit(solution)/shard_map/all_to_all | solution.py:135
  430.6 38.1 %collective-permute-start.67 = (bf16[128,2048]{1,0:T(8,128)(2,1)}, bf16[128,2048]{1,0:T(8,128)(2,1)S(1)}, u32[]{:S(2)}, u32[]{:S(2)}) collective-permute-start(bf16[128,2048]{1,0:T(8,128)(2,1)} %get-tuple-element.1084), channel_id=1, source_target_pairs={{0,2},{1,3},{2,0},{3,1},{4,6},{5,7},{6,4},{7,5},{8,10},{9,11},{10,... | collective-permute-start | bytes 1572872 | tf_op jit(solution)/shard_map/ppermute | solution.py:113
  471.1 36.6 %collective-permute-start.70 = (bf16[512,768]{1,0:T(8,128)(2,1)S(1)}, bf16[512,768]{1,0:T(8,128)(2,1)}, u32[]{:S(2)}, u32[]{:S(2)}) collective-permute-start(bf16[512,768]{1,0:T(8,128)(2,1)S(1)} %grad.29), channel_id=1, source_target_pairs={{0,16},{1,17},{2,18},{3,19},{4,20},{5,21},{6,22},{7,23},{8,24},{9,... | collective-permute-start | bytes 2359304 | tf_op jit(solution)/shard_map/ppermute | solution.py:113
  474.5 33.2 %collective-permute-start.71 = (bf16[512,768]{1,0:T(8,128)(2,1)}, bf16[512,768]{1,0:T(8,128)(2,1)}, u32[]{:S(2)}, u32[]{:S(2)}) collective-permute-start(bf16[512,768]{1,0:T(8,128)(2,1)} %copy-done.95), channel_id=1, source_target_pairs={{0,4},{1,5},{2,6},{3,7},{4,0},{5,1},{6,2},{7,3},{8,12},{9,13},{10,... | collective-permute-start | bytes 2359304 | tf_op jit(solution)/shard_map/ppermute | solution.py:113
  (166 other events, 1832.5 us)

commit v5 on v4

--- a/solution.py
+++ b/solution.py
@@ -284,20 +284,6 @@
             out[rows:, :] = pieces[2 * i + 1][...]
 
 
-def qkv_kernel(count, *refs):
-    pieces, blocks = refs[:8], refs[8:-7]
-    gain, shift, bias, table, normed, mixed, tile = refs[-7:]
-    gathered(pieces, tile)
-    centered, scale = centered_of(tile[...].astype(F32))
-    normed[...] = (centered * scale * gain[...] + shift[...]).astype(BF16)
-    turning = mixed.shape[1] * 2 // 3
-    values = product(normed, in_chunks(blocks, count)) + bias[...]
-    both = turned(values[:, :turning], table[...], 1.0).astype(BF16)
-    mixed[:, : turning // 2] = both[:, : turning // 2] * 0.125
-    mixed[:, turning // 2 : turning] = both[:, turning // 2 :]
-    mixed[:, turning:] = values[:, turning:].astype(BF16)
-
-
 def attended_grad_kernel(count, *refs):
     pieces, blocks = refs[:8], refs[8:-2]
     whole, grads = refs[-2:]
@@ -328,12 +314,30 @@
     return jnp.where(allowed, dot_cols(key, query), -1e30)
 
 
-def attend_kernel(mixed, row, col, attended, sums):
+def attention_kernel(count, *refs):
+    pieces, blocks = refs[:8], refs[8:-12]
+    gain, shift, bias, table, row, col, normed, mixed, attended, sums, tile, low = refs[-12:]
+    tiles = pl.num_programs(0) // 2
     half = mixed.shape[0] // 2
     heads = attended.shape[1] // HEAD_DIM
-
-    @pl.loop(0, 4)
-    def _(i):
+    gathered(pieces, tile)
+
+    @pl.when(pl.program_id(0) < tiles)
+    def _():
+        centered, scale = centered_of(tile[...].astype(F32))
+        low[...] = (centered * scale * gain[...] + shift[...]).astype(BF16)
+        normed[...] = low[...]
+        turning = mixed.shape[1] * 2 // 3
+        values = product(low, in_chunks(blocks, count)) + bias[...]
+        both = turned(values[:, :turning], table[...], 1.0).astype(BF16)
+        span = tile_of(pl.program_id(0))
+        mixed[span, : turning // 2] = both[:, : turning // 2] * 0.125
+        mixed[span, turning // 2 : turning] = both[:, turning // 2 :]
+        mixed[span, turning:] = values[:, turning:].astype(BF16)
+
+    @pl.when(pl.program_id(0) >= tiles)
+    def _():
+        i = pl.program_id(0) - tiles
         sequence, turn = i // 2, i % 2
         allowed = allowed_at(row, col, sequence, turn)
         start = turn * half + sequence * TILE
@@ -587,7 +591,7 @@
                 col += size
 
 
-def grad_blocks(at, ways, spots, kind, addends=()):
+def grad_blocks(at, ways, spots, kind, addends=(), stacked=False):
     tokens, wide = ways[0][0].shape
     width = wide // (2 * at.outer)
     tile = min(TILE, width)
@@ -606,9 +610,22 @@
     tiles = {2 * i: pl.BlockSpec((tokens, tile), lambda i: (0, column(i))) for i in range(len(ways))}
     for k in range(len(addends)):
         tiles[2 * len(ways) + k] = rows_of(shape, tile, row_of(k))
+    kernel = functools.partial(grad_kernel, len(addends), tuple(way[2:] for way in ways))
+    if stacked:
+        shape = (width * len(spots), shape[1])
+        return call(
+            at,
+            kernel,
+            [(shape, kind)],
+            *[v for way in ways for v in way[:2]],
+            steps=len(spots) * each,
+            tiles=tiles,
+            out_tiles={0: rows_of(shape, tile)},
+            name="grad",
+        )[0]
     return call(
         at,
-        functools.partial(grad_kernel, len(addends), tuple(way[2:] for way in ways)),
+        kernel,
         [(shape, kind)] * len(spots),
         *[v for way in ways for v in way[:2]],
         *addends,
@@ -619,9 +636,9 @@
     )
 
 
-def grad_beside(at, *way):
+def grad_beside(at, *way, stacked=False):
     order = list(range(1, at.outer)) + [0]
-    return grad_blocks(at, way, [2 * i + 1 for i in order], BF16)
+    return grad_blocks(at, way, [2 * i + 1 for i in order], BF16, stacked=stacked)
 
 
 def grad_own(at, *way):
@@ -653,19 +670,16 @@
     )
 
 
-def join_kernel(place, near, far, out):
-    rows = near.shape[0] // 4
-    for half, ref in enumerate((near, far)):
-        for d in range(4):
-            start = pl.multiple_of((place[0] ^ d) * rows, rows)
-            low = (half * 4 + d) * rows
-            out[low : low + rows, :] = ref[pl.ds(start, rows), :]
-
-
-def joined_rows(at, near, far):
-    place = jnp.reshape(at.b * 2 + at.x, (1,)).astype(jnp.int32)
-    shape = (2 * near.shape[0], near.shape[1])
-    (out,) = call(at, join_kernel, [(shape, BF16)], place, near, far, name="join")
+def join_kernel(*refs):
+    *pieces, out = refs
+    rows = pieces[0].shape[0]
+    for i, piece in enumerate(pieces):
+        out[i * rows : (i + 1) * rows, :] = piece[...]
+
+
+def joined_rows(at, pieces):
+    shape = (8 * pieces[0].shape[0], pieces[0].shape[1])
+    (out,) = call(at, join_kernel, [(shape, BF16)], *pieces, name="join")
     return out
 
 
@@ -821,13 +835,19 @@
     padded = (units + 127) // 128 * 128
     thin, wide = (tokens, units), (tokens, 2 * units)
 
+    (v.cotangent,) = to_relative(at, cotangent, [1])
+    v.cotangent_near = [at.flip(v.cotangent, x=1), at.flip(v.cotangent, b=1)]
     v.front = at.swap(cut_rows(at, [qkv_weight, out_weight], (3, 1), 4 * part), at.groups)
     v.small = jnp.concatenate([at.after(qkv_bias), ln1_gain, ln1_bias, ln2_gain, ln2_bias])[None]
     v.small = joined(at.c, v.small, at.flip(v.small, c=1), 0)
     v.small = joined(at.x, v.small, at.flip(v.small, x=1), 0)
     (v.inputs,) = to_relative(at, layer_input, [1])
-    v.later = cut_rows(at, [gate_weight, up_weight, down_weight], (1, 1, 1), 2 * units + padded)
-    v.cotangent, v.cotangent_four = to_relative(at, cotangent, [1, 4])
+    v.first, v.later = split(
+        at,
+        cut_rows(at, [gate_weight, up_weight, down_weight], (1, 1, 1), 2 * units + padded),
+        0,
+        (first, second + padded),
+    )
     spots = jnp.concatenate([segment_ids, positions[None]], axis=0)[None]
     v.spots = jnp.concatenate([spots, at.flip(spots, b=1)], axis=0)
     v.close(at)
@@ -853,7 +873,7 @@
     v.qkv_beside += flip_all(at, v.qkv_across[1:])
     v.turned = [at.flip(v.tokens[0], c=1), *v.turned] + [at.flip(t, c=1) for t in v.tokens[2:]]
     v.out_across = cross_block(at, v.out)
-    v.later = at.swap(v.later, at.groups)
+    v.first = at.swap(v.first, at.groups)
 
     v.small = jnp.stack([v.small, at.flip(v.small, e=1)], axis=1)
 
@@ -872,15 +892,21 @@
     v.qkv_blocks = [merge_blocks(v.qkv_across, v.qkv_beside)]
     del v.qkv_across, v.qkv_beside, v.qkv, v.small, v.spots
 
-    (v.first,) = split(at, v.later, 0, (first,))
     v.first_across = cross_block(at, v.first)
     v.first_beside = [at.flip(v.first, e=1)]
     v.out_beside = flip_all(at, v.out_across)
-    v.cotangent_near = at.swap(v.cotangent_four, at.sides)
-    v.normed, v.mixed = call(
-        at,
-        functools.partial(qkv_kernel, count),
-        [((tokens, width), BF16), ((tokens, 3 * part), BF16)],
+    v.cotangent_near.append(at.flip(v.cotangent_near[1], x=1))
+    v.later = at.swap(v.later, at.groups)
+    steps = tokens // TILE
+    v.normed, v.mixed, v.attended, v.sums = call(
+        at,
+        functools.partial(attention_kernel, count),
+        [
+            ((tokens, width), BF16),
+            ((tokens, 3 * part), BF16),
+            ((tokens, part), BF16),
+            ((4 * heads_here, TILE), F32),
+        ],
         *v.tokens,
         *v.turned,
         *v.qkv_blocks[0],
@@ -888,35 +914,28 @@
         v.gains[1],
         v.bias,
         v.table,
-        steps=tokens // TILE,
-        tiles={11 + count: rows_of(v.table.shape, TILE)},
-        out_tiles={0: rows_of((tokens, width), TILE), 1: rows_of((tokens, 3 * part), TILE)},
-        scratch=[pltpu.VMEM((TILE, width), BF16)],
-        name="qkv",
-    )
-    v.attended, v.sums = call(
-        at,
-        attend_kernel,
-        [((tokens, part), BF16), ((4 * heads_here, TILE), F32)],
-        v.mixed,
         v.row,
         v.col,
-        name="attend",
+        steps=2 * steps,
+        tiles={11 + count: rows_of(v.table.shape, TILE, lambda i: jnp.minimum(i, steps - 1))},
+        out_tiles={0: rows_of((tokens, width), TILE, lambda i: jnp.minimum(i, steps - 1))},
+        scratch=[pltpu.VMEM((TILE, width), BF16)] * 2,
+        name="attention",
     )
     v.out_blocks = [merge_blocks(v.out_across, v.out_beside)]
     v.other = expand(at, v.attended, v.out_blocks, 1, BF16)
-    v.second, v.down = split(at, v.later, first, (second, padded))
+    v.close(at)
+    del v.out_across, v.out_beside, v.out
+
+    v.other = at.flip(v.other, c=1)
+    v.cotangent_far = [at.flip(t, c=1) for t in (v.cotangent, *v.cotangent_near)]
+    v.second, v.down = split(at, v.later, 0, (second, padded))
+    v.pieces = expand_pieces(at, v.attended, v.out_blocks, v.other)
     v.close(at)
     del v.later
-    del v.out_across, v.out_beside, v.out, v.cotangent_four
-
-    v.other = at.flip(v.other, c=1)
-    v.cotangent_far = at.flip(v.cotangent_near, c=1)
-    v.pieces = expand_pieces(at, v.attended, v.out_blocks, v.other)
-    v.close(at)
 
     v.terms = pass_pieces(at, send_pieces(at, v.pieces))
-    v.cotangent_all = joined_rows(at, v.cotangent_near, v.cotangent_far)
+    v.cotangent_all = joined_rows(at, [v.cotangent, *v.cotangent_near, *v.cotangent_far])
     v.second_across = cross_block(at, v.second)
     v.second_beside = [at.flip(v.second, e=1)]
     v.first_beside += flip_all(at, v.first_across[1:])
@@ -1041,6 +1060,7 @@
     v.early = at.swap(v.early, at.groups)
     v.second_far = push_all(at, v.second_cross)
     v.second_sent += flip_all(at, v.second_made[-1:])
+    v.result_pieces = send_pieces(at, v.pieces)
     v.branch, v.attended_grad = call(
         at,
         functools.partial(attended_grad_kernel, count),
@@ -1052,7 +1072,7 @@
         out_tiles={0: rows_of((tokens, width), TILE), 1: rows_of((tokens, part), TILE)},
         name="attended_grad",
     )
-    v.out_sent = flip_all(at, grad_beside(at, (v.branch, v.attended, 0, part)))
+    v.out_sent = at.flip(grad_beside(at, (v.branch, v.attended, 0, part), stacked=True), e=1)
     v.mixed_low, v.bias_part = call(
         at,
         attend_back_kernel,
@@ -1072,13 +1092,13 @@
     del v.tokens, v.turned, v.second_made, v.second_cross, v.attended_grad
 
     v.late = at.swap(add(at, [v.second_own, v.second_sent[-1], *v.second_far]), at.groups)
-    v.out_far = push_all(at, grad_across(at, v.out_sent, (v.branch, v.attended, 0, part)))
     v.other = at.flip(v.other, c=1)
     v.qkv_sent = flip_all(at, v.qkv_made[:-1])
-    result_pieces = send_pieces(at, v.pieces)
+    v.result_terms = pass_pieces(at, v.result_pieces)
+    v.out_sent = jnp.split(v.out_sent, at.outer)
+    v.out_far = push_all(at, grad_across(at, v.out_sent, (v.branch, v.attended, 0, part)))
     v.qkv_own = grad_own(at, (v.normed, v.mixed_low, 0, 3 * part))
     v.out_own = grad_own(at, (v.branch, v.attended, 0, part))
-    v.result_terms = pass_pieces(at, result_pieces)
     v.pieces = expand_pieces(at, v.mixed_low, v.qkv_blocks, v.other)
     v.qkv_cross = grad_across(at, v.qkv_sent, (v.normed, v.mixed_low, 0, 3 * part))
     v.close(at)

time: 552 us -> 529 us (0.958)
  local copies, waits for them, and re-layouts: 72.5 us -> 56.1 us
    convert_element_type x8, local copies, waits for them, and re-layouts: 7.62 us -> 0.34 us  [vector(): return v.small[..., start:start + rows].reshape(1, width).astype(F32)]
    unnamed x216 -> x184, local copies, waits for them, and re-layouts: 55.4 us -> 49.4 us
    ppermute x77 -> x82, waiting for transfers between devices: 211 us -> 208 us  [move(): return lax.ppermute(values, AXES, pairs)]
    pallas_call x55 -> x54, Pallas kernels: 132 us -> 135 us  [call(): pl.pallas_call(kernel, grid=(steps,), out_shape=[jax.ShapeDtypeStruct(sha...]
    ppermute x77 -> x82, starting transfers between devices: 82.5 us -> 83.8 us  [move(): return lax.ppermute(values, AXES, pairs)]
  transfers between devices with their start and end apart: 84 -> 89, of which waited for: 33 -> 35; matrix products, arithmetic and copies ran while one was open for 5% -> 2% of each run, Pallas kernels for 23% -> 25%
where the time goes in v5:
time: 529 us; the launch traced here: 523 us
  waiting for transfers between devices  211 us (40%)
  Pallas kernels  135 us (26%)
  starting transfers between devices  112 us (21%)
  local copies, waits for them, and re-layouts  56.1 us (11%)
    ppermute x82, waiting for transfers between devices, move(): return lax.ppermute(values, AXES, pairs)  208 us
    pallas_call x54, Pallas kernels, call(): pl.pallas_call(kernel, grid=(steps,), out_shape=[jax.ShapeDtypeStruct(sha...  135 us
    ppermute x82, starting transfers between devices, move(): return lax.ppermute(values, AXES, pairs)  83.8 us
    unnamed x184, local copies, waits for them, and re-layouts  49.4 us
    all_to_all x7, starting transfers between devices, swap(): lax.all_to_all(view, AXES, 0, 0, axis_index_groups=groups, tiled=True)  28.2 us
  transfers between devices with their start and end apart: 89, of which 35 were waited for; matrix products, arithmetic and copies ran while one was open for 2% of the time, Pallas kernels for 25%

profile of v5, /device:TPU:0, one launch (start us, length us, event | category | flops | bytes accessed | tf_op | source)
XLA Modules:
  0.0 522.8 jit_solution(15418811619711362350)
XLA Ops:
  24.0 6.3 %collective-permute-done.3 = bf16[2,448]{1,0:T(2,128)(2,1)S(1)} collective-permute-done((bf16[2,448]{1,0:T(2,128)(2,1)S(1)}, bf16[2,448]{1,0:T(2,128)(2,1)S(1)}, u32[]{:S(2)}, u32[]{:S(2)}) %collective-permute-start.3) | collective-permute-done | bytes 1824 | tf_op jit(solution)/shard_map/ppermute | solution.py:113
  41.7 10.3 %collective-permute-done.10.refs_2_ = bf16[128,2048]{1,0:T(8,128)(2,1)} collective-permute-done((bf16[128,2048]{1,0:T(8,128)(2,1)S(1)}, bf16[128,2048]{1,0:T(8,128)(2,1)}, u32[]{:S(2)}, u32[]{:S(2)}) %collective-permute-start.10) | collective-permute-done | bytes 524320 | tf_op jit(solution)/shard_map/ppermute | solution.py:113
  62.6 7.6 %collective-permute-done.8 = bf16[8,448]{1,0:T(8,128)(2,1)S(1)} collective-permute-done((bf16[8,448]{1,0:T(8,128)(2,1)S(1)}, bf16[8,448]{1,0:T(8,128)(2,1)S(1)}, u32[]{:S(2)}, u32[]{:S(2)}) %collective-permute-start.8) | collective-permute-done | bytes 7200 | tf_op jit(solution)/shard_map/ppermute | solution.py:113
  78.9 16.1 %collective-permute-done.13 = bf16[2,8,448]{2,1,0:T(8,128)(2,1)S(1)} collective-permute-done((bf16[2,8,448]{2,1,0:T(8,128)(2,1)S(1)}, bf16[2,8,448]{2,1,0:T(8,128)(2,1)S(1)}, u32[]{:S(2)}, u32[]{:S(2)}) %collective-permute-start.13) | collective-permute-done | bytes 14368 | tf_op jit(solution)/shard_map/ppermute | solution.py:113
  112.5 19.0 %attention.1 = (bf16[1024,2048]{1,0:T(8,128)(2,1)S(1)}, bf16[1024,768]{1,0:T(8,128)(2,1)S(1)}, bf16[1024,256]{1,0:T(8,128)(2,1)S(1)}, f32[16,256]{1,0:T(8,128)S(1)}) custom-call(bf16[128,2048]{1,0:T(8,128)(2,1)S(1)} %copy-done.8, bf16[128,2048]{1,0:T(8,128)(2,1)} %collective-permute-done.9.refs_1_, bf16[128,2048]{1,0:T(8,128)(2,1)} %collective-permute-done.10.refs_2_, ...), custom_call_target="tpu_custom_call" | custom-call | tf_op jit(solution)/shard_map/attention/pallas_call | solution.py:228
  152.6 10.7 %collective-permute-done.29.refs_1_ = bf16[128,2048]{1,0:T(8,128)(2,1)S(1)} collective-permute-done((bf16[128,2048]{1,0:T(8,128)(2,1)S(1)}, bf16[128,2048]{1,0:T(8,128)(2,1)S(1)}, u32[]{:S(2)}, u32[]{:S(2)}) %collective-permute-start.29) | collective-permute-done | bytes 524320 | tf_op jit(solution)/shard_map/ppermute | solution.py:113
  165.1 8.6 %collective-permute-done.33.refs_1_ = bf16[128,2048]{1,0:T(8,128)(2,1)S(1)} collective-permute-done((bf16[128,2048]{1,0:T(8,128)(2,1)S(1)}, bf16[128,2048]{1,0:T(8,128)(2,1)S(1)}, u32[]{:S(2)}, u32[]{:S(2)}) %collective-permute-start.33) | collective-permute-done | bytes 524320 | tf_op jit(solution)/shard_map/ppermute | solution.py:113
  173.7 10.0 %collective-permute-done.32.refs_13_.refs_5_ = bf16[512,640]{1,0:T(8,128)(2,1)S(1)} collective-permute-done((bf16[512,640]{1,0:T(8,128)(2,1)S(1)}, bf16[512,640]{1,0:T(8,128)(2,1)S(1)}, u32[]{:S(2)}, u32[]{:S(2)}) %collective-permute-start.32) | collective-permute-done | bytes 655392 | tf_op jit(solution)/shard_map/ppermute | solution.py:113
  183.8 5.9 %collective-permute-done.34.refs_2_ = bf16[128,2048]{1,0:T(8,128)(2,1)S(1)} collective-permute-done((bf16[128,2048]{1,0:T(8,128)(2,1)S(1)}, bf16[128,2048]{1,0:T(8,128)(2,1)S(1)}, u32[]{:S(2)}, u32[]{:S(2)}) %collective-permute-start.34) | collective-permute-done | bytes 524320 | tf_op jit(solution)/shard_map/ppermute | solution.py:113
  197.5 12.3 %collective-permute-done.39.refs_2_ = bf16[128,2048]{1,0:T(8,128)(2,1)S(1)} collective-permute-done((bf16[128,2048]{1,0:T(8,128)(2,1)S(1)}, bf16[128,2048]{1,0:T(8,128)(2,1)S(1)}, u32[]{:S(2)}, u32[]{:S(2)}) %collective-permute-start.39) | collective-permute-done | bytes 524320 | tf_op jit(solution)/shard_map/ppermute | solution.py:113
  212.9 9.9 %collective-permute-done.37.refs_15_.refs_7_ = bf16[512,640]{1,0:T(8,128)(2,1)S(1)} collective-permute-done((bf16[512,640]{1,0:T(8,128)(2,1)S(1)}, bf16[512,640]{1,0:T(8,128)(2,1)S(1)}, u32[]{:S(2)}, u32[]{:S(2)}) %collective-permute-start.37) | collective-permute-done | bytes 655392 | tf_op jit(solution)/shard_map/ppermute | solution.py:113
  222.8 6.8 %collective-permute-done.35.refs_2_ = bf16[512,768]{1,0:T(8,128)(2,1)S(1)} collective-permute-done((bf16[512,768]{1,0:T(8,128)(2,1)S(1)}, bf16[512,768]{1,0:T(8,128)(2,1)S(1)}, u32[]{:S(2)}, u32[]{:S(2)}) %collective-permute-start.35) | collective-permute-done | bytes 786464 | tf_op jit(solution)/shard_map/ppermute | solution.py:113
  233.3 10.2 %mlp.1 = (bf16[1024,2048]{1,0:T(8,128)(2,1)S(1)}, bf16[1024,768]{1,0:T(8,128)(2,1)S(1)}, f32[1024,704]{1,0:T(8,128)S(1)}, f32[1024,704]{1,0:T(8,128)S(1)}) custom-call(bf16[128,2048]{1,0:T(8,128)(2,1)S(1)} %get-tuple-element.768.refs_0_, bf16[128,2048]{1,0:T(8,128)(2,1)S(1)} %collective-permute-done.38.refs_1_, ...), custom_call_target="tpu_custom_call" | custom-call | tf_op jit(solution)/shard_map/mlp/pallas_call | solution.py:228
  252.9 5.1 expand.7
  275.0 10.7 %collective-permute-done.50.refs_1_ = bf16[128,2048]{1,0:T(8,128)(2,1)S(1)} collective-permute-done((bf16[128,2048]{1,0:T(8,128)(2,1)S(1)}, bf16[128,2048]{1,0:T(8,128)(2,1)S(1)}, u32[]{:S(2)}, u32[]{:S(2)}) %collective-permute-start.50) | collective-permute-done | bytes 524320 | tf_op jit(solution)/shard_map/ppermute | solution.py:113
  296.5 8.6 %collective-permute-done.51.refs_2_ = bf16[512,640]{1,0:T(8,128)(2,1)S(1)} collective-permute-done((bf16[512,640]{1,0:T(8,128)(2,1)S(1)}, bf16[512,640]{1,0:T(8,128)(2,1)S(1)}, u32[]{:S(2)}, u32[]{:S(2)}) %collective-permute-start.51) | collective-permute-done | bytes 655392 | tf_op jit(solution)/shard_map/ppermute | solution.py:113
  308.7 7.1 %collective-permute-done.53.refs_2_ = bf16[128,2048]{1,0:T(8,128)(2,1)S(1)} collective-permute-done((bf16[128,2048]{1,0:T(8,128)(2,1)S(1)}, bf16[128,2048]{1,0:T(8,128)(2,1)S(1)}, u32[]{:S(2)}, u32[]{:S(2)}) %collective-permute-start.53) | collective-permute-done | bytes 524320 | tf_op jit(solution)/shard_map/ppermute | solution.py:113
  324.9 12.9 %collective-permute-done.58.refs_2_ = bf16[128,2048]{1,0:T(8,128)(2,1)S(1)} collective-permute-done((bf16[128,2048]{1,0:T(8,128)(2,1)S(1)}, bf16[128,2048]{1,0:T(8,128)(2,1)S(1)}, u32[]{:S(2)}, u32[]{:S(2)}) %collective-permute-start.58) | collective-permute-done | bytes 524320 | tf_op jit(solution)/shard_map/ppermute | solution.py:113
  338.6 11.2 %collective-permute-done.55.refs_4_ = bf16[512,640]{1,0:T(8,128)(2,1)S(1)} collective-permute-done((bf16[512,640]{1,0:T(8,128)(2,1)S(1)}, bf16[512,640]{1,0:T(8,128)(2,1)S(1)}, u32[]{:S(2)}, u32[]{:S(2)}) %collective-permute-start.55) | collective-permute-done | bytes 655392 | tf_op jit(solution)/shard_map/ppermute | solution.py:113
  388.0 9.4 %attend_back.1 = (bf16[1024,768]{1,0:T(8,128)(2,1)S(1)}, f32[1,768]{1,0:T(1,128)S(1)}) custom-call(bf16[1024,256]{1,0:T(8,128)(2,1)S(1)} %copy-done.61, bf16[1024,768]{1,0:T(8,128)(2,1)S(1)} %copy-done.28, f32[16,256]{1,0:T(8,128)S(1)} %get-tuple-element.1035.sums, f32[1024,384]{1,0:T(8,128)S(1)} %convolution_add_fusion.refs_15_.table, ...), custom_call_target="tpu_custom_call" | custom-call | tf_op jit(solution)/shard_map/attend_back/pallas_call | solution.py:228
  431.6 5.5 %expand_add.3 = (bf16[128,2048]{1,0:T(8,128)(2,1)S(1)}, bf16[128,2048]{1,0:T(8,128)(2,1)S(1)}, bf16[128,2048]{1,0:T(8,128)(2,1)S(1)}, bf16[128,2048]{1,0:T(8,128)(2,1)S(1)}) custom-call(bf16[1024,768]{1,0:T(8,128)(2,1)S(1)} %get-tuple-element.1083.refs_1_.values, bf16[512,768]{1,0:T(8,128)(2,1)S(1)} %copy-done.13, ...), custom_call_target="tpu_custom_call" | custom-call | tf_op jit(solution)/shard_map/expand_add/pallas_call | solution.py:228
  452.1 9.5 %collective-permute-done.74.refs_1_ = bf16[128,2048]{1,0:T(8,128)(2,1)S(1)} collective-permute-done((bf16[128,2048]{1,0:T(8,128)(2,1)}, bf16[128,2048]{1,0:T(8,128)(2,1)S(1)}, u32[]{:S(2)}, u32[]{:S(2)}) %collective-permute-start.74) | collective-permute-done | bytes 524320 | tf_op jit(solution)/shard_map/ppermute | solution.py:113
  472.8 12.3 %collective-permute-done.75.refs_2_ = bf16[512,768]{1,0:T(8,128)(2,1)S(1)} collective-permute-done((bf16[512,768]{1,0:T(8,128)(2,1)}, bf16[512,768]{1,0:T(8,128)(2,1)S(1)}, u32[]{:S(2)}, u32[]{:S(2)}) %collective-permute-start.75) | collective-permute-done | bytes 786464 | tf_op jit(solution)/shard_map/ppermute | solution.py:113
  485.1 5.0 collective-permute-done.78.refs_2_
  (485 shorter events, 289.2 us)
Async XLA Ops:
  33.2 37.0 %collective-permute-start.6 = (bf16[512,768]{1,0:T(8,128)(2,1)S(1)}, bf16[512,768]{1,0:T(8,128)(2,1)}, u32[]{:S(2)}, u32[]{:S(2)}) collective-permute-start(bf16[512,768]{1,0:T(8,128)(2,1)S(1)} %get-tuple-element.1086.refs_8_.refs_0_), channel_id=1, source_target_pairs={{0,4},{1,5},{2,6},{3,7},{4,0},{5,1},{6,2},{7,3},{8,12},{9,13},{10,... | collective-permute-start | bytes 2359304 | tf_op jit(solution)/shard_map/ppermute | solution.py:113
  34.7 35.5 %collective-permute-start.5 = (bf16[512,768]{1,0:T(8,128)(2,1)S(1)}, bf16[512,768]{1,0:T(8,128)(2,1)}, u32[]{:S(2)}, u32[]{:S(2)}) collective-permute-start(bf16[512,768]{1,0:T(8,128)(2,1)S(1)} %get-tuple-element.1086.refs_8_.refs_0_), channel_id=1, source_target_pairs={{16,0},{17,1},{18,2},{19,3},{20,4},{21,5},{22,6},{23,7},{24,8},{25... | collective-permute-start | bytes 2359304 | tf_op jit(solution)/shard_map/ppermute | solution.py:113
  97.3 42.5 %all-to-all-start.2 = ((bf16[8,64,1408]{2,1,0:T(8,128)(2,1)}), bf16[8,64,1408]{2,1,0:T(8,128)(2,1)}, u32[]{:S(2)}, u32[]{:S(2)}) async-start(bf16[8,64,1408]{2,1,0:T(8,128)(2,1)} %bitcast.93), calls=%async_computation.2 | async-start | bytes 2883584 | tf_op jit(solution)/shard_map/all_to_all | solution.py:135
  101.7 34.7 %collective-permute-start.21 = (bf16[512,768]{1,0:T(8,128)(2,1)S(1)}, bf16[512,768]{1,0:T(8,128)(2,1)}, u32[]{:S(2)}, u32[]{:S(2)}) collective-permute-start(bf16[512,768]{1,0:T(8,128)(2,1)S(1)} %bitcast.85), channel_id=1, source_target_pairs={{0,4},{1,5},{2,6},{3,7},{4,0},{5,1},{6,2},{7,3},{8,12},{9,13},{10,... | collective-permute-start | bytes 2359304 | tf_op jit(solution)/shard_map/ppermute | solution.py:113
  102.3 37.5 %collective-permute-start.20 = (bf16[512,768]{1,0:T(8,128)(2,1)S(1)}, bf16[512,768]{1,0:T(8,128)(2,1)}, u32[]{:S(2)}, u32[]{:S(2)}) collective-permute-start(bf16[512,768]{1,0:T(8,128)(2,1)S(1)} %bitcast.86), channel_id=1, source_target_pairs={{16,0},{17,1},{18,2},{19,3},{20,4},{21,5},{22,6},{23,7},{24,8},{25... | collective-permute-start | bytes 2359304 | tf_op jit(solution)/shard_map/ppermute | solution.py:113
  104.2 32.3 %collective-permute-start.19 = (bf16[128,2048]{1,0:T(8,128)(2,1)}, bf16[128,2048]{1,0:T(8,128)(2,1)}, u32[]{:S(2)}, u32[]{:S(2)}) collective-permute-start(bf16[128,2048]{1,0:T(8,128)(2,1)} %collective-permute-done.1.refs_2_), channel_id=1, source_target_pairs={{0,2},{1,3},{2,0},{3,1},{4,6},{5,7},{6,4},{7,5},{8,10},{9,11},{10,... | collective-permute-start | bytes 1572872 | tf_op jit(solution)/shard_map/ppermute | solution.py:113
  150.2 33.6 %collective-permute-start.30 = (bf16[512,768]{1,0:T(8,128)(2,1)}, bf16[512,768]{1,0:T(8,128)(2,1)S(1)}, u32[]{:S(2)}, u32[]{:S(2)}) collective-permute-start(bf16[512,768]{1,0:T(8,128)(2,1)} %collective-permute-done.20.refs_10_.refs_2_), channel_id=1, source_target_pairs={{0,4},{1,5},{2,6},{3,7},{4,0},{5,1},{6,2},{7,3},{8,12},{9,13},{10,... | collective-permute-start | bytes 2359304 | tf_op jit(solution)/shard_map/ppermute | solution.py:113
  151.7 32.0 %collective-permute-start.32 = (bf16[512,640]{1,0:T(8,128)(2,1)S(1)}, bf16[512,640]{1,0:T(8,128)(2,1)S(1)}, u32[]{:S(2)}, u32[]{:S(2)}) collective-permute-start(bf16[512,640]{1,0:T(8,128)(2,1)S(1)} %get-tuple-element.827.refs_12_.refs_4_), channel_id=1, source_target_pairs={{0,4},{1,5},{2,6},{3,7},{4,0},{5,1},{6,2},{7,3},{8,12},{9,13},{10,... | collective-permute-start | bytes 1966088 | tf_op jit(solution)/shard_map/ppermute | solution.py:113
  152.2 31.6 %collective-permute-start.31 = (bf16[512,640]{1,0:T(8,128)(2,1)S(1)}, bf16[512,640]{1,0:T(8,128)(2,1)S(1)}, u32[]{:S(2)}, u32[]{:S(2)}) collective-permute-start(bf16[512,640]{1,0:T(8,128)(2,1)S(1)} %get-tuple-element.827.refs_12_.refs_4_), channel_id=1, source_target_pairs={{16,0},{17,1},{18,2},{19,3},{20,4},{21,5},{22,6},{23,7},{24,8},{25... | collective-permute-start | bytes 1966088 | tf_op jit(solution)/shard_map/ppermute | solution.py:113
  191.9 30.9 %collective-permute-start.36 = (bf16[512,768]{1,0:T(8,128)(2,1)S(1)}, bf16[512,768]{1,0:T(8,128)(2,1)S(1)}, u32[]{:S(2)}, u32[]{:S(2)}) collective-permute-start(bf16[512,768]{1,0:T(8,128)(2,1)S(1)} %get-tuple-element.925.refs_0_), channel_id=1, source_target_pairs={{0,4},{1,5},{2,6},{3,7},{4,0},{5,1},{6,2},{7,3},{8,12},{9,13},{10,... | collective-permute-start | bytes 2359304 | tf_op jit(solution)/shard_map/ppermute | solution.py:113
  193.5 36.1 %collective-permute-start.35 = (bf16[512,768]{1,0:T(8,128)(2,1)S(1)}, bf16[512,768]{1,0:T(8,128)(2,1)S(1)}, u32[]{:S(2)}, u32[]{:S(2)}) collective-permute-start(bf16[512,768]{1,0:T(8,128)(2,1)S(1)} %get-tuple-element.925.refs_0_), channel_id=1, source_target_pairs={{16,0},{17,1},{18,2},{19,3},{20,4},{21,5},{22,6},{23,7},{24,8},{25... | collective-permute-start | bytes 2359304 | tf_op jit(solution)/shard_map/ppermute | solution.py:113
  271.2 37.5 %collective-permute-start.48 = (bf16[512,768]{1,0:T(8,128)(2,1)S(1)}, bf16[512,768]{1,0:T(8,128)(2,1)S(1)}, u32[]{:S(2)}, u32[]{:S(2)}) collective-permute-start(bf16[512,768]{1,0:T(8,128)(2,1)S(1)} %grad.17), channel_id=1, source_target_pairs={{0,16},{1,17},{2,18},{3,19},{4,20},{5,21},{6,22},{7,23},{8,24},{9,... | collective-permute-start | bytes 2359304 | tf_op jit(solution)/shard_map/ppermute | solution.py:113
  271.2 37.5 %collective-permute-start.49 = (bf16[512,768]{1,0:T(8,128)(2,1)S(1)}, bf16[512,768]{1,0:T(8,128)(2,1)S(1)}, u32[]{:S(2)}, u32[]{:S(2)}) collective-permute-start(bf16[512,768]{1,0:T(8,128)(2,1)S(1)} %get-tuple-element.896), channel_id=1, source_target_pairs={{0,4},{1,5},{2,6},{3,7},{4,0},{5,1},{6,2},{7,3},{8,12},{9,13},{10,... | collective-permute-start | bytes 2359304 | tf_op jit(solution)/shard_map/ppermute | solution.py:113
  273.0 32.1 %collective-permute-start.51 = (bf16[512,640]{1,0:T(8,128)(2,1)S(1)}, bf16[512,640]{1,0:T(8,128)(2,1)S(1)}, u32[]{:S(2)}, u32[]{:S(2)}) collective-permute-start(bf16[512,640]{1,0:T(8,128)(2,1)S(1)} %get-tuple-element.898), channel_id=1, source_target_pairs={{0,4},{1,5},{2,6},{3,7},{4,0},{5,1},{6,2},{7,3},{8,12},{9,13},{10,... | collective-permute-start | bytes 1966088 | tf_op jit(solution)/shard_map/ppermute | solution.py:113
  285.8 30.0 %collective-permute-start.53 = (bf16[128,2048]{1,0:T(8,128)(2,1)S(1)}, bf16[128,2048]{1,0:T(8,128)(2,1)S(1)}, u32[]{:S(2)}, u32[]{:S(2)}) collective-permute-start(bf16[128,2048]{1,0:T(8,128)(2,1)S(1)} %add.360), channel_id=1, source_target_pairs={{0,8},{1,9},{2,10},{3,11},{4,12},{5,13},{6,14},{7,15},{8,0},{9,1},... | collective-permute-start | bytes 1572872 | tf_op jit(solution)/shard_map/ppermute | solution.py:113
  318.1 33.1 %collective-permute-start.56 = (bf16[512,768]{1,0:T(8,128)(2,1)S(1)}, bf16[512,768]{1,0:T(8,128)(2,1)S(1)}, u32[]{:S(2)}, u32[]{:S(2)}) collective-permute-start(bf16[512,768]{1,0:T(8,128)(2,1)S(1)} %get-tuple-element.965), channel_id=1, source_target_pairs={{0,4},{1,5},{2,6},{3,7},{4,0},{5,1},{6,2},{7,3},{8,12},{9,13},{10,... | collective-permute-start | bytes 2359304 | tf_op jit(solution)/shard_map/ppermute | solution.py:113
  362.7 46.2 %all-to-all-start.3 = ((bf16[8,64,1408]{2,1,0:T(8,128)(2,1)}), bf16[8,64,1408]{2,1,0:T(8,128)(2,1)}, u32[]{:S(2)}, u32[]{:S(2)}) async-start(bf16[8,64,1408]{2,1,0:T(8,128)(2,1)} %bitcast.32), calls=%async_computation.3 | async-start | bytes 2883584 | tf_op jit(solution)/shard_map/all_to_all | solution.py:135
  367.0 41.9 %collective-permute-start.68 = (bf16[512,768]{1,0:T(8,128)(2,1)}, bf16[512,768]{1,0:T(8,128)(2,1)}, u32[]{:S(2)}, u32[]{:S(2)}) collective-permute-start(bf16[512,768]{1,0:T(8,128)(2,1)} %grad.23), channel_id=1, source_target_pairs={{0,16},{1,17},{2,18},{3,19},{4,20},{5,21},{6,22},{7,23},{8,24},{9,... | collective-permute-start | bytes 2359304 | tf_op jit(solution)/shard_map/ppermute | solution.py:113
  368.4 40.5 %collective-permute-start.69 = (bf16[512,768]{1,0:T(8,128)(2,1)}, bf16[512,768]{1,0:T(8,128)(2,1)}, u32[]{:S(2)}, u32[]{:S(2)}) collective-permute-start(bf16[512,768]{1,0:T(8,128)(2,1)} %copy-done.76), channel_id=1, source_target_pairs={{0,4},{1,5},{2,6},{3,7},{4,0},{5,1},{6,2},{7,3},{8,12},{9,13},{10,... | collective-permute-start | bytes 2359304 | tf_op jit(solution)/shard_map/ppermute | solution.py:113
  370.1 38.8 %collective-permute-start.66 = (bf16[128,2048]{1,0:T(8,128)(2,1)}, bf16[128,2048]{1,0:T(8,128)(2,1)}, u32[]{:S(2)}, u32[]{:S(2)}) collective-permute-start(bf16[128,2048]{1,0:T(8,128)(2,1)} %copy-done.80), channel_id=1, source_target_pairs={{0,2},{1,3},{2,0},{3,1},{4,6},{5,7},{6,4},{7,5},{8,10},{9,11},{10,... | collective-permute-start | bytes 1572872 | tf_op jit(solution)/shard_map/ppermute | solution.py:113
  371.9 37.0 %collective-permute-start.67 = (bf16[128,2048]{1,0:T(8,128)(2,1)}, bf16[128,2048]{1,0:T(8,128)(2,1)}, u32[]{:S(2)}, u32[]{:S(2)}) collective-permute-start(bf16[128,2048]{1,0:T(8,128)(2,1)} %copy-done.79), channel_id=1, source_target_pairs={{0,2},{1,3},{2,0},{3,1},{4,6},{5,7},{6,4},{7,5},{8,10},{9,11},{10,... | collective-permute-start | bytes 1572872 | tf_op jit(solution)/shard_map/ppermute | solution.py:113
  412.8 33.8 %all-to-all-start.4 = ((bf16[8,64,768]{2,1,0:T(8,128)(2,1)}), bf16[8,64,768]{2,1,0:T(8,128)(2,1)}, u32[]{:S(2)}, u32[]{:S(2)}) async-start(bf16[8,64,768]{2,1,0:T(8,128)(2,1)} %bitcast.92), calls=%async_computation.4 | async-start | bytes 1572864 | tf_op jit(solution)/shard_map/all_to_all | solution.py:135
  448.0 37.0 %collective-permute-start.75 = (bf16[512,768]{1,0:T(8,128)(2,1)}, bf16[512,768]{1,0:T(8,128)(2,1)S(1)}, u32[]{:S(2)}, u32[]{:S(2)}) collective-permute-start(bf16[512,768]{1,0:T(8,128)(2,1)} %copy-done.34), channel_id=1, source_target_pairs={{0,16},{1,17},{2,18},{3,19},{4,20},{5,21},{6,22},{7,23},{8,24},{9,... | collective-permute-start | bytes 2359304 | tf_op jit(solution)/shard_map/ppermute | solution.py:113
  450.2 34.9 %collective-permute-start.76 = (bf16[512,768]{1,0:T(8,128)(2,1)}, bf16[512,768]{1,0:T(8,128)(2,1)S(1)}, u32[]{:S(2)}, u32[]{:S(2)}) collective-permute-start(bf16[512,768]{1,0:T(8,128)(2,1)} %copy-done.75), channel_id=1, source_target_pairs={{0,4},{1,5},{2,6},{3,7},{4,0},{5,1},{6,2},{7,3},{8,12},{9,13},{10,... | collective-permute-start | bytes 2359304 | tf_op jit(solution)/shard_map/ppermute | solution.py:113
  (155 other events, 1901.1 us)

commit v6 on v5

--- a/solution.py
+++ b/solution.py
@@ -840,7 +840,8 @@
     v.front = at.swap(cut_rows(at, [qkv_weight, out_weight], (3, 1), 4 * part), at.groups)
     v.small = jnp.concatenate([at.after(qkv_bias), ln1_gain, ln1_bias, ln2_gain, ln2_bias])[None]
     v.small = joined(at.c, v.small, at.flip(v.small, c=1), 0)
-    v.small = joined(at.x, v.small, at.flip(v.small, x=1), 0)
+    v.small = jnp.stack([v.small, at.flip(v.small, e=1)])
+    v.small = jnp.stack([v.small] + [at.shift(v.small, i) for i in range(1, at.outer)])
     (v.inputs,) = to_relative(at, layer_input, [1])
     v.first, v.later = split(
         at,
@@ -858,8 +859,8 @@
     v.qkv_beside = [at.flip(v.qkv, e=1)]
     v.tokens = spread_tokens(at, v.inputs)
     v.turned = [at.flip(v.tokens[1], c=1)]
-    v.small = joined(at.b, v.small, at.flip(v.small, b=1), 0)
-    v.small = jnp.stack([v.small] + [at.shift(v.small, i) for i in range(1, at.outer)])
+    v.small = joined(at.x, v.small, at.flip(v.small, x=1), 2)
+    v.small = joined(at.b, v.small, at.flip(v.small, b=1), 2)
     segments_here = order_tokens(at, v.spots[:, 0])
     places = order_tokens(at, v.spots[:, 1])
     index = order_tokens(at, jnp.arange(length)[None])
@@ -875,7 +876,6 @@
     v.out_across = cross_block(at, v.out)
     v.first = at.swap(v.first, at.groups)
 
-    v.small = jnp.stack([v.small, at.flip(v.small, e=1)], axis=1)
 
     def vector(i):
         start = bias_rows + i * rows
@@ -1111,7 +1111,23 @@
         at, result_kernel, [((near, width), BF16)], v.hidden, *v.result_terms, name="result"
     )
     (v.result,) = to_absolute(at, v.result)
+    v.gate_grad, v.up_grad = grad_spread(
+        at,
+        [v.early, v.late],
+        (1, 1),
+        ((1, 0, first), (0, padded, second)),
+        (8 * units,) * 2,
+    )
     (v.down_grad,) = grad_spread(at, [v.early], (1,), ((0, 0, units),), (8 * units,))
+    bias_part = v.bias_part.reshape(3, 1, part)
+    own_slot = (jnp.arange(8) == slot).astype(F32)[None, :, None]
+    bias_whole = (bias_part * own_slot).reshape(at.outer, 2, 2, 4, bias_rows).swapaxes(1, 2)
+    bias_whole = jnp.roll(bias_whole, -at.a, axis=0)
+    bias_whole = pick(at.e, bias_whole, bias_whole[:, ::-1])
+    v.small_first = bias_whole.reshape(at.outer, 2, 8, bias_rows)
+    v.small_last = jnp.concatenate(
+        [g.reshape(at.outer, 2, 8, rows) for g in (v.gain_two_grad, v.shift_two_grad)], axis=-1
+    )
     v.close(at)
     del v.other, v.qkv_made, v.pieces
 
@@ -1133,25 +1149,11 @@
         *v.terms,
         name="inputs",
     )
-    gate_wgrad, up_wgrad = grad_spread(
-        at,
-        [v.early, v.late],
-        (1, 1),
-        ((1, 0, first), (0, padded, second)),
-        (8 * units,) * 2,
-    )
     (input_grad,) = to_absolute(at, v.input_grad)
-    v.done = [gate_wgrad, up_wgrad, input_grad]
-    bias_part = v.bias_part.reshape(3, 1, part)
-    own_slot = (jnp.arange(8) == slot).astype(F32)[None, :, None]
-    bias_whole = (bias_part * own_slot).reshape(at.outer, 2, 2, 4, bias_rows).swapaxes(1, 2)
-    bias_whole = jnp.roll(bias_whole, -at.a, axis=0)
-    bias_whole = pick(at.e, bias_whole, bias_whole[:, ::-1]).reshape(at.outer, 2, 8, bias_rows)
-    grads = [
-        g.reshape(at.outer, 2, 8, rows)
-        for g in (gain_one_grad, shift_one_grad, v.gain_two_grad, v.shift_two_grad)
-    ]
-    v.small = send_small(at, jnp.concatenate([bias_whole] + grads, axis=-1))
+    v.done = [v.gate_grad, v.up_grad, input_grad]
+    grads = [g.reshape(at.outer, 2, 8, rows) for g in (gain_one_grad, shift_one_grad)]
+    v.small = jnp.concatenate([v.small_first, *grads, v.small_last], axis=-1)
+    v.small = send_small(at, v.small)
     v.close(at)
     gate_wgrad, up_wgrad, input_grad = v.done
     result, down_grad = v.result, v.down_grad

time: 529 us -> 526 us (level)
  starting transfers between devices: 112 us -> 106 us
    ppermute x82, starting transfers between devices: 83.8 us -> 76.1 us  [move(): return lax.ppermute(values, AXES, pairs)]
    unnamed x184 -> x178, local copies, waits for them, and re-layouts: 49.4 us -> 48.9 us
  transfers between devices with their start and end apart: 89 -> 89, of which waited for: 35 -> 40; matrix products, arithmetic and copies ran while one was open for 2% -> 2% of each run, Pallas kernels for 25% -> 25%
where the time goes in v6:
time: 526 us; the launch traced here: 520 us
  waiting for transfers between devices  214 us (41%)
  Pallas kernels  135 us (26%)
  starting transfers between devices  106 us (20%)
  local copies, waits for them, and re-layouts  55.5 us (11%)
  other arithmetic  6.3 us (1%)
    ppermute x82, waiting for transfers between devices, move(): return lax.ppermute(values, AXES, pairs)  208 us
    pallas_call x54, Pallas kernels, call(): pl.pallas_call(kernel, grid=(steps,), out_shape=[jax.ShapeDtypeStruct(sha...  135 us
    ppermute x82, starting transfers between devices, move(): return lax.ppermute(values, AXES, pairs)  76.1 us
    unnamed x178, local copies, waits for them, and re-layouts  48.9 us
    all_to_all x7, starting transfers between devices, swap(): lax.all_to_all(view, AXES, 0, 0, axis_index_groups=groups, tiled=True)  29.9 us
  transfers between devices with their start and end apart: 89, of which 40 were waited for; matrix products, arithmetic and copies ran while one was open for 2% of the time, Pallas kernels for 25%

profile of v6, /device:TPU:0, one launch (start us, length us, event | category | flops | bytes accessed | tf_op | source)
XLA Modules:
  0.0 520.0 jit_solution(18218637432871698413)
XLA Ops:
  40.6 10.1 %collective-permute-done.11.refs_2_ = bf16[128,2048]{1,0:T(8,128)(2,1)} collective-permute-done((bf16[128,2048]{1,0:T(8,128)(2,1)S(1)}, bf16[128,2048]{1,0:T(8,128)(2,1)}, u32[]{:S(2)}, u32[]{:S(2)}) %collective-permute-start.11) | collective-permute-done | bytes 524320 | tf_op jit(solution)/shard_map/ppermute | solution.py:113
  59.9 11.6 %collective-permute-done.6.refs_10_.refs_2_ = bf16[512,768]{1,0:T(8,128)(2,1)} collective-permute-done((bf16[512,768]{1,0:T(8,128)(2,1)S(1)}, bf16[512,768]{1,0:T(8,128)(2,1)}, u32[]{:S(2)}, u32[]{:S(2)}) %collective-permute-start.6) | collective-permute-done | bytes 786464 | tf_op jit(solution)/shard_map/ppermute | solution.py:113
  77.1 13.2 %collective-permute-done.14.refs_2_.refs_10_ = bf16[512,256]{1,0:T(8,128)(2,1)} collective-permute-done((bf16[512,256]{1,0:T(8,128)(2,1)}, bf16[512,256]{1,0:T(8,128)(2,1)}, u32[]{:S(2)}, u32[]{:S(2)}) %collective-permute-start.14) | collective-permute-done | bytes 262176 | tf_op jit(solution)/shard_map/ppermute | solution.py:113
  107.7 19.2 %attention.1 = (bf16[1024,2048]{1,0:T(8,128)(2,1)S(1)}, bf16[1024,768]{1,0:T(8,128)(2,1)S(1)}, bf16[1024,256]{1,0:T(8,128)(2,1)S(1)}, f32[16,256]{1,0:T(8,128)S(1)}) custom-call(bf16[128,2048]{1,0:T(8,128)(2,1)S(1)} %copy-done.8, bf16[128,2048]{1,0:T(8,128)(2,1)} %collective-permute-done.10.refs_1_, bf16[128,2048]{1,0:T(8,128)(2,1)} %collective-permute-done.11.refs_2_, ...), custom_call_target="tpu_custom_call" | custom-call | tf_op jit(solution)/shard_map/attention/pallas_call | solution.py:228
  150.6 10.7 %collective-permute-done.29.refs_1_ = bf16[128,2048]{1,0:T(8,128)(2,1)S(1)} collective-permute-done((bf16[128,2048]{1,0:T(8,128)(2,1)S(1)}, bf16[128,2048]{1,0:T(8,128)(2,1)S(1)}, u32[]{:S(2)}, u32[]{:S(2)}) %collective-permute-start.29) | collective-permute-done | bytes 524320 | tf_op jit(solution)/shard_map/ppermute | solution.py:113
  163.0 8.7 %collective-permute-done.33.refs_1_ = bf16[128,2048]{1,0:T(8,128)(2,1)S(1)} collective-permute-done((bf16[128,2048]{1,0:T(8,128)(2,1)S(1)}, bf16[128,2048]{1,0:T(8,128)(2,1)S(1)}, u32[]{:S(2)}, u32[]{:S(2)}) %collective-permute-start.33) | collective-permute-done | bytes 524320 | tf_op jit(solution)/shard_map/ppermute | solution.py:113
  171.7 10.0 %collective-permute-done.32.refs_13_.refs_5_ = bf16[512,640]{1,0:T(8,128)(2,1)S(1)} collective-permute-done((bf16[512,640]{1,0:T(8,128)(2,1)S(1)}, bf16[512,640]{1,0:T(8,128)(2,1)S(1)}, u32[]{:S(2)}, u32[]{:S(2)}) %collective-permute-start.32) | collective-permute-done | bytes 655392 | tf_op jit(solution)/shard_map/ppermute | solution.py:113
  181.8 6.0 %collective-permute-done.34.refs_2_ = bf16[128,2048]{1,0:T(8,128)(2,1)S(1)} collective-permute-done((bf16[128,2048]{1,0:T(8,128)(2,1)S(1)}, bf16[128,2048]{1,0:T(8,128)(2,1)S(1)}, u32[]{:S(2)}, u32[]{:S(2)}) %collective-permute-start.34) | collective-permute-done | bytes 524320 | tf_op jit(solution)/shard_map/ppermute | solution.py:113
  194.0 12.8 %collective-permute-done.39.refs_2_ = bf16[128,2048]{1,0:T(8,128)(2,1)S(1)} collective-permute-done((bf16[128,2048]{1,0:T(8,128)(2,1)S(1)}, bf16[128,2048]{1,0:T(8,128)(2,1)S(1)}, u32[]{:S(2)}, u32[]{:S(2)}) %collective-permute-start.39) | collective-permute-done | bytes 524320 | tf_op jit(solution)/shard_map/ppermute | solution.py:113
  210.3 11.6 %collective-permute-done.37.refs_15_.refs_7_ = bf16[512,640]{1,0:T(8,128)(2,1)S(1)} collective-permute-done((bf16[512,640]{1,0:T(8,128)(2,1)S(1)}, bf16[512,640]{1,0:T(8,128)(2,1)S(1)}, u32[]{:S(2)}, u32[]{:S(2)}) %collective-permute-start.37) | collective-permute-done | bytes 655392 | tf_op jit(solution)/shard_map/ppermute | solution.py:113
  230.8 10.2 %mlp.1 = (bf16[1024,2048]{1,0:T(8,128)(2,1)S(1)}, bf16[1024,768]{1,0:T(8,128)(2,1)S(1)}, f32[1024,704]{1,0:T(8,128)S(1)}, f32[1024,704]{1,0:T(8,128)S(1)}) custom-call(bf16[128,2048]{1,0:T(8,128)(2,1)S(1)} %get-tuple-element.767.refs_0_, bf16[128,2048]{1,0:T(8,128)(2,1)S(1)} %collective-permute-done.38.refs_1_, ...), custom_call_target="tpu_custom_call" | custom-call | tf_op jit(solution)/shard_map/mlp/pallas_call | solution.py:228
  250.3 5.1 expand.7
  255.4 5.0 expand.8.own
  272.5 10.7 %collective-permute-done.50.refs_1_ = bf16[128,2048]{1,0:T(8,128)(2,1)S(1)} collective-permute-done((bf16[128,2048]{1,0:T(8,128)(2,1)S(1)}, bf16[128,2048]{1,0:T(8,128)(2,1)S(1)}, u32[]{:S(2)}, u32[]{:S(2)}) %collective-permute-start.50) | collective-permute-done | bytes 524320 | tf_op jit(solution)/shard_map/ppermute | solution.py:113
  294.0 8.6 %collective-permute-done.51.refs_2_ = bf16[512,640]{1,0:T(8,128)(2,1)S(1)} collective-permute-done((bf16[512,640]{1,0:T(8,128)(2,1)S(1)}, bf16[512,640]{1,0:T(8,128)(2,1)S(1)}, u32[]{:S(2)}, u32[]{:S(2)}) %collective-permute-start.51) | collective-permute-done | bytes 655392 | tf_op jit(solution)/shard_map/ppermute | solution.py:113
  305.1 8.2 %collective-permute-done.53.refs_2_ = bf16[128,2048]{1,0:T(8,128)(2,1)S(1)} collective-permute-done((bf16[128,2048]{1,0:T(8,128)(2,1)S(1)}, bf16[128,2048]{1,0:T(8,128)(2,1)S(1)}, u32[]{:S(2)}, u32[]{:S(2)}) %collective-permute-start.53) | collective-permute-done | bytes 524320 | tf_op jit(solution)/shard_map/ppermute | solution.py:113
  321.3 13.1 %collective-permute-done.58.refs_2_ = bf16[128,2048]{1,0:T(8,128)(2,1)S(1)} collective-permute-done((bf16[128,2048]{1,0:T(8,128)(2,1)S(1)}, bf16[128,2048]{1,0:T(8,128)(2,1)S(1)}, u32[]{:S(2)}, u32[]{:S(2)}) %collective-permute-start.58) | collective-permute-done | bytes 524320 | tf_op jit(solution)/shard_map/ppermute | solution.py:113
  335.3 12.1 %collective-permute-done.55.refs_4_ = bf16[512,640]{1,0:T(8,128)(2,1)S(1)} collective-permute-done((bf16[512,640]{1,0:T(8,128)(2,1)S(1)}, bf16[512,640]{1,0:T(8,128)(2,1)S(1)}, u32[]{:S(2)}, u32[]{:S(2)}) %collective-permute-start.55) | collective-permute-done | bytes 655392 | tf_op jit(solution)/shard_map/ppermute | solution.py:113
  384.3 9.4 %attend_back.1 = (bf16[1024,768]{1,0:T(8,128)(2,1)S(1)}, f32[1,768]{1,0:T(1,128)S(1)}) custom-call(bf16[1024,256]{1,0:T(8,128)(2,1)S(1)} %copy-done.61, bf16[1024,768]{1,0:T(8,128)(2,1)S(1)} %copy-done.28, f32[16,256]{1,0:T(8,128)S(1)} %get-tuple-element.1034.sums, f32[1024,384]{1,0:T(8,128)S(1)} %convolution_add_fusion.refs_15_.table, ...), custom_call_target="tpu_custom_call" | custom-call | tf_op jit(solution)/shard_map/attend_back/pallas_call | solution.py:228
  428.9 5.5 %expand_add.3 = (bf16[128,2048]{1,0:T(8,128)(2,1)S(1)}, bf16[128,2048]{1,0:T(8,128)(2,1)S(1)}, bf16[128,2048]{1,0:T(8,128)(2,1)S(1)}, bf16[128,2048]{1,0:T(8,128)(2,1)S(1)}) custom-call(bf16[1024,768]{1,0:T(8,128)(2,1)S(1)} %get-tuple-element.1082.refs_1_.values, bf16[512,768]{1,0:T(8,128)(2,1)S(1)} %copy-done.13, ...), custom_call_target="tpu_custom_call" | custom-call | tf_op jit(solution)/shard_map/expand_add/pallas_call | solution.py:228
  448.8 9.3 %collective-permute-done.74.refs_1_ = bf16[128,2048]{1,0:T(8,128)(2,1)S(1)} collective-permute-done((bf16[128,2048]{1,0:T(8,128)(2,1)}, bf16[128,2048]{1,0:T(8,128)(2,1)S(1)}, u32[]{:S(2)}, u32[]{:S(2)}) %collective-permute-start.74) | collective-permute-done | bytes 524320 | tf_op jit(solution)/shard_map/ppermute | solution.py:113
  476.5 5.0 collective-permute-done.75.refs_2_
  481.6 5.9 %collective-permute-done.78.refs_2_ = bf16[128,2048]{1,0:T(8,128)(2,1)} collective-permute-done((bf16[128,2048]{1,0:T(8,128)(2,1)}, bf16[128,2048]{1,0:T(8,128)(2,1)}, u32[]{:S(2)}, u32[]{:S(2)}) %collective-permute-start.78) | collective-permute-done | bytes 524320 | tf_op jit(solution)/shard_map/ppermute | solution.py:113
  508.1 5.8 %all-to-all-start.6 = ((f32[8,1,448]{2,1,0:T(1,128)}), f32[8,1,448]{2,1,0:T(1,128)S(1)}, u32[]{:S(2)}, u32[]{:S(2)}) async-start(f32[8,1,448]{2,1,0:T(1,128)} %copy.97), calls=%async_computation.6 | async-start | bytes 32768 | tf_op jit(solution)/shard_map/all_to_all | solution.py:135
  (479 shorter events, 289.7 us)
Async XLA Ops:
  35.7 35.8 %collective-permute-start.6 = (bf16[512,768]{1,0:T(8,128)(2,1)S(1)}, bf16[512,768]{1,0:T(8,128)(2,1)}, u32[]{:S(2)}, u32[]{:S(2)}) collective-permute-start(bf16[512,768]{1,0:T(8,128)(2,1)S(1)} %get-tuple-element.1085.refs_8_.refs_0_), channel_id=1, source_target_pairs={{16,0},{17,1},{18,2},{19,3},{20,4},{21,5},{22,6},{23,7},{24,8},{25... | collective-permute-start | bytes 2359304 | tf_op jit(solution)/shard_map/ppermute | solution.py:113
  95.2 42.6 %all-to-all-start.2 = ((bf16[8,64,1408]{2,1,0:T(8,128)(2,1)}), bf16[8,64,1408]{2,1,0:T(8,128)(2,1)}, u32[]{:S(2)}, u32[]{:S(2)}) async-start(bf16[8,64,1408]{2,1,0:T(8,128)(2,1)} %bitcast.93), calls=%async_computation.2 | async-start | bytes 2883584 | tf_op jit(solution)/shard_map/all_to_all | solution.py:135
  99.7 33.5 %collective-permute-start.21 = (bf16[512,768]{1,0:T(8,128)(2,1)S(1)}, bf16[512,768]{1,0:T(8,128)(2,1)}, u32[]{:S(2)}, u32[]{:S(2)}) collective-permute-start(bf16[512,768]{1,0:T(8,128)(2,1)S(1)} %bitcast.85), channel_id=1, source_target_pairs={{0,4},{1,5},{2,6},{3,7},{4,0},{5,1},{6,2},{7,3},{8,12},{9,13},{10,... | collective-permute-start | bytes 2359304 | tf_op jit(solution)/shard_map/ppermute | solution.py:113
  100.3 37.5 %collective-permute-start.20 = (bf16[512,768]{1,0:T(8,128)(2,1)S(1)}, bf16[512,768]{1,0:T(8,128)(2,1)}, u32[]{:S(2)}, u32[]{:S(2)}) collective-permute-start(bf16[512,768]{1,0:T(8,128)(2,1)S(1)} %bitcast.86), channel_id=1, source_target_pairs={{16,0},{17,1},{18,2},{19,3},{20,4},{21,5},{22,6},{23,7},{24,8},{25... | collective-permute-start | bytes 2359304 | tf_op jit(solution)/shard_map/ppermute | solution.py:113
  100.5 32.7 %collective-permute-start.19 = (bf16[128,2048]{1,0:T(8,128)(2,1)}, bf16[128,2048]{1,0:T(8,128)(2,1)}, u32[]{:S(2)}, u32[]{:S(2)}) collective-permute-start(bf16[128,2048]{1,0:T(8,128)(2,1)} %collective-permute-done.1.refs_2_), channel_id=1, source_target_pairs={{0,2},{1,3},{2,0},{3,1},{4,6},{5,7},{6,4},{7,5},{8,10},{9,11},{10,... | collective-permute-start | bytes 1572872 | tf_op jit(solution)/shard_map/ppermute | solution.py:113
  148.2 33.6 %collective-permute-start.30 = (bf16[512,768]{1,0:T(8,128)(2,1)}, bf16[512,768]{1,0:T(8,128)(2,1)S(1)}, u32[]{:S(2)}, u32[]{:S(2)}) collective-permute-start(bf16[512,768]{1,0:T(8,128)(2,1)} %collective-permute-done.20.refs_10_.refs_2_), channel_id=1, source_target_pairs={{0,4},{1,5},{2,6},{3,7},{4,0},{5,1},{6,2},{7,3},{8,12},{9,13},{10,... | collective-permute-start | bytes 2359304 | tf_op jit(solution)/shard_map/ppermute | solution.py:113
  149.7 32.0 %collective-permute-start.32 = (bf16[512,640]{1,0:T(8,128)(2,1)S(1)}, bf16[512,640]{1,0:T(8,128)(2,1)S(1)}, u32[]{:S(2)}, u32[]{:S(2)}) collective-permute-start(bf16[512,640]{1,0:T(8,128)(2,1)S(1)} %get-tuple-element.826.refs_12_.refs_4_), channel_id=1, source_target_pairs={{0,4},{1,5},{2,6},{3,7},{4,0},{5,1},{6,2},{7,3},{8,12},{9,13},{10,... | collective-permute-start | bytes 1966088 | tf_op jit(solution)/shard_map/ppermute | solution.py:113
  150.2 31.5 %collective-permute-start.31 = (bf16[512,640]{1,0:T(8,128)(2,1)S(1)}, bf16[512,640]{1,0:T(8,128)(2,1)S(1)}, u32[]{:S(2)}, u32[]{:S(2)}) collective-permute-start(bf16[512,640]{1,0:T(8,128)(2,1)S(1)} %get-tuple-element.826.refs_12_.refs_4_), channel_id=1, source_target_pairs={{16,0},{17,1},{18,2},{19,3},{20,4},{21,5},{22,6},{23,7},{24,8},{25... | collective-permute-start | bytes 1966088 | tf_op jit(solution)/shard_map/ppermute | solution.py:113
  190.2 31.7 %collective-permute-start.36 = (bf16[512,768]{1,0:T(8,128)(2,1)S(1)}, bf16[512,768]{1,0:T(8,128)(2,1)S(1)}, u32[]{:S(2)}, u32[]{:S(2)}) collective-permute-start(bf16[512,768]{1,0:T(8,128)(2,1)S(1)} %get-tuple-element.924.refs_0_), channel_id=1, source_target_pairs={{0,4},{1,5},{2,6},{3,7},{4,0},{5,1},{6,2},{7,3},{8,12},{9,13},{10,... | collective-permute-start | bytes 2359304 | tf_op jit(solution)/shard_map/ppermute | solution.py:113
  191.8 35.2 %collective-permute-start.35 = (bf16[512,768]{1,0:T(8,128)(2,1)S(1)}, bf16[512,768]{1,0:T(8,128)(2,1)S(1)}, u32[]{:S(2)}, u32[]{:S(2)}) collective-permute-start(bf16[512,768]{1,0:T(8,128)(2,1)S(1)} %get-tuple-element.924.refs_0_), channel_id=1, source_target_pairs={{16,0},{17,1},{18,2},{19,3},{20,4},{21,5},{22,6},{23,7},{24,8},{25... | collective-permute-start | bytes 2359304 | tf_op jit(solution)/shard_map/ppermute | solution.py:113
  268.8 36.3 %collective-permute-start.48 = (bf16[512,768]{1,0:T(8,128)(2,1)S(1)}, bf16[512,768]{1,0:T(8,128)(2,1)S(1)}, u32[]{:S(2)}, u32[]{:S(2)}) collective-permute-start(bf16[512,768]{1,0:T(8,128)(2,1)S(1)} %grad.17), channel_id=1, source_target_pairs={{0,16},{1,17},{2,18},{3,19},{4,20},{5,21},{6,22},{7,23},{8,24},{9,... | collective-permute-start | bytes 2359304 | tf_op jit(solution)/shard_map/ppermute | solution.py:113
  268.8 36.3 %collective-permute-start.49 = (bf16[512,768]{1,0:T(8,128)(2,1)S(1)}, bf16[512,768]{1,0:T(8,128)(2,1)S(1)}, u32[]{:S(2)}, u32[]{:S(2)}) collective-permute-start(bf16[512,768]{1,0:T(8,128)(2,1)S(1)} %get-tuple-element.895), channel_id=1, source_target_pairs={{0,4},{1,5},{2,6},{3,7},{4,0},{5,1},{6,2},{7,3},{8,12},{9,13},{10,... | collective-permute-start | bytes 2359304 | tf_op jit(solution)/shard_map/ppermute | solution.py:113
  270.4 32.3 %collective-permute-start.51 = (bf16[512,640]{1,0:T(8,128)(2,1)S(1)}, bf16[512,640]{1,0:T(8,128)(2,1)S(1)}, u32[]{:S(2)}, u32[]{:S(2)}) collective-permute-start(bf16[512,640]{1,0:T(8,128)(2,1)S(1)} %get-tuple-element.897), channel_id=1, source_target_pairs={{0,4},{1,5},{2,6},{3,7},{4,0},{5,1},{6,2},{7,3},{8,12},{9,13},{10,... | collective-permute-start | bytes 1966088 | tf_op jit(solution)/shard_map/ppermute | solution.py:113
  283.3 30.0 %collective-permute-start.53 = (bf16[128,2048]{1,0:T(8,128)(2,1)S(1)}, bf16[128,2048]{1,0:T(8,128)(2,1)S(1)}, u32[]{:S(2)}, u32[]{:S(2)}) collective-permute-start(bf16[128,2048]{1,0:T(8,128)(2,1)S(1)} %add.360), channel_id=1, source_target_pairs={{0,8},{1,9},{2,10},{3,11},{4,12},{5,13},{6,14},{7,15},{8,0},{9,1},... | collective-permute-start | bytes 1572872 | tf_op jit(solution)/shard_map/ppermute | solution.py:113
  315.7 32.9 %collective-permute-start.56 = (bf16[512,768]{1,0:T(8,128)(2,1)S(1)}, bf16[512,768]{1,0:T(8,128)(2,1)S(1)}, u32[]{:S(2)}, u32[]{:S(2)}) collective-permute-start(bf16[512,768]{1,0:T(8,128)(2,1)S(1)} %get-tuple-element.964), channel_id=1, source_target_pairs={{0,4},{1,5},{2,6},{3,7},{4,0},{5,1},{6,2},{7,3},{8,12},{9,13},{10,... | collective-permute-start | bytes 2359304 | tf_op jit(solution)/shard_map/ppermute | solution.py:113
  317.2 30.1 %collective-permute-start.55 = (bf16[512,640]{1,0:T(8,128)(2,1)S(1)}, bf16[512,640]{1,0:T(8,128)(2,1)S(1)}, u32[]{:S(2)}, u32[]{:S(2)}) collective-permute-start(bf16[512,640]{1,0:T(8,128)(2,1)S(1)} %get-tuple-element.946), channel_id=1, source_target_pairs={{0,4},{1,5},{2,6},{3,7},{4,0},{5,1},{6,2},{7,3},{8,12},{9,13},{10,... | collective-permute-start | bytes 1966088 | tf_op jit(solution)/shard_map/ppermute | solution.py:113
  360.2 45.4 %all-to-all-start.3 = ((bf16[8,64,1408]{2,1,0:T(8,128)(2,1)}), bf16[8,64,1408]{2,1,0:T(8,128)(2,1)}, u32[]{:S(2)}, u32[]{:S(2)}) async-start(bf16[8,64,1408]{2,1,0:T(8,128)(2,1)} %bitcast.31), calls=%async_computation.3 | async-start | bytes 2883584 | tf_op jit(solution)/shard_map/all_to_all | solution.py:135
  364.5 41.1 %collective-permute-start.68 = (bf16[512,768]{1,0:T(8,128)(2,1)}, bf16[512,768]{1,0:T(8,128)(2,1)}, u32[]{:S(2)}, u32[]{:S(2)}) collective-permute-start(bf16[512,768]{1,0:T(8,128)(2,1)} %grad.23), channel_id=1, source_target_pairs={{0,16},{1,17},{2,18},{3,19},{4,20},{5,21},{6,22},{7,23},{8,24},{9,... | collective-permute-start | bytes 2359304 | tf_op jit(solution)/shard_map/ppermute | solution.py:113
  364.9 40.8 %collective-permute-start.69 = (bf16[512,768]{1,0:T(8,128)(2,1)}, bf16[512,768]{1,0:T(8,128)(2,1)}, u32[]{:S(2)}, u32[]{:S(2)}) collective-permute-start(bf16[512,768]{1,0:T(8,128)(2,1)} %copy-done.74), channel_id=1, source_target_pairs={{0,4},{1,5},{2,6},{3,7},{4,0},{5,1},{6,2},{7,3},{8,12},{9,13},{10,... | collective-permute-start | bytes 2359304 | tf_op jit(solution)/shard_map/ppermute | solution.py:113
  366.4 38.8 %collective-permute-start.66 = (bf16[128,2048]{1,0:T(8,128)(2,1)}, bf16[128,2048]{1,0:T(8,128)(2,1)}, u32[]{:S(2)}, u32[]{:S(2)}) collective-permute-start(bf16[128,2048]{1,0:T(8,128)(2,1)} %copy-done.79), channel_id=1, source_target_pairs={{0,2},{1,3},{2,0},{3,1},{4,6},{5,7},{6,4},{7,5},{8,10},{9,11},{10,... | collective-permute-start | bytes 1572872 | tf_op jit(solution)/shard_map/ppermute | solution.py:113
  368.2 37.4 %collective-permute-start.67 = (bf16[128,2048]{1,0:T(8,128)(2,1)}, bf16[128,2048]{1,0:T(8,128)(2,1)}, u32[]{:S(2)}, u32[]{:S(2)}) collective-permute-start(bf16[128,2048]{1,0:T(8,128)(2,1)} %copy-done.78), channel_id=1, source_target_pairs={{0,2},{1,3},{2,0},{3,1},{4,6},{5,7},{6,4},{7,5},{8,10},{9,11},{10,... | collective-permute-start | bytes 1572872 | tf_op jit(solution)/shard_map/ppermute | solution.py:113
  409.5 33.6 %all-to-all-start.4 = ((bf16[8,64,768]{2,1,0:T(8,128)(2,1)}), bf16[8,64,768]{2,1,0:T(8,128)(2,1)}, u32[]{:S(2)}, u32[]{:S(2)}) async-start(bf16[8,64,768]{2,1,0:T(8,128)(2,1)} %bitcast.92), calls=%async_computation.4 | async-start | bytes 1572864 | tf_op jit(solution)/shard_map/all_to_all | solution.py:135
  444.7 36.9 %collective-permute-start.75 = (bf16[512,768]{1,0:T(8,128)(2,1)}, bf16[512,768]{1,0:T(8,128)(2,1)S(1)}, u32[]{:S(2)}, u32[]{:S(2)}) collective-permute-start(bf16[512,768]{1,0:T(8,128)(2,1)} %copy-done.34), channel_id=1, source_target_pairs={{0,16},{1,17},{2,18},{3,19},{4,20},{5,21},{6,22},{7,23},{8,24},{9,... | collective-permute-start | bytes 2359304 | tf_op jit(solution)/shard_map/ppermute | solution.py:113
  446.8 34.8 %collective-permute-start.76 = (bf16[512,768]{1,0:T(8,128)(2,1)}, bf16[512,768]{1,0:T(8,128)(2,1)S(1)}, u32[]{:S(2)}, u32[]{:S(2)}) collective-permute-start(bf16[512,768]{1,0:T(8,128)(2,1)} %copy-done.73), channel_id=1, source_target_pairs={{0,4},{1,5},{2,6},{3,7},{4,0},{5,1},{6,2},{7,3},{8,12},{9,13},{10,... | collective-permute-start | bytes 2359304 | tf_op jit(solution)/shard_map/ppermute | solution.py:113
  (152 other events, 1816.8 us)

commit v7 on v6

--- a/solution.py
+++ b/solution.py
@@ -1053,14 +1053,6 @@
     )
     v.second_cross = grad_across(at, v.second_sent, (v.normed2, v.pair_low, 0, first))
     v.pieces = add_pieces(at, v.result_own, v.result_other)
-    v.close(at)
-    del v.first_own, v.first_sent, v.first_far, v.down_own, v.down_sent, v.down_far
-    del v.result_own, v.result_other
-
-    v.early = at.swap(v.early, at.groups)
-    v.second_far = push_all(at, v.second_cross)
-    v.second_sent += flip_all(at, v.second_made[-1:])
-    v.result_pieces = send_pieces(at, v.pieces)
     v.branch, v.attended_grad = call(
         at,
         functools.partial(attended_grad_kernel, count),
@@ -1072,6 +1064,14 @@
         out_tiles={0: rows_of((tokens, width), TILE), 1: rows_of((tokens, part), TILE)},
         name="attended_grad",
     )
+    v.close(at)
+    del v.first_own, v.first_sent, v.first_far, v.down_own, v.down_sent, v.down_far
+    del v.result_own, v.result_other
+
+    v.early = at.swap(v.early, at.groups)
+    v.second_far = push_all(at, v.second_cross)
+    v.second_sent += flip_all(at, v.second_made[-1:])
+    v.result_pieces = [*v.pieces[:3], at.flip(v.pieces[3], x=1)]
     v.out_sent = at.flip(grad_beside(at, (v.branch, v.attended, 0, part), stacked=True), e=1)
     v.mixed_low, v.bias_part = call(
         at,
@@ -1094,6 +1094,7 @@
     v.late = at.swap(add(at, [v.second_own, v.second_sent[-1], *v.second_far]), at.groups)
     v.other = at.flip(v.other, c=1)
     v.qkv_sent = flip_all(at, v.qkv_made[:-1])
+    v.result_pieces[1] = at.flip(v.result_pieces[1], x=1)
     v.result_terms = pass_pieces(at, v.result_pieces)
     v.out_sent = jnp.split(v.out_sent, at.outer)
     v.out_far = push_all(at, grad_across(at, v.out_sent, (v.branch, v.attended, 0, part)))

time: 526 us -> 523 us (level)
    unnamed x178 -> x152, local copies, waits for them, and re-layouts: 48.9 us -> 44 us
  transfers between devices with their start and end apart: 89 -> 89, of which waited for: 40 -> 39; matrix products, arithmetic and copies ran while one was open for 2% -> 2% of each run, Pallas kernels for 25% -> 25%
where the time goes in v7:
time: 523 us; the launch traced here: 516 us
  waiting for transfers between devices  218 us (42%)
  Pallas kernels  135 us (26%)
  starting transfers between devices  103 us (20%)
  local copies, waits for them, and re-layouts  50.5 us (10%)
  other arithmetic  6.31 us (1%)
    ppermute x82, waiting for transfers between devices, move(): return lax.ppermute(values, AXES, pairs)  212 us
    pallas_call x54, Pallas kernels, call(): pl.pallas_call(kernel, grid=(steps,), out_shape=[jax.ShapeDtypeStruct(sha...  135 us
    ppermute x82, starting transfers between devices, move(): return lax.ppermute(values, AXES, pairs)  74.9 us
    unnamed x152, local copies, waits for them, and re-layouts  44 us
    all_to_all x7, starting transfers between devices, swap(): lax.all_to_all(view, AXES, 0, 0, axis_index_groups=groups, tiled=True)  27.8 us
  transfers between devices with their start and end apart: 89, of which 39 were waited for; matrix products, arithmetic and copies ran while one was open for 2% of the time, Pallas kernels for 25%

profile of v7, /device:TPU:0, one launch (start us, length us, event | category | flops | bytes accessed | tf_op | source)
XLA Modules:
  0.0 516.4 jit_solution(15233603288409969099)
XLA Ops:
  40.5 10.1 %collective-permute-done.11.refs_2_ = bf16[128,2048]{1,0:T(8,128)(2,1)} collective-permute-done((bf16[128,2048]{1,0:T(8,128)(2,1)S(1)}, bf16[128,2048]{1,0:T(8,128)(2,1)}, u32[]{:S(2)}, u32[]{:S(2)}) %collective-permute-start.11) | collective-permute-done | bytes 524320 | tf_op jit(solution)/shard_map/ppermute | solution.py:113
  59.9 11.6 %collective-permute-done.6.refs_10_.refs_2_ = bf16[512,768]{1,0:T(8,128)(2,1)} collective-permute-done((bf16[512,768]{1,0:T(8,128)(2,1)S(1)}, bf16[512,768]{1,0:T(8,128)(2,1)}, u32[]{:S(2)}, u32[]{:S(2)}) %collective-permute-start.6) | collective-permute-done | bytes 786464 | tf_op jit(solution)/shard_map/ppermute | solution.py:113
  77.1 13.2 %collective-permute-done.14.refs_2_.refs_10_ = bf16[512,256]{1,0:T(8,128)(2,1)} collective-permute-done((bf16[512,256]{1,0:T(8,128)(2,1)}, bf16[512,256]{1,0:T(8,128)(2,1)}, u32[]{:S(2)}, u32[]{:S(2)}) %collective-permute-start.14) | collective-permute-done | bytes 262176 | tf_op jit(solution)/shard_map/ppermute | solution.py:113
  107.7 19.3 %attention.1 = (bf16[1024,2048]{1,0:T(8,128)(2,1)S(1)}, bf16[1024,768]{1,0:T(8,128)(2,1)S(1)}, bf16[1024,256]{1,0:T(8,128)(2,1)S(1)}, f32[16,256]{1,0:T(8,128)S(1)}) custom-call(bf16[128,2048]{1,0:T(8,128)(2,1)S(1)} %copy-done.9, bf16[128,2048]{1,0:T(8,128)(2,1)} %collective-permute-done.10.refs_1_, bf16[128,2048]{1,0:T(8,128)(2,1)} %collective-permute-done.11.refs_2_, ...), custom_call_target="tpu_custom_call" | custom-call | tf_op jit(solution)/shard_map/attention/pallas_call | solution.py:228
  150.5 10.7 %collective-permute-done.29.refs_1_ = bf16[128,2048]{1,0:T(8,128)(2,1)S(1)} collective-permute-done((bf16[128,2048]{1,0:T(8,128)(2,1)S(1)}, bf16[128,2048]{1,0:T(8,128)(2,1)S(1)}, u32[]{:S(2)}, u32[]{:S(2)}) %collective-permute-start.29) | collective-permute-done | bytes 524320 | tf_op jit(solution)/shard_map/ppermute | solution.py:113
  163.0 8.7 %collective-permute-done.33.refs_1_ = bf16[128,2048]{1,0:T(8,128)(2,1)S(1)} collective-permute-done((bf16[128,2048]{1,0:T(8,128)(2,1)S(1)}, bf16[128,2048]{1,0:T(8,128)(2,1)S(1)}, u32[]{:S(2)}, u32[]{:S(2)}) %collective-permute-start.33) | collective-permute-done | bytes 524320 | tf_op jit(solution)/shard_map/ppermute | solution.py:113
  171.7 10.0 %collective-permute-done.32.refs_13_.refs_5_ = bf16[512,640]{1,0:T(8,128)(2,1)S(1)} collective-permute-done((bf16[512,640]{1,0:T(8,128)(2,1)S(1)}, bf16[512,640]{1,0:T(8,128)(2,1)S(1)}, u32[]{:S(2)}, u32[]{:S(2)}) %collective-permute-start.32) | collective-permute-done | bytes 655392 | tf_op jit(solution)/shard_map/ppermute | solution.py:113
  181.7 6.1 %collective-permute-done.34.refs_2_ = bf16[128,2048]{1,0:T(8,128)(2,1)S(1)} collective-permute-done((bf16[128,2048]{1,0:T(8,128)(2,1)S(1)}, bf16[128,2048]{1,0:T(8,128)(2,1)S(1)}, u32[]{:S(2)}, u32[]{:S(2)}) %collective-permute-start.34) | collective-permute-done | bytes 524320 | tf_op jit(solution)/shard_map/ppermute | solution.py:113
  194.0 12.8 %collective-permute-done.39.refs_2_ = bf16[128,2048]{1,0:T(8,128)(2,1)S(1)} collective-permute-done((bf16[128,2048]{1,0:T(8,128)(2,1)S(1)}, bf16[128,2048]{1,0:T(8,128)(2,1)S(1)}, u32[]{:S(2)}, u32[]{:S(2)}) %collective-permute-start.39) | collective-permute-done | bytes 524320 | tf_op jit(solution)/shard_map/ppermute | solution.py:113
  210.4 11.4 %collective-permute-done.37.refs_15_.refs_7_ = bf16[512,640]{1,0:T(8,128)(2,1)S(1)} collective-permute-done((bf16[512,640]{1,0:T(8,128)(2,1)S(1)}, bf16[512,640]{1,0:T(8,128)(2,1)S(1)}, u32[]{:S(2)}, u32[]{:S(2)}) %collective-permute-start.37) | collective-permute-done | bytes 655392 | tf_op jit(solution)/shard_map/ppermute | solution.py:113
  230.8 10.2 %mlp.1 = (bf16[1024,2048]{1,0:T(8,128)(2,1)S(1)}, bf16[1024,768]{1,0:T(8,128)(2,1)S(1)}, f32[1024,704]{1,0:T(8,128)S(1)}, f32[1024,704]{1,0:T(8,128)S(1)}) custom-call(bf16[128,2048]{1,0:T(8,128)(2,1)S(1)} %get-tuple-element.757.refs_0_, bf16[128,2048]{1,0:T(8,128)(2,1)S(1)} %collective-permute-done.38.refs_1_, ...), custom_call_target="tpu_custom_call" | custom-call | tf_op jit(solution)/shard_map/mlp/pallas_call | solution.py:228
  250.2 5.1 expand.7
  255.3 5.0 expand.8.own
  272.5 10.7 %collective-permute-done.50.refs_1_ = bf16[128,2048]{1,0:T(8,128)(2,1)S(1)} collective-permute-done((bf16[128,2048]{1,0:T(8,128)(2,1)S(1)}, bf16[128,2048]{1,0:T(8,128)(2,1)S(1)}, u32[]{:S(2)}, u32[]{:S(2)}) %collective-permute-start.50) | collective-permute-done | bytes 524320 | tf_op jit(solution)/shard_map/ppermute | solution.py:113
  294.1 8.5 %collective-permute-done.51.refs_2_ = bf16[512,640]{1,0:T(8,128)(2,1)S(1)} collective-permute-done((bf16[512,640]{1,0:T(8,128)(2,1)S(1)}, bf16[512,640]{1,0:T(8,128)(2,1)S(1)}, u32[]{:S(2)}, u32[]{:S(2)}) %collective-permute-start.51) | collective-permute-done | bytes 655392 | tf_op jit(solution)/shard_map/ppermute | solution.py:113
  305.0 8.2 %collective-permute-done.53.refs_2_ = bf16[128,2048]{1,0:T(8,128)(2,1)S(1)} collective-permute-done((bf16[128,2048]{1,0:T(8,128)(2,1)S(1)}, bf16[128,2048]{1,0:T(8,128)(2,1)S(1)}, u32[]{:S(2)}, u32[]{:S(2)}) %collective-permute-start.53) | collective-permute-done | bytes 524320 | tf_op jit(solution)/shard_map/ppermute | solution.py:113
  321.2 13.1 %collective-permute-done.58.refs_2_ = bf16[128,2048]{1,0:T(8,128)(2,1)S(1)} collective-permute-done((bf16[128,2048]{1,0:T(8,128)(2,1)S(1)}, bf16[128,2048]{1,0:T(8,128)(2,1)S(1)}, u32[]{:S(2)}, u32[]{:S(2)}) %collective-permute-start.58) | collective-permute-done | bytes 524320 | tf_op jit(solution)/shard_map/ppermute | solution.py:113
  334.4 12.9 %collective-permute-done.55.refs_4_ = bf16[512,640]{1,0:T(8,128)(2,1)S(1)} collective-permute-done((bf16[512,640]{1,0:T(8,128)(2,1)S(1)}, bf16[512,640]{1,0:T(8,128)(2,1)S(1)}, u32[]{:S(2)}, u32[]{:S(2)}) %collective-permute-start.55) | collective-permute-done | bytes 655392 | tf_op jit(solution)/shard_map/ppermute | solution.py:113
  377.8 9.4 %attend_back.1 = (bf16[1024,768]{1,0:T(8,128)(2,1)S(1)}, f32[1,768]{1,0:T(1,128)S(1)}) custom-call(bf16[1024,256]{1,0:T(8,128)(2,1)S(1)} %copy-done.48, bf16[1024,768]{1,0:T(8,128)(2,1)S(1)} %copy-done.29, f32[16,256]{1,0:T(8,128)S(1)} %get-tuple-element.1014.sums, f32[1024,384]{1,0:T(8,128)S(1)} %convolution_add_fusion.refs_15_.table, ...), custom_call_target="tpu_custom_call" | custom-call | tf_op jit(solution)/shard_map/attend_back/pallas_call | solution.py:228
  398.7 5.4 %collective-permute-done.67.refs_2_ = bf16[512,768]{1,0:T(8,128)(2,1)} collective-permute-done((bf16[512,768]{1,0:T(8,128)(2,1)}, bf16[512,768]{1,0:T(8,128)(2,1)}, u32[]{:S(2)}, u32[]{:S(2)}) %collective-permute-start.67) | collective-permute-done | bytes 786464 | tf_op jit(solution)/shard_map/ppermute | solution.py:113
  427.7 5.5 %expand_add.3 = (bf16[128,2048]{1,0:T(8,128)(2,1)S(1)}, bf16[128,2048]{1,0:T(8,128)(2,1)S(1)}, bf16[128,2048]{1,0:T(8,128)(2,1)S(1)}, bf16[128,2048]{1,0:T(8,128)(2,1)S(1)}) custom-call(bf16[1024,768]{1,0:T(8,128)(2,1)S(1)} %get-tuple-element.1062.refs_1_.values, bf16[512,768]{1,0:T(8,128)(2,1)S(1)} %copy-done.14, ...), custom_call_target="tpu_custom_call" | custom-call | tf_op jit(solution)/shard_map/expand_add/pallas_call | solution.py:228
  448.0 8.5 %collective-permute-done.74.refs_1_ = bf16[128,2048]{1,0:T(8,128)(2,1)S(1)} collective-permute-done((bf16[128,2048]{1,0:T(8,128)(2,1)}, bf16[128,2048]{1,0:T(8,128)(2,1)S(1)}, u32[]{:S(2)}, u32[]{:S(2)}) %collective-permute-start.74) | collective-permute-done | bytes 524320 | tf_op jit(solution)/shard_map/ppermute | solution.py:113
  473.7 6.6 %collective-permute-done.75.refs_2_ = bf16[512,768]{1,0:T(8,128)(2,1)S(1)} collective-permute-done((bf16[512,768]{1,0:T(8,128)(2,1)}, bf16[512,768]{1,0:T(8,128)(2,1)S(1)}, u32[]{:S(2)}, u32[]{:S(2)}) %collective-permute-start.75) | collective-permute-done | bytes 786464 | tf_op jit(solution)/shard_map/ppermute | solution.py:113
  480.3 5.9 %collective-permute-done.78.refs_2_ = bf16[128,2048]{1,0:T(8,128)(2,1)} collective-permute-done((bf16[128,2048]{1,0:T(8,128)(2,1)}, bf16[128,2048]{1,0:T(8,128)(2,1)}, u32[]{:S(2)}, u32[]{:S(2)}) %collective-permute-start.78) | collective-permute-done | bytes 524320 | tf_op jit(solution)/shard_map/ppermute | solution.py:113
  (453 shorter events, 285.0 us)
Async XLA Ops:
  35.7 35.8 %collective-permute-start.6 = (bf16[512,768]{1,0:T(8,128)(2,1)S(1)}, bf16[512,768]{1,0:T(8,128)(2,1)}, u32[]{:S(2)}, u32[]{:S(2)}) collective-permute-start(bf16[512,768]{1,0:T(8,128)(2,1)S(1)} %get-tuple-element.1065.refs_8_.refs_0_), channel_id=1, source_target_pairs={{16,0},{17,1},{18,2},{19,3},{20,4},{21,5},{22,6},{23,7},{24,8},{25... | collective-permute-start | bytes 2359304 | tf_op jit(solution)/shard_map/ppermute | solution.py:113
  95.2 42.6 %all-to-all-start.2 = ((bf16[8,64,1408]{2,1,0:T(8,128)(2,1)}), bf16[8,64,1408]{2,1,0:T(8,128)(2,1)}, u32[]{:S(2)}, u32[]{:S(2)}) async-start(bf16[8,64,1408]{2,1,0:T(8,128)(2,1)} %bitcast.93), calls=%async_computation.2 | async-start | bytes 2883584 | tf_op jit(solution)/shard_map/all_to_all | solution.py:135
  99.7 33.5 %collective-permute-start.21 = (bf16[512,768]{1,0:T(8,128)(2,1)S(1)}, bf16[512,768]{1,0:T(8,128)(2,1)}, u32[]{:S(2)}, u32[]{:S(2)}) collective-permute-start(bf16[512,768]{1,0:T(8,128)(2,1)S(1)} %bitcast.85), channel_id=1, source_target_pairs={{0,4},{1,5},{2,6},{3,7},{4,0},{5,1},{6,2},{7,3},{8,12},{9,13},{10,... | collective-permute-start | bytes 2359304 | tf_op jit(solution)/shard_map/ppermute | solution.py:113
  100.3 37.5 %collective-permute-start.20 = (bf16[512,768]{1,0:T(8,128)(2,1)S(1)}, bf16[512,768]{1,0:T(8,128)(2,1)}, u32[]{:S(2)}, u32[]{:S(2)}) collective-permute-start(bf16[512,768]{1,0:T(8,128)(2,1)S(1)} %bitcast.86), channel_id=1, source_target_pairs={{16,0},{17,1},{18,2},{19,3},{20,4},{21,5},{22,6},{23,7},{24,8},{25... | collective-permute-start | bytes 2359304 | tf_op jit(solution)/shard_map/ppermute | solution.py:113
  100.5 32.7 %collective-permute-start.19 = (bf16[128,2048]{1,0:T(8,128)(2,1)}, bf16[128,2048]{1,0:T(8,128)(2,1)}, u32[]{:S(2)}, u32[]{:S(2)}) collective-permute-start(bf16[128,2048]{1,0:T(8,128)(2,1)} %collective-permute-done.1.refs_2_), channel_id=1, source_target_pairs={{0,2},{1,3},{2,0},{3,1},{4,6},{5,7},{6,4},{7,5},{8,10},{9,11},{10,... | collective-permute-start | bytes 1572872 | tf_op jit(solution)/shard_map/ppermute | solution.py:113
  148.2 33.5 %collective-permute-start.30 = (bf16[512,768]{1,0:T(8,128)(2,1)}, bf16[512,768]{1,0:T(8,128)(2,1)S(1)}, u32[]{:S(2)}, u32[]{:S(2)}) collective-permute-start(bf16[512,768]{1,0:T(8,128)(2,1)} %collective-permute-done.20.refs_10_.refs_2_), channel_id=1, source_target_pairs={{0,4},{1,5},{2,6},{3,7},{4,0},{5,1},{6,2},{7,3},{8,12},{9,13},{10,... | collective-permute-start | bytes 2359304 | tf_op jit(solution)/shard_map/ppermute | solution.py:113
  149.7 32.0 %collective-permute-start.32 = (bf16[512,640]{1,0:T(8,128)(2,1)S(1)}, bf16[512,640]{1,0:T(8,128)(2,1)S(1)}, u32[]{:S(2)}, u32[]{:S(2)}) collective-permute-start(bf16[512,640]{1,0:T(8,128)(2,1)S(1)} %get-tuple-element.816.refs_12_.refs_4_), channel_id=1, source_target_pairs={{0,4},{1,5},{2,6},{3,7},{4,0},{5,1},{6,2},{7,3},{8,12},{9,13},{10,... | collective-permute-start | bytes 1966088 | tf_op jit(solution)/shard_map/ppermute | solution.py:113
  150.2 31.5 %collective-permute-start.31 = (bf16[512,640]{1,0:T(8,128)(2,1)S(1)}, bf16[512,640]{1,0:T(8,128)(2,1)S(1)}, u32[]{:S(2)}, u32[]{:S(2)}) collective-permute-start(bf16[512,640]{1,0:T(8,128)(2,1)S(1)} %get-tuple-element.816.refs_12_.refs_4_), channel_id=1, source_target_pairs={{16,0},{17,1},{18,2},{19,3},{20,4},{21,5},{22,6},{23,7},{24,8},{25... | collective-permute-start | bytes 1966088 | tf_op jit(solution)/shard_map/ppermute | solution.py:113
  190.2 31.7 %collective-permute-start.36 = (bf16[512,768]{1,0:T(8,128)(2,1)S(1)}, bf16[512,768]{1,0:T(8,128)(2,1)S(1)}, u32[]{:S(2)}, u32[]{:S(2)}) collective-permute-start(bf16[512,768]{1,0:T(8,128)(2,1)S(1)} %get-tuple-element.914.refs_0_), channel_id=1, source_target_pairs={{0,4},{1,5},{2,6},{3,7},{4,0},{5,1},{6,2},{7,3},{8,12},{9,13},{10,... | collective-permute-start | bytes 2359304 | tf_op jit(solution)/shard_map/ppermute | solution.py:113
  191.7 35.1 %collective-permute-start.35 = (bf16[512,768]{1,0:T(8,128)(2,1)S(1)}, bf16[512,768]{1,0:T(8,128)(2,1)S(1)}, u32[]{:S(2)}, u32[]{:S(2)}) collective-permute-start(bf16[512,768]{1,0:T(8,128)(2,1)S(1)} %get-tuple-element.914.refs_0_), channel_id=1, source_target_pairs={{16,0},{17,1},{18,2},{19,3},{20,4},{21,5},{22,6},{23,7},{24,8},{25... | collective-permute-start | bytes 2359304 | tf_op jit(solution)/shard_map/ppermute | solution.py:113
  193.5 28.4 %collective-permute-start.37 = (bf16[512,640]{1,0:T(8,128)(2,1)S(1)}, bf16[512,640]{1,0:T(8,128)(2,1)S(1)}, u32[]{:S(2)}, u32[]{:S(2)}) collective-permute-start(bf16[512,640]{1,0:T(8,128)(2,1)S(1)} %collective-permute-done.31.refs_14_.refs_6_), channel_id=1, source_target_pairs={{0,4},{1,5},{2,6},{3,7},{4,0},{5,1},{6,2},{7,3},{8,12},{9,13},{10,... | collective-permute-start | bytes 1966088 | tf_op jit(solution)/shard_map/ppermute | solution.py:113
  268.8 36.3 %collective-permute-start.48 = (bf16[512,768]{1,0:T(8,128)(2,1)S(1)}, bf16[512,768]{1,0:T(8,128)(2,1)S(1)}, u32[]{:S(2)}, u32[]{:S(2)}) collective-permute-start(bf16[512,768]{1,0:T(8,128)(2,1)S(1)} %grad.17), channel_id=1, source_target_pairs={{0,16},{1,17},{2,18},{3,19},{4,20},{5,21},{6,22},{7,23},{8,24},{9,... | collective-permute-start | bytes 2359304 | tf_op jit(solution)/shard_map/ppermute | solution.py:113
  268.8 36.3 %collective-permute-start.49 = (bf16[512,768]{1,0:T(8,128)(2,1)S(1)}, bf16[512,768]{1,0:T(8,128)(2,1)S(1)}, u32[]{:S(2)}, u32[]{:S(2)}) collective-permute-start(bf16[512,768]{1,0:T(8,128)(2,1)S(1)} %get-tuple-element.885), channel_id=1, source_target_pairs={{0,4},{1,5},{2,6},{3,7},{4,0},{5,1},{6,2},{7,3},{8,12},{9,13},{10,... | collective-permute-start | bytes 2359304 | tf_op jit(solution)/shard_map/ppermute | solution.py:113
  270.3 32.3 %collective-permute-start.51 = (bf16[512,640]{1,0:T(8,128)(2,1)S(1)}, bf16[512,640]{1,0:T(8,128)(2,1)S(1)}, u32[]{:S(2)}, u32[]{:S(2)}) collective-permute-start(bf16[512,640]{1,0:T(8,128)(2,1)S(1)} %get-tuple-element.887), channel_id=1, source_target_pairs={{0,4},{1,5},{2,6},{3,7},{4,0},{5,1},{6,2},{7,3},{8,12},{9,13},{10,... | collective-permute-start | bytes 1966088 | tf_op jit(solution)/shard_map/ppermute | solution.py:113
  283.2 30.0 %collective-permute-start.53 = (bf16[128,2048]{1,0:T(8,128)(2,1)S(1)}, bf16[128,2048]{1,0:T(8,128)(2,1)S(1)}, u32[]{:S(2)}, u32[]{:S(2)}) collective-permute-start(bf16[128,2048]{1,0:T(8,128)(2,1)S(1)} %add.360), channel_id=1, source_target_pairs={{0,8},{1,9},{2,10},{3,11},{4,12},{5,13},{6,14},{7,15},{8,0},{9,1},... | collective-permute-start | bytes 1572872 | tf_op jit(solution)/shard_map/ppermute | solution.py:113
  315.7 32.9 %collective-permute-start.56 = (bf16[512,768]{1,0:T(8,128)(2,1)S(1)}, bf16[512,768]{1,0:T(8,128)(2,1)S(1)}, u32[]{:S(2)}, u32[]{:S(2)}) collective-permute-start(bf16[512,768]{1,0:T(8,128)(2,1)S(1)} %get-tuple-element.954), channel_id=1, source_target_pairs={{0,4},{1,5},{2,6},{3,7},{4,0},{5,1},{6,2},{7,3},{8,12},{9,13},{10,... | collective-permute-start | bytes 2359304 | tf_op jit(solution)/shard_map/ppermute | solution.py:113
  317.2 30.1 %collective-permute-start.55 = (bf16[512,640]{1,0:T(8,128)(2,1)S(1)}, bf16[512,640]{1,0:T(8,128)(2,1)S(1)}, u32[]{:S(2)}, u32[]{:S(2)}) collective-permute-start(bf16[512,640]{1,0:T(8,128)(2,1)S(1)} %get-tuple-element.936), channel_id=1, source_target_pairs={{0,4},{1,5},{2,6},{3,7},{4,0},{5,1},{6,2},{7,3},{8,12},{9,13},{10,... | collective-permute-start | bytes 1966088 | tf_op jit(solution)/shard_map/ppermute | solution.py:113
  319.3 29.3 %collective-permute-start.54 = (bf16[512,640]{1,0:T(8,128)(2,1)S(1)}, bf16[512,640]{1,0:T(8,128)(2,1)S(1)}, u32[]{:S(2)}, u32[]{:S(2)}) collective-permute-start(bf16[512,640]{1,0:T(8,128)(2,1)S(1)} %grad.22), channel_id=1, source_target_pairs={{0,16},{1,17},{2,18},{3,19},{4,20},{5,21},{6,22},{7,23},{8,24},{9,... | collective-permute-start | bytes 1966088 | tf_op jit(solution)/shard_map/ppermute | solution.py:113
  361.7 42.4 %all-to-all-start.3 = ((bf16[8,64,1408]{2,1,0:T(8,128)(2,1)}), bf16[8,64,1408]{2,1,0:T(8,128)(2,1)}, u32[]{:S(2)}, u32[]{:S(2)}) async-start(bf16[8,64,1408]{2,1,0:T(8,128)(2,1)} %bitcast.31), calls=%async_computation.3 | async-start | bytes 2883584 | tf_op jit(solution)/shard_map/all_to_all | solution.py:135
  366.1 37.9 %collective-permute-start.67 = (bf16[512,768]{1,0:T(8,128)(2,1)}, bf16[512,768]{1,0:T(8,128)(2,1)}, u32[]{:S(2)}, u32[]{:S(2)}) collective-permute-start(bf16[512,768]{1,0:T(8,128)(2,1)} %grad.23), channel_id=1, source_target_pairs={{0,16},{1,17},{2,18},{3,19},{4,20},{5,21},{6,22},{7,23},{8,24},{9,... | collective-permute-start | bytes 2359304 | tf_op jit(solution)/shard_map/ppermute | solution.py:113
  366.5 37.6 %collective-permute-start.68 = (bf16[512,768]{1,0:T(8,128)(2,1)}, bf16[512,768]{1,0:T(8,128)(2,1)}, u32[]{:S(2)}, u32[]{:S(2)}) collective-permute-start(bf16[512,768]{1,0:T(8,128)(2,1)} %get-tuple-element.1039), channel_id=1, source_target_pairs={{0,4},{1,5},{2,6},{3,7},{4,0},{5,1},{6,2},{7,3},{8,12},{9,13},{10,... | collective-permute-start | bytes 2359304 | tf_op jit(solution)/shard_map/ppermute | solution.py:113
  407.9 33.6 %all-to-all-start.4 = ((bf16[8,64,768]{2,1,0:T(8,128)(2,1)}), bf16[8,64,768]{2,1,0:T(8,128)(2,1)}, u32[]{:S(2)}, u32[]{:S(2)}) async-start(bf16[8,64,768]{2,1,0:T(8,128)(2,1)} %bitcast.92), calls=%async_computation.4 | async-start | bytes 1572864 | tf_op jit(solution)/shard_map/all_to_all | solution.py:135
  443.1 37.2 %collective-permute-start.75 = (bf16[512,768]{1,0:T(8,128)(2,1)}, bf16[512,768]{1,0:T(8,128)(2,1)S(1)}, u32[]{:S(2)}, u32[]{:S(2)}) collective-permute-start(bf16[512,768]{1,0:T(8,128)(2,1)} %copy-done.35), channel_id=1, source_target_pairs={{0,16},{1,17},{2,18},{3,19},{4,20},{5,21},{6,22},{7,23},{8,24},{9,... | collective-permute-start | bytes 2359304 | tf_op jit(solution)/shard_map/ppermute | solution.py:113
  446.0 34.2 %collective-permute-start.76 = (bf16[512,768]{1,0:T(8,128)(2,1)}, bf16[512,768]{1,0:T(8,128)(2,1)S(1)}, u32[]{:S(2)}, u32[]{:S(2)}) collective-permute-start(bf16[512,768]{1,0:T(8,128)(2,1)} %copy-done.62), channel_id=1, source_target_pairs={{0,4},{1,5},{2,6},{3,7},{4,0},{5,1},{6,2},{7,3},{8,12},{9,13},{10,... | collective-permute-start | bytes 2359304 | tf_op jit(solution)/shard_map/ppermute | solution.py:113
  (139 other events, 1756.4 us)

commit v8 on v7

--- a/solution.py
+++ b/solution.py
@@ -1064,6 +1064,7 @@
         out_tiles={0: rows_of((tokens, width), TILE), 1: rows_of((tokens, part), TILE)},
         name="attended_grad",
     )
+    v.out_made = grad_beside(at, (v.branch, v.attended, 0, part), stacked=True)
     v.close(at)
     del v.first_own, v.first_sent, v.first_far, v.down_own, v.down_sent, v.down_far
     del v.result_own, v.result_other
@@ -1072,7 +1073,7 @@
     v.second_far = push_all(at, v.second_cross)
     v.second_sent += flip_all(at, v.second_made[-1:])
     v.result_pieces = [*v.pieces[:3], at.flip(v.pieces[3], x=1)]
-    v.out_sent = at.flip(grad_beside(at, (v.branch, v.attended, 0, part), stacked=True), e=1)
+    v.out_sent = at.flip(v.out_made, e=1)
     v.mixed_low, v.bias_part = call(
         at,
         attend_back_kernel,

time: 523 us -> 523 us (level)
    unnamed x152 -> x150, local copies, waits for them, and re-layouts: 44 us -> 39 us
  transfers between devices with their start and end apart: 89 -> 89, of which waited for: 39 -> 40; matrix products, arithmetic and copies ran while one was open for 2% -> 2% of each run, Pallas kernels for 25% -> 24%
where the time goes in v8:
time: 523 us; the launch traced here: 517 us
  waiting for transfers between devices  223 us (43%)
  Pallas kernels  136 us (26%)
  starting transfers between devices  103 us (20%)
  local copies, waits for them, and re-layouts  45.5 us (9%)
  other arithmetic  6.31 us (1%)
    ppermute x82, waiting for transfers between devices, move(): return lax.ppermute(values, AXES, pairs)  217 us
    pallas_call x54, Pallas kernels, call(): pl.pallas_call(kernel, grid=(steps,), out_shape=[jax.ShapeDtypeStruct(sha...  136 us
    ppermute x82, starting transfers between devices, move(): return lax.ppermute(values, AXES, pairs)  74.9 us
    unnamed x150, local copies, waits for them, and re-layouts  39 us
    all_to_all x7, starting transfers between devices, swap(): lax.all_to_all(view, AXES, 0, 0, axis_index_groups=groups, tiled=True)  27.7 us
  transfers between devices with their start and end apart: 89, of which 40 were waited for; matrix products, arithmetic and copies ran while one was open for 2% of the time, Pallas kernels for 24%

profile of v8, /device:TPU:0, one launch (start us, length us, event | category | flops | bytes accessed | tf_op | source)
XLA Modules:
  0.0 516.8 jit_solution(2330571438695890629)
XLA Ops:
  40.5 10.1 %collective-permute-done.11.refs_2_ = bf16[128,2048]{1,0:T(8,128)(2,1)} collective-permute-done((bf16[128,2048]{1,0:T(8,128)(2,1)S(1)}, bf16[128,2048]{1,0:T(8,128)(2,1)}, u32[]{:S(2)}, u32[]{:S(2)}) %collective-permute-start.11) | collective-permute-done | bytes 524320 | tf_op jit(solution)/shard_map/ppermute | solution.py:113
  59.9 11.6 %collective-permute-done.6.refs_10_.refs_2_ = bf16[512,768]{1,0:T(8,128)(2,1)} collective-permute-done((bf16[512,768]{1,0:T(8,128)(2,1)S(1)}, bf16[512,768]{1,0:T(8,128)(2,1)}, u32[]{:S(2)}, u32[]{:S(2)}) %collective-permute-start.6) | collective-permute-done | bytes 786464 | tf_op jit(solution)/shard_map/ppermute | solution.py:113
  77.1 13.2 %collective-permute-done.14.refs_2_.refs_10_ = bf16[512,256]{1,0:T(8,128)(2,1)} collective-permute-done((bf16[512,256]{1,0:T(8,128)(2,1)}, bf16[512,256]{1,0:T(8,128)(2,1)}, u32[]{:S(2)}, u32[]{:S(2)}) %collective-permute-start.14) | collective-permute-done | bytes 262176 | tf_op jit(solution)/shard_map/ppermute | solution.py:113
  107.7 19.3 %attention.1 = (bf16[1024,2048]{1,0:T(8,128)(2,1)S(1)}, bf16[1024,768]{1,0:T(8,128)(2,1)S(1)}, bf16[1024,256]{1,0:T(8,128)(2,1)S(1)}, f32[16,256]{1,0:T(8,128)S(1)}) custom-call(bf16[128,2048]{1,0:T(8,128)(2,1)S(1)} %copy-done.8, bf16[128,2048]{1,0:T(8,128)(2,1)} %collective-permute-done.10.refs_1_, bf16[128,2048]{1,0:T(8,128)(2,1)} %collective-permute-done.11.refs_2_, ...), custom_call_target="tpu_custom_call" | custom-call | tf_op jit(solution)/shard_map/attention/pallas_call | solution.py:228
  150.6 10.7 %collective-permute-done.29.refs_1_ = bf16[128,2048]{1,0:T(8,128)(2,1)S(1)} collective-permute-done((bf16[128,2048]{1,0:T(8,128)(2,1)S(1)}, bf16[128,2048]{1,0:T(8,128)(2,1)S(1)}, u32[]{:S(2)}, u32[]{:S(2)}) %collective-permute-start.29) | collective-permute-done | bytes 524320 | tf_op jit(solution)/shard_map/ppermute | solution.py:113
  163.0 8.7 %collective-permute-done.33.refs_1_ = bf16[128,2048]{1,0:T(8,128)(2,1)S(1)} collective-permute-done((bf16[128,2048]{1,0:T(8,128)(2,1)S(1)}, bf16[128,2048]{1,0:T(8,128)(2,1)S(1)}, u32[]{:S(2)}, u32[]{:S(2)}) %collective-permute-start.33) | collective-permute-done | bytes 524320 | tf_op jit(solution)/shard_map/ppermute | solution.py:113
  171.7 10.0 %collective-permute-done.32.refs_13_.refs_5_ = bf16[512,640]{1,0:T(8,128)(2,1)S(1)} collective-permute-done((bf16[512,640]{1,0:T(8,128)(2,1)S(1)}, bf16[512,640]{1,0:T(8,128)(2,1)S(1)}, u32[]{:S(2)}, u32[]{:S(2)}) %collective-permute-start.32) | collective-permute-done | bytes 655392 | tf_op jit(solution)/shard_map/ppermute | solution.py:113
  181.7 6.0 %collective-permute-done.34.refs_2_ = bf16[128,2048]{1,0:T(8,128)(2,1)S(1)} collective-permute-done((bf16[128,2048]{1,0:T(8,128)(2,1)S(1)}, bf16[128,2048]{1,0:T(8,128)(2,1)S(1)}, u32[]{:S(2)}, u32[]{:S(2)}) %collective-permute-start.34) | collective-permute-done | bytes 524320 | tf_op jit(solution)/shard_map/ppermute | solution.py:113
  194.0 12.8 %collective-permute-done.39.refs_2_ = bf16[128,2048]{1,0:T(8,128)(2,1)S(1)} collective-permute-done((bf16[128,2048]{1,0:T(8,128)(2,1)S(1)}, bf16[128,2048]{1,0:T(8,128)(2,1)S(1)}, u32[]{:S(2)}, u32[]{:S(2)}) %collective-permute-start.39) | collective-permute-done | bytes 524320 | tf_op jit(solution)/shard_map/ppermute | solution.py:113
  210.5 11.4 %collective-permute-done.37.refs_15_.refs_7_ = bf16[512,640]{1,0:T(8,128)(2,1)S(1)} collective-permute-done((bf16[512,640]{1,0:T(8,128)(2,1)S(1)}, bf16[512,640]{1,0:T(8,128)(2,1)S(1)}, u32[]{:S(2)}, u32[]{:S(2)}) %collective-permute-start.37) | collective-permute-done | bytes 655392 | tf_op jit(solution)/shard_map/ppermute | solution.py:113
  230.9 10.2 %mlp.1 = (bf16[1024,2048]{1,0:T(8,128)(2,1)S(1)}, bf16[1024,768]{1,0:T(8,128)(2,1)S(1)}, f32[1024,704]{1,0:T(8,128)S(1)}, f32[1024,704]{1,0:T(8,128)S(1)}) custom-call(bf16[128,2048]{1,0:T(8,128)(2,1)S(1)} %get-tuple-element.758.refs_0_, bf16[128,2048]{1,0:T(8,128)(2,1)S(1)} %collective-permute-done.38.refs_1_, ...), custom_call_target="tpu_custom_call" | custom-call | tf_op jit(solution)/shard_map/mlp/pallas_call | solution.py:228
  250.2 5.1 expand.7
  255.3 5.0 expand.8.own
  272.6 10.7 %collective-permute-done.50.refs_1_ = bf16[128,2048]{1,0:T(8,128)(2,1)S(1)} collective-permute-done((bf16[128,2048]{1,0:T(8,128)(2,1)S(1)}, bf16[128,2048]{1,0:T(8,128)(2,1)S(1)}, u32[]{:S(2)}, u32[]{:S(2)}) %collective-permute-start.50) | collective-permute-done | bytes 524320 | tf_op jit(solution)/shard_map/ppermute | solution.py:113
  294.2 8.5 %collective-permute-done.51.refs_2_ = bf16[512,640]{1,0:T(8,128)(2,1)S(1)} collective-permute-done((bf16[512,640]{1,0:T(8,128)(2,1)S(1)}, bf16[512,640]{1,0:T(8,128)(2,1)S(1)}, u32[]{:S(2)}, u32[]{:S(2)}) %collective-permute-start.51) | collective-permute-done | bytes 655392 | tf_op jit(solution)/shard_map/ppermute | solution.py:113
  305.2 8.2 %collective-permute-done.53.refs_2_ = bf16[128,2048]{1,0:T(8,128)(2,1)S(1)} collective-permute-done((bf16[128,2048]{1,0:T(8,128)(2,1)S(1)}, bf16[128,2048]{1,0:T(8,128)(2,1)S(1)}, u32[]{:S(2)}, u32[]{:S(2)}) %collective-permute-start.53) | collective-permute-done | bytes 524320 | tf_op jit(solution)/shard_map/ppermute | solution.py:113
  321.3 13.2 %collective-permute-done.58.refs_2_ = bf16[128,2048]{1,0:T(8,128)(2,1)S(1)} collective-permute-done((bf16[128,2048]{1,0:T(8,128)(2,1)S(1)}, bf16[128,2048]{1,0:T(8,128)(2,1)S(1)}, u32[]{:S(2)}, u32[]{:S(2)}) %collective-permute-start.58) | collective-permute-done | bytes 524320 | tf_op jit(solution)/shard_map/ppermute | solution.py:113
  334.5 12.9 %collective-permute-done.55.refs_4_ = bf16[512,640]{1,0:T(8,128)(2,1)S(1)} collective-permute-done((bf16[512,640]{1,0:T(8,128)(2,1)S(1)}, bf16[512,640]{1,0:T(8,128)(2,1)S(1)}, u32[]{:S(2)}, u32[]{:S(2)}) %collective-permute-start.55) | collective-permute-done | bytes 655392 | tf_op jit(solution)/shard_map/ppermute | solution.py:113
  373.4 9.5 %attend_back.1 = (bf16[1024,768]{1,0:T(8,128)(2,1)S(1)}, f32[1,768]{1,0:T(1,128)S(1)}) custom-call(bf16[1024,256]{1,0:T(8,128)(2,1)S(1)} %copy-done.47, bf16[1024,768]{1,0:T(8,128)(2,1)S(1)} %copy-done.28, f32[16,256]{1,0:T(8,128)S(1)} %get-tuple-element.1014.sums, f32[1024,384]{1,0:T(8,128)S(1)} %convolution_add_fusion.refs_15_.table, ...), custom_call_target="tpu_custom_call" | custom-call | tf_op jit(solution)/shard_map/attend_back/pallas_call | solution.py:228
  398.1 6.5 %collective-permute-done.67.refs_2_ = bf16[512,768]{1,0:T(8,128)(2,1)} collective-permute-done((bf16[512,768]{1,0:T(8,128)(2,1)}, bf16[512,768]{1,0:T(8,128)(2,1)}, u32[]{:S(2)}, u32[]{:S(2)}) %collective-permute-start.67) | collective-permute-done | bytes 786464 | tf_op jit(solution)/shard_map/ppermute | solution.py:113
  428.1 5.5 %expand_add.3 = (bf16[128,2048]{1,0:T(8,128)(2,1)S(1)}, bf16[128,2048]{1,0:T(8,128)(2,1)S(1)}, bf16[128,2048]{1,0:T(8,128)(2,1)S(1)}, bf16[128,2048]{1,0:T(8,128)(2,1)S(1)}) custom-call(bf16[1024,768]{1,0:T(8,128)(2,1)S(1)} %get-tuple-element.1064.refs_1_.values, bf16[512,768]{1,0:T(8,128)(2,1)S(1)} %copy-done.13, ...), custom_call_target="tpu_custom_call" | custom-call | tf_op jit(solution)/shard_map/expand_add/pallas_call | solution.py:228
  448.4 8.6 %collective-permute-done.74.refs_1_ = bf16[128,2048]{1,0:T(8,128)(2,1)S(1)} collective-permute-done((bf16[128,2048]{1,0:T(8,128)(2,1)}, bf16[128,2048]{1,0:T(8,128)(2,1)S(1)}, u32[]{:S(2)}, u32[]{:S(2)}) %collective-permute-start.74) | collective-permute-done | bytes 524320 | tf_op jit(solution)/shard_map/ppermute | solution.py:113
  474.2 6.6 %collective-permute-done.75.refs_2_ = bf16[512,768]{1,0:T(8,128)(2,1)S(1)} collective-permute-done((bf16[512,768]{1,0:T(8,128)(2,1)}, bf16[512,768]{1,0:T(8,128)(2,1)S(1)}, u32[]{:S(2)}, u32[]{:S(2)}) %collective-permute-start.75) | collective-permute-done | bytes 786464 | tf_op jit(solution)/shard_map/ppermute | solution.py:113
  480.8 5.9 %collective-permute-done.78.refs_2_ = bf16[128,2048]{1,0:T(8,128)(2,1)} collective-permute-done((bf16[128,2048]{1,0:T(8,128)(2,1)}, bf16[128,2048]{1,0:T(8,128)(2,1)}, u32[]{:S(2)}, u32[]{:S(2)}) %collective-permute-start.78) | collective-permute-done | bytes 524320 | tf_op jit(solution)/shard_map/ppermute | solution.py:113
  (451 shorter events, 284.3 us)
Async XLA Ops:
  35.7 35.8 %collective-permute-start.6 = (bf16[512,768]{1,0:T(8,128)(2,1)S(1)}, bf16[512,768]{1,0:T(8,128)(2,1)}, u32[]{:S(2)}, u32[]{:S(2)}) collective-permute-start(bf16[512,768]{1,0:T(8,128)(2,1)S(1)} %get-tuple-element.1067.refs_8_.refs_0_), channel_id=1, source_target_pairs={{16,0},{17,1},{18,2},{19,3},{20,4},{21,5},{22,6},{23,7},{24,8},{25... | collective-permute-start | bytes 2359304 | tf_op jit(solution)/shard_map/ppermute | solution.py:113
  95.2 42.6 %all-to-all-start.2 = ((bf16[8,64,1408]{2,1,0:T(8,128)(2,1)}), bf16[8,64,1408]{2,1,0:T(8,128)(2,1)}, u32[]{:S(2)}, u32[]{:S(2)}) async-start(bf16[8,64,1408]{2,1,0:T(8,128)(2,1)} %bitcast.93), calls=%async_computation.2 | async-start | bytes 2883584 | tf_op jit(solution)/shard_map/all_to_all | solution.py:135
  99.7 33.5 %collective-permute-start.21 = (bf16[512,768]{1,0:T(8,128)(2,1)S(1)}, bf16[512,768]{1,0:T(8,128)(2,1)}, u32[]{:S(2)}, u32[]{:S(2)}) collective-permute-start(bf16[512,768]{1,0:T(8,128)(2,1)S(1)} %bitcast.85), channel_id=1, source_target_pairs={{0,4},{1,5},{2,6},{3,7},{4,0},{5,1},{6,2},{7,3},{8,12},{9,13},{10,... | collective-permute-start | bytes 2359304 | tf_op jit(solution)/shard_map/ppermute | solution.py:113
  100.3 37.5 %collective-permute-start.20 = (bf16[512,768]{1,0:T(8,128)(2,1)S(1)}, bf16[512,768]{1,0:T(8,128)(2,1)}, u32[]{:S(2)}, u32[]{:S(2)}) collective-permute-start(bf16[512,768]{1,0:T(8,128)(2,1)S(1)} %bitcast.86), channel_id=1, source_target_pairs={{16,0},{17,1},{18,2},{19,3},{20,4},{21,5},{22,6},{23,7},{24,8},{25... | collective-permute-start | bytes 2359304 | tf_op jit(solution)/shard_map/ppermute | solution.py:113
  100.5 32.7 %collective-permute-start.19 = (bf16[128,2048]{1,0:T(8,128)(2,1)}, bf16[128,2048]{1,0:T(8,128)(2,1)}, u32[]{:S(2)}, u32[]{:S(2)}) collective-permute-start(bf16[128,2048]{1,0:T(8,128)(2,1)} %collective-permute-done.1.refs_2_), channel_id=1, source_target_pairs={{0,2},{1,3},{2,0},{3,1},{4,6},{5,7},{6,4},{7,5},{8,10},{9,11},{10,... | collective-permute-start | bytes 1572872 | tf_op jit(solution)/shard_map/ppermute | solution.py:113
  148.1 33.6 %collective-permute-start.30 = (bf16[512,768]{1,0:T(8,128)(2,1)}, bf16[512,768]{1,0:T(8,128)(2,1)S(1)}, u32[]{:S(2)}, u32[]{:S(2)}) collective-permute-start(bf16[512,768]{1,0:T(8,128)(2,1)} %collective-permute-done.20.refs_10_.refs_2_), channel_id=1, source_target_pairs={{0,4},{1,5},{2,6},{3,7},{4,0},{5,1},{6,2},{7,3},{8,12},{9,13},{10,... | collective-permute-start | bytes 2359304 | tf_op jit(solution)/shard_map/ppermute | solution.py:113
  149.7 32.0 %collective-permute-start.32 = (bf16[512,640]{1,0:T(8,128)(2,1)S(1)}, bf16[512,640]{1,0:T(8,128)(2,1)S(1)}, u32[]{:S(2)}, u32[]{:S(2)}) collective-permute-start(bf16[512,640]{1,0:T(8,128)(2,1)S(1)} %get-tuple-element.817.refs_12_.refs_4_), channel_id=1, source_target_pairs={{0,4},{1,5},{2,6},{3,7},{4,0},{5,1},{6,2},{7,3},{8,12},{9,13},{10,... | collective-permute-start | bytes 1966088 | tf_op jit(solution)/shard_map/ppermute | solution.py:113
  150.2 31.6 %collective-permute-start.31 = (bf16[512,640]{1,0:T(8,128)(2,1)S(1)}, bf16[512,640]{1,0:T(8,128)(2,1)S(1)}, u32[]{:S(2)}, u32[]{:S(2)}) collective-permute-start(bf16[512,640]{1,0:T(8,128)(2,1)S(1)} %get-tuple-element.817.refs_12_.refs_4_), channel_id=1, source_target_pairs={{16,0},{17,1},{18,2},{19,3},{20,4},{21,5},{22,6},{23,7},{24,8},{25... | collective-permute-start | bytes 1966088 | tf_op jit(solution)/shard_map/ppermute | solution.py:113
  190.2 31.7 %collective-permute-start.36 = (bf16[512,768]{1,0:T(8,128)(2,1)S(1)}, bf16[512,768]{1,0:T(8,128)(2,1)S(1)}, u32[]{:S(2)}, u32[]{:S(2)}) collective-permute-start(bf16[512,768]{1,0:T(8,128)(2,1)S(1)} %get-tuple-element.915.refs_0_), channel_id=1, source_target_pairs={{0,4},{1,5},{2,6},{3,7},{4,0},{5,1},{6,2},{7,3},{8,12},{9,13},{10,... | collective-permute-start | bytes 2359304 | tf_op jit(solution)/shard_map/ppermute | solution.py:113
  191.7 35.2 %collective-permute-start.35 = (bf16[512,768]{1,0:T(8,128)(2,1)S(1)}, bf16[512,768]{1,0:T(8,128)(2,1)S(1)}, u32[]{:S(2)}, u32[]{:S(2)}) collective-permute-start(bf16[512,768]{1,0:T(8,128)(2,1)S(1)} %get-tuple-element.915.refs_0_), channel_id=1, source_target_pairs={{16,0},{17,1},{18,2},{19,3},{20,4},{21,5},{22,6},{23,7},{24,8},{25... | collective-permute-start | bytes 2359304 | tf_op jit(solution)/shard_map/ppermute | solution.py:113
  268.9 36.3 %collective-permute-start.48 = (bf16[512,768]{1,0:T(8,128)(2,1)S(1)}, bf16[512,768]{1,0:T(8,128)(2,1)S(1)}, u32[]{:S(2)}, u32[]{:S(2)}) collective-permute-start(bf16[512,768]{1,0:T(8,128)(2,1)S(1)} %grad.17), channel_id=1, source_target_pairs={{0,16},{1,17},{2,18},{3,19},{4,20},{5,21},{6,22},{7,23},{8,24},{9,... | collective-permute-start | bytes 2359304 | tf_op jit(solution)/shard_map/ppermute | solution.py:113
  268.9 36.3 %collective-permute-start.49 = (bf16[512,768]{1,0:T(8,128)(2,1)S(1)}, bf16[512,768]{1,0:T(8,128)(2,1)S(1)}, u32[]{:S(2)}, u32[]{:S(2)}) collective-permute-start(bf16[512,768]{1,0:T(8,128)(2,1)S(1)} %get-tuple-element.886), channel_id=1, source_target_pairs={{0,4},{1,5},{2,6},{3,7},{4,0},{5,1},{6,2},{7,3},{8,12},{9,13},{10,... | collective-permute-start | bytes 2359304 | tf_op jit(solution)/shard_map/ppermute | solution.py:113
  270.3 32.4 %collective-permute-start.51 = (bf16[512,640]{1,0:T(8,128)(2,1)S(1)}, bf16[512,640]{1,0:T(8,128)(2,1)S(1)}, u32[]{:S(2)}, u32[]{:S(2)}) collective-permute-start(bf16[512,640]{1,0:T(8,128)(2,1)S(1)} %get-tuple-element.888), channel_id=1, source_target_pairs={{0,4},{1,5},{2,6},{3,7},{4,0},{5,1},{6,2},{7,3},{8,12},{9,13},{10,... | collective-permute-start | bytes 1966088 | tf_op jit(solution)/shard_map/ppermute | solution.py:113
  283.4 30.0 %collective-permute-start.53 = (bf16[128,2048]{1,0:T(8,128)(2,1)S(1)}, bf16[128,2048]{1,0:T(8,128)(2,1)S(1)}, u32[]{:S(2)}, u32[]{:S(2)}) collective-permute-start(bf16[128,2048]{1,0:T(8,128)(2,1)S(1)} %add.360), channel_id=1, source_target_pairs={{0,8},{1,9},{2,10},{3,11},{4,12},{5,13},{6,14},{7,15},{8,0},{9,1},... | collective-permute-start | bytes 1572872 | tf_op jit(solution)/shard_map/ppermute | solution.py:113
  315.8 32.9 %collective-permute-start.56 = (bf16[512,768]{1,0:T(8,128)(2,1)S(1)}, bf16[512,768]{1,0:T(8,128)(2,1)S(1)}, u32[]{:S(2)}, u32[]{:S(2)}) collective-permute-start(bf16[512,768]{1,0:T(8,128)(2,1)S(1)} %get-tuple-element.955), channel_id=1, source_target_pairs={{0,4},{1,5},{2,6},{3,7},{4,0},{5,1},{6,2},{7,3},{8,12},{9,13},{10,... | collective-permute-start | bytes 2359304 | tf_op jit(solution)/shard_map/ppermute | solution.py:113
  317.1 30.3 %collective-permute-start.55 = (bf16[512,640]{1,0:T(8,128)(2,1)S(1)}, bf16[512,640]{1,0:T(8,128)(2,1)S(1)}, u32[]{:S(2)}, u32[]{:S(2)}) collective-permute-start(bf16[512,640]{1,0:T(8,128)(2,1)S(1)} %get-tuple-element.937), channel_id=1, source_target_pairs={{0,4},{1,5},{2,6},{3,7},{4,0},{5,1},{6,2},{7,3},{8,12},{9,13},{10,... | collective-permute-start | bytes 1966088 | tf_op jit(solution)/shard_map/ppermute | solution.py:113
  319.4 29.3 %collective-permute-start.54 = (bf16[512,640]{1,0:T(8,128)(2,1)S(1)}, bf16[512,640]{1,0:T(8,128)(2,1)S(1)}, u32[]{:S(2)}, u32[]{:S(2)}) collective-permute-start(bf16[512,640]{1,0:T(8,128)(2,1)S(1)} %grad.22), channel_id=1, source_target_pairs={{0,16},{1,17},{2,18},{3,19},{4,20},{5,21},{6,22},{7,23},{8,24},{9,... | collective-permute-start | bytes 1966088 | tf_op jit(solution)/shard_map/ppermute | solution.py:113
  362.2 42.4 %all-to-all-start.3 = ((bf16[8,64,1408]{2,1,0:T(8,128)(2,1)}), bf16[8,64,1408]{2,1,0:T(8,128)(2,1)}, u32[]{:S(2)}, u32[]{:S(2)}) async-start(bf16[8,64,1408]{2,1,0:T(8,128)(2,1)} %bitcast.31), calls=%async_computation.3 | async-start | bytes 2883584 | tf_op jit(solution)/shard_map/all_to_all | solution.py:135
  366.6 37.9 %collective-permute-start.67 = (bf16[512,768]{1,0:T(8,128)(2,1)}, bf16[512,768]{1,0:T(8,128)(2,1)}, u32[]{:S(2)}, u32[]{:S(2)}) collective-permute-start(bf16[512,768]{1,0:T(8,128)(2,1)} %grad.23), channel_id=1, source_target_pairs={{0,16},{1,17},{2,18},{3,19},{4,20},{5,21},{6,22},{7,23},{8,24},{9,... | collective-permute-start | bytes 2359304 | tf_op jit(solution)/shard_map/ppermute | solution.py:113
  367.0 37.6 %collective-permute-start.68 = (bf16[512,768]{1,0:T(8,128)(2,1)}, bf16[512,768]{1,0:T(8,128)(2,1)}, u32[]{:S(2)}, u32[]{:S(2)}) collective-permute-start(bf16[512,768]{1,0:T(8,128)(2,1)} %get-tuple-element.1041), channel_id=1, source_target_pairs={{0,4},{1,5},{2,6},{3,7},{4,0},{5,1},{6,2},{7,3},{8,12},{9,13},{10,... | collective-permute-start | bytes 2359304 | tf_op jit(solution)/shard_map/ppermute | solution.py:113
  368.4 29.6 %collective-permute-start.65 = (bf16[1024,256]{1,0:T(8,128)(2,1)}, bf16[1024,256]{1,0:T(8,128)(2,1)}, u32[]{:S(2)}, u32[]{:S(2)}) collective-permute-start(bf16[1024,256]{1,0:T(8,128)(2,1)} %grad.24), channel_id=1, source_target_pairs={{0,4},{1,5},{2,6},{3,7},{4,0},{5,1},{6,2},{7,3},{8,12},{9,13},{10,... | collective-permute-start | bytes 1572872 | tf_op jit(solution)/shard_map/ppermute | solution.py:113
  408.4 33.6 %all-to-all-start.4 = ((bf16[8,64,768]{2,1,0:T(8,128)(2,1)}), bf16[8,64,768]{2,1,0:T(8,128)(2,1)}, u32[]{:S(2)}, u32[]{:S(2)}) async-start(bf16[8,64,768]{2,1,0:T(8,128)(2,1)} %bitcast.92), calls=%async_computation.4 | async-start | bytes 1572864 | tf_op jit(solution)/shard_map/all_to_all | solution.py:135
  443.6 37.2 %collective-permute-start.75 = (bf16[512,768]{1,0:T(8,128)(2,1)}, bf16[512,768]{1,0:T(8,128)(2,1)S(1)}, u32[]{:S(2)}, u32[]{:S(2)}) collective-permute-start(bf16[512,768]{1,0:T(8,128)(2,1)} %copy-done.34), channel_id=1, source_target_pairs={{0,16},{1,17},{2,18},{3,19},{4,20},{5,21},{6,22},{7,23},{8,24},{9,... | collective-permute-start | bytes 2359304 | tf_op jit(solution)/shard_map/ppermute | solution.py:113
  446.5 34.3 %collective-permute-start.76 = (bf16[512,768]{1,0:T(8,128)(2,1)}, bf16[512,768]{1,0:T(8,128)(2,1)S(1)}, u32[]{:S(2)}, u32[]{:S(2)}) collective-permute-start(bf16[512,768]{1,0:T(8,128)(2,1)} %copy-done.61), channel_id=1, source_target_pairs={{0,4},{1,5},{2,6},{3,7},{4,0},{5,1},{6,2},{7,3},{8,12},{9,13},{10,... | collective-permute-start | bytes 2359304 | tf_op jit(solution)/shard_map/ppermute | solution.py:113
  (138 other events, 1746.4 us)
